TPU v7x, 32 devices: a whole 2x2x4 slice. The times are simulated.
32 devices in a mesh: grp: 2 (over x), wide: 16 (over z, y, core).
Axes of the slice: x: 2, y: 2, z: 4, core: 2. Of those that a mesh axis runs over, the one named last changes fastest.
Arguments:
- queries: bfloat16 [256, 4096], P(('grp', 'wide')), parts along dimension 0, may hold values from -8 to 8
- draft_keys: bfloat16 [256, 512], P(('grp', 'wide')), parts along dimension 0, may hold values from -8 to 8
- draft_values: bfloat16 [256, 512], P(('grp', 'wide')), parts along dimension 0, may hold values from -24 to 24
- cache_keys: bfloat16 [262144, 128], P(('grp', 'wide')), parts along dimension 0, may hold values from -8 to 8
- cache_values: bfloat16 [262144, 128], P(('grp', 'wide')), parts along dimension 0, may hold values from -24 to 24
- block_owner: int32 [32], P('grp'), parts along dimension 0, may hold values from 0 to 15, each once
- block_lengths: int32 [32], P('grp'), parts along dimension 0, may hold values from 1024 to 8192, as said below
- draft_mask: int32 [4, 64, 64], P('grp'), parts along dimension 0, may hold values from 0 to 1, as said below
- out_weight: bfloat16 [4096, 8192], P(None, 'wide'), may hold values from -1 to 1
- norm_gain: float32 [8192], replicated, may hold values from 0.25 to 1.75
- gate_weight: bfloat16 [8192, 14336], P(None, 'wide'), may hold values from -0.0625 to 0.0625
- up_weight: bfloat16 [8192, 14336], P(None, 'wide'), may hold values from -0.0625 to 0.0625
Outputs:
- projected: bfloat16 [256, 8192], P('grp', 'wide'), parts along dimension 0
- hidden: bfloat16 [256, 14336], P('grp', 'wide'), parts along dimension 0
There are 2 independent parts, one for each index of `grp`. A program takes and returns all parts, laid end to end along the dimension named above; an argument that names none is the same for every part. Nothing has to cross between parts.
Inputs may be any that keep to these rules, and one draw needn't show every extreme that they name: `block_owner`: each device holds exactly one block. `block_lengths`: at most 8192 rows a block, and some block has exactly 8192 rows. In each sequence row 0 is the root of a tree in which every other row's parent lies 1 to 4 rows before it; draft_mask[s, i, t] is 1 exactly when t is i or an ancestor of i.
All inputs are finite; a program needn't handle non-finite values.
Results may differ from a plain program's by a relative error of at most 0.02.
Values may be sent and summed in bfloat16 or wider, within the bound.
No kernel may reach another device: no remote copies, remote signals or barrier semaphores. Data moves between devices by JAX's collectives and lax.ppermute only.
A program may use at most 128 MiB of HBM per device.

v0:
```python
import functools
import math

import jax
import jax.numpy as jnp
from jax import lax
from jax.experimental import pallas as pl
from jax.experimental.pallas import tpu as pltpu
from jax.sharding import PartitionSpec as P


very_low = -1e30
epsilon = 1e-05
log2e = 1.4426950408889634
lanes = 128


def attention_kernel(pieces, sequences, rows, group, head_size, info, order, *refs):
    blocks = refs[:pieces]
    mask, keys, values, out, land, q, top, total, acc, sem = refs[pieces:]
    step = pl.program_id(0)
    block = keys.shape[0]
    length, own_sequence, own_head, is_last = info[0], info[1], info[2], info[3]
    scale = log2e / math.sqrt(head_size)
    width = group * head_size

    def fold(scores, valid, block_values):
        if valid is not None:
            scores = jnp.where(valid, scores, very_low)
        peak = top[...]
        newest = jnp.maximum(peak, jnp.max(scores, axis=1, keepdims=True))
        factor = jnp.exp2(peak - newest)
        part, weights = None, []
        for at in range(0, scores.shape[1], lanes):
            tile = jnp.exp2(scores[:, at : at + lanes] - newest)
            if valid is not None:
                tile = jnp.where(valid[:, at : at + lanes], tile, 0.0)
            part = tile if part is None else part + tile
            weights.append(tile.astype(jnp.bfloat16))
        total[...] = total[...] * factor + part
        acc[...] = acc[...] * factor + jnp.dot(
            jnp.concatenate(weights, axis=1), block_values, preferred_element_type=jnp.float32
        )
        top[...] = newest

    def score(block_keys):
        return (
            lax.dot_general(
                q[...], block_keys, (((1,), (1,)), ((), ())), preferred_element_type=jnp.float32
            )
            * scale
        )

    @pl.when(step == 0)
    def _():
        sources = pieces // sequences
        extent = land.shape[2]
        columns = pl.ds(pl.multiple_of(own_head * extent, lanes), extent)
        for phase in range(2):
            for piece in range(pieces):
                slot = order[piece] % sources
                copy = pltpu.make_async_copy(
                    blocks[piece].at[:, columns], land.at[slot], sem.at[slot]
                )
                pl.when(order[piece] // sources == own_sequence)(
                    copy.wait if phase else copy.start
                )
        mine = land[...].reshape(rows, land.shape[2])
        for head in range(group):
            q[head * rows : (head + 1) * rows, :] = mine[:, head * head_size : (head + 1) * head_size]
        own_keys = jnp.concatenate(
            [mine[:, width : width + head_size], jnp.zeros((lanes - rows, head_size), jnp.bfloat16)], 0
        )
        own_values = jnp.concatenate(
            [
                mine[:, width + head_size : width + 2 * head_size],
                jnp.zeros((lanes - rows, head_size), jnp.bfloat16),
            ],
            0,
        )
        seen = jnp.where(is_last > 0, mask[0].astype(jnp.float32), 0.0)
        seen = jnp.concatenate([seen, jnp.zeros((rows, lanes - rows), jnp.float32)], 1)
        valid = jnp.concatenate([seen] * group, 0) > 0.0
        top[...] = jnp.full_like(top, very_low)
        total[...] = jnp.zeros_like(total)
        acc[...] = jnp.zeros_like(acc)
        fold(score(own_keys), valid, own_values)

    @pl.when((step + 1) * block <= length)
    def _():
        fold(score(keys[...]), None, values[...])

    @pl.when((step * block < length) & ((step + 1) * block > length))
    def _():
        at = step * block + lax.broadcasted_iota(jnp.int32, (1, block), 1)
        valid = jnp.broadcast_to(at < length, (q.shape[0], block))
        fold(score(keys[...]), valid, values[...])

    @pl.when(step == pl.num_programs(0) - 1)
    def _():
        summed = jnp.sum(total[...], axis=1, keepdims=True)
        result = acc[...] / summed
        level = top[...] + jnp.log2(summed)
        lane = lax.broadcasted_iota(jnp.int32, (rows, lanes), 1)
        notes = jnp.zeros((rows, lanes), jnp.float32)
        for head in range(group):
            part = slice(head * rows, (head + 1) * rows)
            out[:, head * head_size : (head + 1) * head_size] = result[part].astype(jnp.bfloat16)
            rest = jnp.broadcast_to(level[part, :1], (rows, lanes))
            for piece in range(3):
                cut = rest.astype(jnp.bfloat16).astype(jnp.float32)
                notes = jnp.where(lane == piece * group + head, cut, notes)
                rest = rest - cut
        out[:, width:] = notes.astype(jnp.bfloat16)


def attention(info, order, blocks, mask, keys, values, group):
    head_size = keys.shape[1]
    sequences, rows = mask.shape[0], mask.shape[1]
    capacity = keys.shape[0]
    block = min(1024, capacity)
    width = group * head_size
    pieces = len(blocks)
    extent = width + 2 * head_size

    def at(step, info, order):
        return (jnp.minimum(step, (info[0] + block - 1) // block - 1), 0)

    return pl.pallas_call(
        functools.partial(attention_kernel, pieces, sequences, rows, group, head_size),
        out_shape=jax.ShapeDtypeStruct((rows, width + lanes), jnp.bfloat16),
        grid_spec=pltpu.PrefetchScalarGridSpec(
            num_scalar_prefetch=2,
            grid=(capacity // block,),
            in_specs=[pl.BlockSpec(memory_space=pl.ANY)] * pieces
            + [
                pl.BlockSpec((1, rows, rows), lambda step, info, order: (info[1], 0, 0)),
                pl.BlockSpec((block, head_size), at),
                pl.BlockSpec((block, head_size), at),
            ],
            out_specs=pl.BlockSpec((rows, width + lanes), lambda step, info, order: (0, 0)),
            scratch_shapes=[
                pltpu.VMEM((pieces // sequences, blocks[0].shape[0], extent), jnp.bfloat16),
                pltpu.VMEM((group * rows, head_size), jnp.bfloat16),
                pltpu.VMEM((group * rows, lanes), jnp.float32),
                pltpu.VMEM((group * rows, lanes), jnp.float32),
                pltpu.VMEM((group * rows, head_size), jnp.float32),
                pltpu.SemaphoreType.DMA((pieces // sequences,)),
            ],
        ),
        compiler_params=pltpu.CompilerParams(vmem_limit_bytes=16 << 20),
        cost_estimate=pl.CostEstimate(
            flops=16 * 4 * group * rows * capacity * head_size,
            bytes_accessed=4 * capacity * head_size,
            transcendentals=16 * group * rows * capacity,
        ),
        name="attention",
    )(info, order, *blocks, mask, keys, values)


def projection_kernel(pieces, per_pair, key_heads, sequences, group, head_size, *refs):
    where_from = refs[0]
    blocks = refs[1 : 1 + pieces]
    weight = refs[1 + pieces]
    out = refs[2 + pieces]
    held, attended, piece_sem = refs[3 + pieces :]
    rows = held.shape[1]
    width = group * head_size
    copies = []
    for piece in range(pieces):
        copy = pltpu.make_async_copy(blocks[piece], held.at[piece], piece_sem.at[piece])
        copy.start()
        copies.append(copy)
    for copy in copies:
        copy.wait()
    for head in range(key_heads):
        for sequence in range(sequences):
            pair = sequence * key_heads + head
            slots = [where_from[pair * per_pair + number] for number in range(per_pair)]
            levels = []
            for slot in slots:
                notes = held[slot, :, width:].astype(jnp.float32)
                levels.append(
                    notes
                    + pltpu.roll(notes, lanes - group, 1)
                    + pltpu.roll(notes, lanes - 2 * group, 1)
                )
            highest = functools.reduce(jnp.maximum, levels)
            mixing = [jnp.exp2(level - highest) for level in levels]
            whole = functools.reduce(jnp.add, mixing)
            mixing = [part / whole for part in mixing]
            for member in range(group):
                columns = slice(member * head_size, (member + 1) * head_size)
                gathered = None
                for slot, part in zip(slots, mixing):
                    term = part[:, member : member + 1] * held[slot, :, columns].astype(jnp.float32)
                    gathered = term if gathered is None else gathered + term
                attended[
                    sequence * rows : (sequence + 1) * rows,
                    head * width + member * head_size : head * width + (member + 1) * head_size,
                ] = gathered.astype(jnp.bfloat16)
    out[...] = jnp.dot(
        attended[...], weight[...], preferred_element_type=jnp.float32
    ).astype(jnp.bfloat16)


def projection(where_from, blocks, weight, per_pair, key_heads, sequences, group, head_size):
    pieces = len(blocks)
    rows, extent = blocks[0].shape
    return pl.pallas_call(
        functools.partial(
            projection_kernel, pieces, per_pair, key_heads, sequences, group, head_size
        ),
        out_shape=pltpu.VMEM((sequences * rows, weight.shape[1]), jnp.bfloat16),
        in_specs=[pl.BlockSpec(memory_space=pltpu.SMEM)]
        + [pl.BlockSpec(memory_space=pl.ANY)] * pieces
        + [pl.BlockSpec(memory_space=pltpu.VMEM)],
        out_specs=pl.BlockSpec(memory_space=pltpu.VMEM),
        scratch_shapes=[
            pltpu.VMEM((pieces, rows, extent), jnp.bfloat16),
            pltpu.VMEM((sequences * rows, weight.shape[0]), jnp.bfloat16),
            pltpu.SemaphoreType.DMA((pieces,)),
        ],
        compiler_params=pltpu.CompilerParams(vmem_limit_bytes=16 << 20),
        cost_estimate=pl.CostEstimate(
            flops=2 * sequences * rows * weight.size,
            bytes_accessed=2 * (weight.size + pieces * rows * extent),
            transcendentals=0,
        ),
        name="projection",
    )(where_from, *blocks, weight)


def feed_kernel(pieces, order, *refs):
    blocks = refs[:pieces]
    gain, gate_weight, up_weight, out, gate, up = refs[pieces:]
    rows, depth = blocks[0].shape
    squares = jnp.zeros((rows, lanes), jnp.float32)
    for piece in range(pieces):
        branch = blocks[piece][...].astype(jnp.float32)
        square = branch * branch
        for at in range(0, depth, lanes):
            squares = squares + square[:, at : at + lanes]
        scaled = (branch * gain[order[piece]]).astype(jnp.bfloat16)
        part = pl.ds(pl.multiple_of(order[piece] * depth, depth), depth)
        for weight, total in ((gate_weight, gate), (up_weight, up)):
            term = jnp.dot(scaled, weight[part, :], preferred_element_type=jnp.float32)
            total[...] = term if piece == 0 else total[...] + term
    inverse = lax.rsqrt(jnp.sum(squares, axis=1, keepdims=True) / (pieces * depth) + epsilon)
    opened = gate[...] * inverse
    out[...] = (opened / (1.0 + jnp.exp(-opened)) * (up[...] * inverse)).astype(jnp.bfloat16)


def feed(order, blocks, gain, gate_weight, up_weight):
    pieces = len(blocks)
    rows, depth = blocks[0].shape
    width = gate_weight.shape[1]
    whole = pl.BlockSpec(memory_space=pltpu.VMEM)
    return pl.pallas_call(
        functools.partial(feed_kernel, pieces),
        out_shape=jax.ShapeDtypeStruct((rows, width), jnp.bfloat16),
        in_specs=[pl.BlockSpec(memory_space=pltpu.SMEM)] + [whole] * (pieces + 3),
        out_specs=whole,
        scratch_shapes=[pltpu.VMEM((rows, width), jnp.float32)] * 2,
        compiler_params=pltpu.CompilerParams(vmem_limit_bytes=16 << 20),
        cost_estimate=pl.CostEstimate(
            flops=4 * rows * pieces * depth * width,
            bytes_accessed=2 * rows * pieces * depth,
            transcendentals=rows * width,
        ),
        name="feed",
    )(order, *blocks, gain.reshape(pieces, 1, depth), gate_weight, up_weight)


def spread(block, devices):
    def swap(value, bits):
        return lax.ppermute(value, "wide", [(i, i ^ bits) for i in range(devices)])

    found = [block] + [swap(block, 4 * far) for far in range(1, devices // 4)]
    found = found + [swap(value, 2) for value in found]
    return found + [swap(value, 1) for value in found]


def origins(devices, own_index):
    far = devices // 4
    number = jnp.arange(devices, dtype=jnp.int32)
    swapped = number // far
    return own_index ^ (number % far * 4 + swapped % 2 * 2 + swapped // 2)


def per_device(
    queries,
    draft_keys,
    draft_values,
    cache_keys,
    cache_values,
    block_owner,
    block_lengths,
    draft_mask,
    out_weight,
    norm_gain,
    gate_weight,
    up_weight,
):
    devices = lax.axis_size("wide")
    own_index = lax.axis_index("wide").astype(jnp.int32)
    local_rows = queries.shape[0]
    head_size = cache_keys.shape[1]
    key_heads = draft_keys.shape[1] // head_size
    group_width = queries.shape[1] // key_heads
    group = group_width // head_size
    sequences = draft_mask.shape[0]
    local_rows = queries.shape[0]
    per_pair = devices // (sequences * key_heads)
    device_ids = jnp.arange(devices, dtype=jnp.int32)
    mine = (block_owner == own_index).astype(jnp.int32)
    own_block = jnp.sum(mine * device_ids)
    own_length = jnp.sum(mine * block_lengths)
    own_pair = own_block // per_pair
    is_last = (own_block % per_pair == per_pair - 1).astype(jnp.int32)
    info = jnp.stack([own_length, own_pair // key_heads, own_pair % key_heads, is_last])
    order = origins(devices, own_index)
    slot_of = jnp.sum(
        (block_owner[:, None] == order[None, :]).astype(jnp.int32) * device_ids[None, :], axis=1
    )

    packed = jnp.concatenate(
        [
            queries.reshape(local_rows, key_heads, group_width),
            draft_keys.reshape(local_rows, key_heads, head_size),
            draft_values.reshape(local_rows, key_heads, head_size),
        ],
        axis=2,
    ).reshape(local_rows, -1)
    inputs = spread(packed, devices)
    block = attention(
        info,
        order,
        inputs,
        pltpu.with_memory_space_constraint(draft_mask, pltpu.HBM),
        pltpu.with_memory_space_constraint(cache_keys, pltpu.HBM),
        pltpu.with_memory_space_constraint(cache_values, pltpu.HBM),
        group,
    )
    projected = projection(
        slot_of,
        spread(block, devices),
        pltpu.with_memory_space_constraint(out_weight, pltpu.VMEM),
        per_pair,
        key_heads,
        sequences,
        group,
        head_size,
    )
    hidden = feed(
        order,
        spread(projected, devices),
        norm_gain,
        gate_weight,
        up_weight,
    )
    return (projected, hidden)


def solution(mesh):
    placed = (
        P(("grp", "wide"), None),
        P(("grp", "wide"), None),
        P(("grp", "wide"), None),
        P(("grp", "wide"), None),
        P(("grp", "wide"), None),
        P("grp"),
        P("grp"),
        P("grp", None, None),
        P(None, "wide"),
        P(),
        P(None, "wide"),
        P(None, "wide"),
    )
    return jax.shard_map(
        per_device,
        mesh=mesh,
        in_specs=placed,
        out_specs=(P("grp", "wide"), P("grp", "wide")),
        check_vma=False,
    )
```

profile of v0, /device:TPU:0, one launch (start us, length us, event | category | flops | bytes accessed | tf_op | source)
XLA Modules:
  0.0 98.3 jit_solution(1007023493869239345)
XLA Ops:
  0.6 0.9 pad_maximum_fusion
  1.5 0.5 collective-permute-start.7
  2.0 2.6 %collective-permute-start.3 = (bf16[8,5120]{1,0:T(8,128)(2,1)S(1)}, bf16[8,5120]{1,0:T(8,128)(2,1)S(1)}, u32[]{:S(2)}, u32[]{:S(2)}) collective-permute-start(bf16[8,5120]{1,0:T(8,128)(2,1)S(1)} %bitcast.14), channel_id=1, source_target_pairs={{0,2},{1,3},{2,0},{3,1},{4,6},{5,7},{6,4},{7,5},{8,10},{9,11},{10,... | collective-permute-start | bytes 245768 | tf_op jit(solution)/shard_map/ppermute | solution.py:277
  4.6 3.6 %collective-permute-start.2 = (bf16[8,5120]{1,0:T(8,128)(2,1)S(1)}, bf16[8,5120]{1,0:T(8,128)(2,1)S(1)}, u32[]{:S(2)}, u32[]{:S(2)}) collective-permute-start(bf16[8,5120]{1,0:T(8,128)(2,1)S(1)} %bitcast.15), channel_id=1, source_target_pairs={{0,12},{1,13},{2,14},{3,15},{4,8},{5,9},{6,10},{7,11},{8,4},{9,5},... | collective-permute-start | bytes 245768 | tf_op jit(solution)/shard_map/ppermute | solution.py:277
  8.2 0.0 collective-permute-start.1
  8.2 0.8 collective-permute-start
  9.0 1.3 %fusion.3 = (s32[]{:T(128)}, s32[]{:T(128)}) fusion(s32[16]{0:T(128)} %param.18, s32[16]{0:T(128)} %param.17, s32[]{:T(128)S(6)} %axis_index.12), kind=kLoop, calls=%fused_computation.17 | loop fusion | flops 78 | bytes 140 | tf_op jit(solution)/shard_map/reduce_sum | solution.py:318
  13.0 0.1 collective-permute-start.10
  13.0 0.0 collective-permute-done.7.refs_8_
  13.0 0.4 collective-permute-start.6
  13.4 0.0 collective-permute-done.3.refs_4_
  13.4 0.2 collective-permute-start.11
  13.6 1.8 %collective-permute-done.1.refs_2_ = bf16[8,5120]{1,0:T(8,128)(2,1)S(1)} collective-permute-done((bf16[8,5120]{1,0:T(8,128)(2,1)S(1)}, bf16[8,5120]{1,0:T(8,128)(2,1)S(1)}, u32[]{:S(2)}, u32[]{:S(2)}) %collective-permute-start.1) | collective-permute-done | bytes 81952 | tf_op jit(solution)/shard_map/ppermute | solution.py:277
  15.4 0.5 collective-permute-start.5
  15.9 0.0 collective-permute-done.refs_1_
  15.9 1.5 %collective-permute-start.4 = (bf16[8,5120]{1,0:T(8,128)(2,1)S(1)}, bf16[8,5120]{1,0:T(8,128)(2,1)S(1)}, u32[]{:S(2)}, u32[]{:S(2)}) collective-permute-start(bf16[8,5120]{1,0:T(8,128)(2,1)S(1)} %collective-permute-done.refs_1_), channel_id=1, source_target_pairs={{0,2},{1,3},{2,0},{3,1},{4,6},{5,7},{6,4},{7,5},{8,10},{9,11},{10,... | collective-permute-start | bytes 245768 | tf_op jit(solution)/shard_map/ppermute | solution.py:277
  17.4 0.0 collective-permute-done.11.refs_12_
  17.4 0.1 collective-permute-start.9
  17.5 0.0 collective-permute-done.10.refs_11_
  17.5 0.5 collective-permute-start.8
  18.0 0.4 collective-permute-done.6.refs_7_
  18.4 0.0 collective-permute-start.14
  18.4 2.1 %collective-permute-done.5.refs_6_ = bf16[8,5120]{1,0:T(8,128)(2,1)S(1)} collective-permute-done((bf16[8,5120]{1,0:T(8,128)(2,1)S(1)}, bf16[8,5120]{1,0:T(8,128)(2,1)S(1)}, u32[]{:S(2)}, u32[]{:S(2)}) %collective-permute-start.5) | collective-permute-done | bytes 81952 | tf_op jit(solution)/shard_map/ppermute | solution.py:277
  20.5 0.0 collective-permute-start.13
  20.5 0.9 collective-permute-done.4.refs_5_
  21.4 0.0 collective-permute-start.12
  21.4 0.9 pad_add_fusion.info
  22.3 0.0 slice-start.5
  22.4 0.3 collective-permute-done.12.refs_13_
  22.7 7.8 %attention.1.refs_1_ = bf16[64,1152]{1,0:T(8,128)(2,1)S(1)} custom-call(s32[4]{0:T(128)S(1)} %pad_add_fusion.info, s32[16]{0:T(128)S(1)} %fusion.6.order, bf16[8,5120]{1,0:T(8,128)(2,1)S(1)} %bitcast.18, bf16[8,5120]{1,0:T(8,128)(2,1)S(1)} %collective-permute-done.refs_1_, bf16[8,5120]{1,0:T(8,128)(2,1)S(1)} %collective-permute-done.1.refs_2_, ...), custom_call_target="tpu_custom_call" | custom-call | flops 34359738368 | bytes 4194304 | tf_op jit(solution)/shard_map/attention/pallas_call | solution.py:129
  30.5 0.0 copy-start.1
  30.5 0.1 collective-permute-start.18
  30.6 4.1 %collective-permute-start.17 = (bf16[64,1152]{1,0:T(8,128)(2,1)S(1)}, bf16[64,1152]{1,0:T(8,128)(2,1)S(1)}, u32[]{:S(2)}, u32[]{:S(2)}) collective-permute-start(bf16[64,1152]{1,0:T(8,128)(2,1)S(1)} %attention.1.refs_1_), channel_id=1, source_target_pairs={{0,12},{1,13},{2,14},{3,15},{4,8},{5,9},{6,10},{7,11},{8,4},{9,5},... | collective-permute-start | bytes 442376 | tf_op jit(solution)/shard_map/ppermute | solution.py:277
  34.7 1.8 %collective-permute-start.22 = (bf16[64,1152]{1,0:T(8,128)(2,1)S(1)}, bf16[64,1152]{1,0:T(8,128)(2,1)S(1)}, u32[]{:S(2)}, u32[]{:S(2)}) collective-permute-start(bf16[64,1152]{1,0:T(8,128)(2,1)S(1)} %attention.1.refs_1_), channel_id=1, source_target_pairs={{0,1},{1,0},{2,3},{3,2},{4,5},{5,4},{6,7},{7,6},{8,9},{9,8},{10,11... | collective-permute-start | bytes 442376 | tf_op jit(solution)/shard_map/ppermute | solution.py:277
  36.5 0.5 collective-permute-start.16
  37.0 3.6 %collective-permute-start.15 = (bf16[64,1152]{1,0:T(8,128)(2,1)S(1)}, bf16[64,1152]{1,0:T(8,128)(2,1)S(1)}, u32[]{:S(2)}, u32[]{:S(2)}) collective-permute-start(bf16[64,1152]{1,0:T(8,128)(2,1)S(1)} %attention.1.refs_1_), channel_id=1, source_target_pairs={{0,4},{1,5},{2,6},{3,7},{4,0},{5,1},{6,2},{7,3},{8,12},{9,13},{10,... | collective-permute-start | bytes 442376 | tf_op jit(solution)/shard_map/ppermute | solution.py:277
  40.6 2.7 %collective-permute-start.25 = (bf16[64,1152]{1,0:T(8,128)(2,1)S(1)}, bf16[64,1152]{1,0:T(8,128)(2,1)S(1)}, u32[]{:S(2)}, u32[]{:S(2)}) collective-permute-start(bf16[64,1152]{1,0:T(8,128)(2,1)S(1)} %collective-permute-done.17.refs_4_), channel_id=1, source_target_pairs={{0,1},{1,0},{2,3},{3,2},{4,5},{5,4},{6,7},{7,6},{8,9},{9,8},{10,11... | collective-permute-start | bytes 442376 | tf_op jit(solution)/shard_map/ppermute | solution.py:277
  43.2 1.7 %collective-permute-start.21 = (bf16[64,1152]{1,0:T(8,128)(2,1)S(1)}, bf16[64,1152]{1,0:T(8,128)(2,1)S(1)}, u32[]{:S(2)}, u32[]{:S(2)}) collective-permute-start(bf16[64,1152]{1,0:T(8,128)(2,1)S(1)} %collective-permute-done.17.refs_4_), channel_id=1, source_target_pairs={{0,2},{1,3},{2,0},{3,1},{4,6},{5,7},{6,4},{7,5},{8,10},{9,11},{10,... | collective-permute-start | bytes 442376 | tf_op jit(solution)/shard_map/ppermute | solution.py:277
  44.9 4.0 %collective-permute-done.16.refs_3_ = bf16[64,1152]{1,0:T(8,128)(2,1)S(1)} collective-permute-done((bf16[64,1152]{1,0:T(8,128)(2,1)S(1)}, bf16[64,1152]{1,0:T(8,128)(2,1)S(1)}, u32[]{:S(2)}, u32[]{:S(2)}) %collective-permute-start.16) | collective-permute-done | bytes 147488 | tf_op jit(solution)/shard_map/ppermute | solution.py:277
  48.9 1.7 %collective-permute-start.20 = (bf16[64,1152]{1,0:T(8,128)(2,1)S(1)}, bf16[64,1152]{1,0:T(8,128)(2,1)S(1)}, u32[]{:S(2)}, u32[]{:S(2)}) collective-permute-start(bf16[64,1152]{1,0:T(8,128)(2,1)S(1)} %collective-permute-done.16.refs_3_), channel_id=1, source_target_pairs={{0,2},{1,3},{2,0},{3,1},{4,6},{5,7},{6,4},{7,5},{8,10},{9,11},{10,... | collective-permute-start | bytes 442376 | tf_op jit(solution)/shard_map/ppermute | solution.py:277
  50.6 0.3 collective-permute-start.19
  50.9 0.5 collective-permute-start.23
  51.4 0.1 collective-permute-start.29
  51.5 4.1 %collective-permute-done.20.refs_7_ = bf16[64,1152]{1,0:T(8,128)(2,1)S(1)} collective-permute-done((bf16[64,1152]{1,0:T(8,128)(2,1)S(1)}, bf16[64,1152]{1,0:T(8,128)(2,1)S(1)}, u32[]{:S(2)}, u32[]{:S(2)}) %collective-permute-start.20) | collective-permute-done | bytes 147488 | tf_op jit(solution)/shard_map/ppermute | solution.py:277
  55.6 1.8 %collective-permute-done.19.refs_6_ = bf16[64,1152]{1,0:T(8,128)(2,1)S(1)} collective-permute-done((bf16[64,1152]{1,0:T(8,128)(2,1)S(1)}, bf16[64,1152]{1,0:T(8,128)(2,1)S(1)}, u32[]{:S(2)}, u32[]{:S(2)}) %collective-permute-start.19) | collective-permute-done | bytes 147488 | tf_op jit(solution)/shard_map/ppermute | solution.py:277
  57.4 0.2 select_reduce_fusion.refs_0_
  57.6 1.1 %collective-permute-done.27.refs_14_ = bf16[64,1152]{1,0:T(8,128)(2,1)S(1)} collective-permute-done((bf16[64,1152]{1,0:T(8,128)(2,1)S(1)}, bf16[64,1152]{1,0:T(8,128)(2,1)S(1)}, u32[]{:S(2)}, u32[]{:S(2)}) %collective-permute-start.27) | collective-permute-done | bytes 147488 | tf_op jit(solution)/shard_map/ppermute | solution.py:277
  58.8 6.9 %projection.1.refs_0_ = bf16[128,512]{1,0:T(8,128)(2,1)S(1)} custom-call(s32[16]{0:T(128)S(1)} %select_reduce_fusion.refs_0_, bf16[64,1152]{1,0:T(8,128)(2,1)S(1)} %attention.1.refs_1_, bf16[64,1152]{1,0:T(8,128)(2,1)S(1)} %collective-permute-done.15.refs_2_, bf16[64,1152]{1,0:T(8,128)(2,1)S(1)} %collective-permute-done.16.refs_3_, ...), custom_call_target="tpu_custom_call" | custom-call | flops 536870912 | bytes 6553600 | tf_op jit(solution)/shard_map/projection/pallas_call | solution.py:210
  65.6 1.5 %collective-permute-start.33 = (bf16[128,512]{1,0:T(8,128)(2,1)S(1)}, bf16[128,512]{1,0:T(8,128)(2,1)S(1)}, u32[]{:S(2)}, u32[]{:S(2)}) collective-permute-start(bf16[128,512]{1,0:T(8,128)(2,1)S(1)} %projection.1.refs_0_), channel_id=1, source_target_pairs={{0,2},{1,3},{2,0},{3,1},{4,6},{5,7},{6,4},{7,5},{8,10},{9,11},{10,... | collective-permute-start | bytes 393224 | tf_op jit(solution)/shard_map/ppermute | solution.py:277
  67.2 1.9 %collective-permute-start.32 = (bf16[128,512]{1,0:T(8,128)(2,1)S(1)}, bf16[128,512]{1,0:T(8,128)(2,1)S(1)}, u32[]{:S(2)}, u32[]{:S(2)}) collective-permute-start(bf16[128,512]{1,0:T(8,128)(2,1)S(1)} %projection.1.refs_0_), channel_id=1, source_target_pairs={{0,12},{1,13},{2,14},{3,15},{4,8},{5,9},{6,10},{7,11},{8,4},{9,5},... | collective-permute-start | bytes 393224 | tf_op jit(solution)/shard_map/ppermute | solution.py:277
  69.0 2.1 %collective-permute-start.31 = (bf16[128,512]{1,0:T(8,128)(2,1)S(1)}, bf16[128,512]{1,0:T(8,128)(2,1)S(1)}, u32[]{:S(2)}, u32[]{:S(2)}) collective-permute-start(bf16[128,512]{1,0:T(8,128)(2,1)S(1)} %projection.1.refs_0_), channel_id=1, source_target_pairs={{0,8},{1,9},{2,10},{3,11},{4,12},{5,13},{6,14},{7,15},{8,0},{9,1},... | collective-permute-start | bytes 393224 | tf_op jit(solution)/shard_map/ppermute | solution.py:277
  71.1 0.4 collective-permute-start.30
  71.6 3.3 %collective-permute-done.32.refs_3_ = bf16[128,512]{1,0:T(8,128)(2,1)S(1)} collective-permute-done((bf16[128,512]{1,0:T(8,128)(2,1)S(1)}, bf16[128,512]{1,0:T(8,128)(2,1)S(1)}, u32[]{:S(2)}, u32[]{:S(2)}) %collective-permute-start.32) | collective-permute-done | bytes 131104 | tf_op jit(solution)/shard_map/ppermute | solution.py:277
  74.9 0.1 collective-permute-start.36
  75.0 7.7 %collective-permute-done.31.refs_2_ = bf16[128,512]{1,0:T(8,128)(2,1)S(1)} collective-permute-done((bf16[128,512]{1,0:T(8,128)(2,1)S(1)}, bf16[128,512]{1,0:T(8,128)(2,1)S(1)}, u32[]{:S(2)}, u32[]{:S(2)}) %collective-permute-start.31) | collective-permute-done | bytes 131104 | tf_op jit(solution)/shard_map/ppermute | solution.py:277
  82.7 0.5 collective-permute-start.35
  83.2 1.5 %collective-permute-start.34 = (bf16[128,512]{1,0:T(8,128)(2,1)S(1)}, bf16[128,512]{1,0:T(8,128)(2,1)S(1)}, u32[]{:S(2)}, u32[]{:S(2)}) collective-permute-start(bf16[128,512]{1,0:T(8,128)(2,1)S(1)} %collective-permute-done.30.refs_1_), channel_id=1, source_target_pairs={{0,2},{1,3},{2,0},{3,1},{4,6},{5,7},{6,4},{7,5},{8,10},{9,11},{10,... | collective-permute-start | bytes 393224 | tf_op jit(solution)/shard_map/ppermute | solution.py:277
  84.7 0.5 collective-permute-start.38
  85.2 0.1 collective-permute-start.44
  85.3 3.7 %collective-permute-done.35.refs_6_ = bf16[128,512]{1,0:T(8,128)(2,1)S(1)} collective-permute-done((bf16[128,512]{1,0:T(8,128)(2,1)S(1)}, bf16[128,512]{1,0:T(8,128)(2,1)S(1)}, u32[]{:S(2)}, u32[]{:S(2)}) %collective-permute-start.35) | collective-permute-done | bytes 131104 | tf_op jit(solution)/shard_map/ppermute | solution.py:277
  89.0 1.9 %collective-permute-done.34.refs_5_ = bf16[128,512]{1,0:T(8,128)(2,1)S(1)} collective-permute-done((bf16[128,512]{1,0:T(8,128)(2,1)S(1)}, bf16[128,512]{1,0:T(8,128)(2,1)S(1)}, u32[]{:S(2)}, u32[]{:S(2)}) %collective-permute-start.34) | collective-permute-done | bytes 131104 | tf_op jit(solution)/shard_map/ppermute | solution.py:277
  90.9 0.7 copy.14
  91.6 0.7 collective-permute-done.42.refs_13_
  92.3 6.0 %feed.1 = bf16[128,896]{1,0:T(8,128)(2,1)} custom-call(s32[16]{0:T(128)S(1)} %fusion.6.order, bf16[128,512]{1,0:T(8,128)(2,1)S(1)} %projection.1.refs_0_, bf16[128,512]{1,0:T(8,128)(2,1)S(1)} %collective-permute-done.30.refs_1_, bf16[128,512]{1,0:T(8,128)(2,1)S(1)} %collective-permute-done.31.refs_2_, bf16[128,512]{1,0:T(8,128)(2,1)S(1)} %collective-permute-done.32.refs_3_, ...), custom_call_target="tpu_custom_call" | custom-call | flops 3758096384 | bytes 2097152 | tf_op jit(solution)/shard_map/feed/pallas_call | solution.py:259
  (59 shorter events, 0.1 us)
Async XLA Ops:
  1.5 11.5 %collective-permute-start.7 = (bf16[8,5120]{1,0:T(8,128)(2,1)S(1)}, bf16[8,5120]{1,0:T(8,128)(2,1)S(1)}, u32[]{:S(2)}, u32[]{:S(2)}) collective-permute-start(bf16[8,5120]{1,0:T(8,128)(2,1)S(1)} %bitcast.13), channel_id=1, source_target_pairs={{0,1},{1,0},{2,3},{3,2},{4,5},{5,4},{6,7},{7,6},{8,9},{9,8},{10,11... | collective-permute-start | bytes 245768 | tf_op jit(solution)/shard_map/ppermute | solution.py:277
  2.0 11.4 %collective-permute-start.3 = (bf16[8,5120]{1,0:T(8,128)(2,1)S(1)}, bf16[8,5120]{1,0:T(8,128)(2,1)S(1)}, u32[]{:S(2)}, u32[]{:S(2)}) collective-permute-start(bf16[8,5120]{1,0:T(8,128)(2,1)S(1)} %bitcast.14), channel_id=1, source_target_pairs={{0,2},{1,3},{2,0},{3,1},{4,6},{5,7},{6,4},{7,5},{8,10},{9,11},{10,... | collective-permute-start | bytes 245768 | tf_op jit(solution)/shard_map/ppermute | solution.py:277
  4.6 8.3 %collective-permute-start.2 = (bf16[8,5120]{1,0:T(8,128)(2,1)S(1)}, bf16[8,5120]{1,0:T(8,128)(2,1)S(1)}, u32[]{:S(2)}, u32[]{:S(2)}) collective-permute-start(bf16[8,5120]{1,0:T(8,128)(2,1)S(1)} %bitcast.15), channel_id=1, source_target_pairs={{0,12},{1,13},{2,14},{3,15},{4,8},{5,9},{6,10},{7,11},{8,4},{9,5},... | collective-permute-start | bytes 245768 | tf_op jit(solution)/shard_map/ppermute | solution.py:277
  8.2 7.2 %collective-permute-start.1 = (bf16[8,5120]{1,0:T(8,128)(2,1)S(1)}, bf16[8,5120]{1,0:T(8,128)(2,1)S(1)}, u32[]{:S(2)}, u32[]{:S(2)}) collective-permute-start(bf16[8,5120]{1,0:T(8,128)(2,1)S(1)} %bitcast.16), channel_id=1, source_target_pairs={{0,8},{1,9},{2,10},{3,11},{4,12},{5,13},{6,14},{7,15},{8,0},{9,1},... | collective-permute-start | bytes 245768 | tf_op jit(solution)/shard_map/ppermute | solution.py:277
  8.2 7.7 %collective-permute-start = (bf16[8,5120]{1,0:T(8,128)(2,1)S(1)}, bf16[8,5120]{1,0:T(8,128)(2,1)S(1)}, u32[]{:S(2)}, u32[]{:S(2)}) collective-permute-start(bf16[8,5120]{1,0:T(8,128)(2,1)S(1)} %bitcast.17), channel_id=1, source_target_pairs={{0,4},{1,5},{2,6},{3,7},{4,0},{5,1},{6,2},{7,3},{8,12},{9,13},{10,... | collective-permute-start | bytes 245768 | tf_op jit(solution)/shard_map/ppermute | solution.py:277
  13.0 4.6 %collective-permute-start.10 = (bf16[8,5120]{1,0:T(8,128)(2,1)S(1)}, bf16[8,5120]{1,0:T(8,128)(2,1)S(1)}, u32[]{:S(2)}, u32[]{:S(2)}) collective-permute-start(bf16[8,5120]{1,0:T(8,128)(2,1)S(1)} %collective-permute-done.2.refs_3_), channel_id=1, source_target_pairs={{0,1},{1,0},{2,3},{3,2},{4,5},{5,4},{6,7},{7,6},{8,9},{9,8},{10,11... | collective-permute-start | bytes 245768 | tf_op jit(solution)/shard_map/ppermute | solution.py:277
  13.0 5.4 %collective-permute-start.6 = (bf16[8,5120]{1,0:T(8,128)(2,1)S(1)}, bf16[8,5120]{1,0:T(8,128)(2,1)S(1)}, u32[]{:S(2)}, u32[]{:S(2)}) collective-permute-start(bf16[8,5120]{1,0:T(8,128)(2,1)S(1)} %collective-permute-done.2.refs_3_), channel_id=1, source_target_pairs={{0,2},{1,3},{2,0},{3,1},{4,6},{5,7},{6,4},{7,5},{8,10},{9,11},{10,... | collective-permute-start | bytes 245768 | tf_op jit(solution)/shard_map/ppermute | solution.py:277
  13.4 4.0 %collective-permute-start.11 = (bf16[8,5120]{1,0:T(8,128)(2,1)S(1)}, bf16[8,5120]{1,0:T(8,128)(2,1)S(1)}, u32[]{:S(2)}, u32[]{:S(2)}) collective-permute-start(bf16[8,5120]{1,0:T(8,128)(2,1)S(1)} %collective-permute-done.3.refs_4_), channel_id=1, source_target_pairs={{0,1},{1,0},{2,3},{3,2},{4,5},{5,4},{6,7},{7,6},{8,9},{9,8},{10,11... | collective-permute-start | bytes 245768 | tf_op jit(solution)/shard_map/ppermute | solution.py:277
  15.4 5.1 %collective-permute-start.5 = (bf16[8,5120]{1,0:T(8,128)(2,1)S(1)}, bf16[8,5120]{1,0:T(8,128)(2,1)S(1)}, u32[]{:S(2)}, u32[]{:S(2)}) collective-permute-start(bf16[8,5120]{1,0:T(8,128)(2,1)S(1)} %collective-permute-done.1.refs_2_), channel_id=1, source_target_pairs={{0,2},{1,3},{2,0},{3,1},{4,6},{5,7},{6,4},{7,5},{8,10},{9,11},{10,... | collective-permute-start | bytes 245768 | tf_op jit(solution)/shard_map/ppermute | solution.py:277
  15.9 5.5 %collective-permute-start.4 = (bf16[8,5120]{1,0:T(8,128)(2,1)S(1)}, bf16[8,5120]{1,0:T(8,128)(2,1)S(1)}, u32[]{:S(2)}, u32[]{:S(2)}) collective-permute-start(bf16[8,5120]{1,0:T(8,128)(2,1)S(1)} %collective-permute-done.refs_1_), channel_id=1, source_target_pairs={{0,2},{1,3},{2,0},{3,1},{4,6},{5,7},{6,4},{7,5},{8,10},{9,11},{10,... | collective-permute-start | bytes 245768 | tf_op jit(solution)/shard_map/ppermute | solution.py:277
  17.4 4.9 %collective-permute-start.9 = (bf16[8,5120]{1,0:T(8,128)(2,1)S(1)}, bf16[8,5120]{1,0:T(8,128)(2,1)S(1)}, u32[]{:S(2)}, u32[]{:S(2)}) collective-permute-start(bf16[8,5120]{1,0:T(8,128)(2,1)S(1)} %collective-permute-done.1.refs_2_), channel_id=1, source_target_pairs={{0,1},{1,0},{2,3},{3,2},{4,5},{5,4},{6,7},{7,6},{8,9},{9,8},{10,11... | collective-permute-start | bytes 245768 | tf_op jit(solution)/shard_map/ppermute | solution.py:277
  17.5 4.8 %collective-permute-start.8 = (bf16[8,5120]{1,0:T(8,128)(2,1)S(1)}, bf16[8,5120]{1,0:T(8,128)(2,1)S(1)}, u32[]{:S(2)}, u32[]{:S(2)}) collective-permute-start(bf16[8,5120]{1,0:T(8,128)(2,1)S(1)} %collective-permute-done.refs_1_), channel_id=1, source_target_pairs={{0,1},{1,0},{2,3},{3,2},{4,5},{5,4},{6,7},{7,6},{8,9},{9,8},{10,11... | collective-permute-start | bytes 245768 | tf_op jit(solution)/shard_map/ppermute | solution.py:277
  18.4 3.9 %collective-permute-start.14 = (bf16[8,5120]{1,0:T(8,128)(2,1)S(1)}, bf16[8,5120]{1,0:T(8,128)(2,1)S(1)}, u32[]{:S(2)}, u32[]{:S(2)}) collective-permute-start(bf16[8,5120]{1,0:T(8,128)(2,1)S(1)} %collective-permute-done.6.refs_7_), channel_id=1, source_target_pairs={{0,1},{1,0},{2,3},{3,2},{4,5},{5,4},{6,7},{7,6},{8,9},{9,8},{10,11... | collective-permute-start | bytes 245768 | tf_op jit(solution)/shard_map/ppermute | solution.py:277
  20.5 1.8 %collective-permute-start.13 = (bf16[8,5120]{1,0:T(8,128)(2,1)S(1)}, bf16[8,5120]{1,0:T(8,128)(2,1)S(1)}, u32[]{:S(2)}, u32[]{:S(2)}) collective-permute-start(bf16[8,5120]{1,0:T(8,128)(2,1)S(1)} %collective-permute-done.5.refs_6_), channel_id=1, source_target_pairs={{0,1},{1,0},{2,3},{3,2},{4,5},{5,4},{6,7},{7,6},{8,9},{9,8},{10,11... | collective-permute-start | bytes 245768 | tf_op jit(solution)/shard_map/ppermute | solution.py:277
  21.4 1.3 %collective-permute-start.12 = (bf16[8,5120]{1,0:T(8,128)(2,1)S(1)}, bf16[8,5120]{1,0:T(8,128)(2,1)S(1)}, u32[]{:S(2)}, u32[]{:S(2)}) collective-permute-start(bf16[8,5120]{1,0:T(8,128)(2,1)S(1)} %collective-permute-done.4.refs_5_), channel_id=1, source_target_pairs={{0,1},{1,0},{2,3},{3,2},{4,5},{5,4},{6,7},{7,6},{8,9},{9,8},{10,11... | collective-permute-start | bytes 245768 | tf_op jit(solution)/shard_map/ppermute | solution.py:277
  21.4 70.8 %slice-start = ((s8[14680064]{0:T(1024)(128)(4,1)}), s8[4194304]{0:T(1024)(128)(4,1)S(1)}, s32[]{:S(2)}) async-start(s8[14680064]{0:T(1024)(128)(4,1)} %bitcast.9), calls=%async_computation | async-start | bytes 8388608
  21.4 70.8 %slice-start.4 = ((s8[14680064]{0:T(1024)(128)(4,1)}), s8[4194304]{0:T(1024)(128)(4,1)S(1)}, s32[]{:S(2)}) async-start(s8[14680064]{0:T(1024)(128)(4,1)} %bitcast.11), calls=%async_computation.4 | async-start | bytes 8388608
  22.3 35.1 %copy-start.2 = (s32[16]{0:T(128)S(1)}, s32[16]{0:T(128)}, u32[]{:S(2)}) copy-start(s32[16]{0:T(128)} %param.17) | copy-start | bytes 196
  22.3 36.5 %copy-start = (bf16[4096,512]{1,0:T(8,128)(2,1)S(1)}, bf16[4096,512]{1,0:T(8,128)(2,1)}, u32[]{:S(2)}) copy-start(bf16[4096,512]{1,0:T(8,128)(2,1)} %refs_17_.4) | copy-start | bytes 12582916
  22.3 70.0 %slice-start.1 = ((s8[14680064]{0:T(1024)(128)(4,1)}), s8[4194304]{0:T(1024)(128)(4,1)S(1)}, s32[]{:S(2)}) async-start(s8[14680064]{0:T(1024)(128)(4,1)} %bitcast.9), calls=%async_computation.1 | async-start | bytes 8388608
  22.3 70.0 %slice-start.2 = ((s8[14680064]{0:T(1024)(128)(4,1)}), s8[4194304]{0:T(1024)(128)(4,1)S(1)}, s32[]{:S(2)}) async-start(s8[14680064]{0:T(1024)(128)(4,1)} %bitcast.9), calls=%async_computation.2 | async-start | bytes 8388608
  22.3 70.0 %slice-start.3 = ((s8[14680064]{0:T(1024)(128)(4,1)}), s8[2097152]{0:T(1024)(128)(4,1)S(1)}, s32[]{:S(2)}) async-start(s8[14680064]{0:T(1024)(128)(4,1)} %bitcast.9), calls=%async_computation.3 | async-start | bytes 4194304
  22.3 70.0 %slice-start.5 = ((s8[14680064]{0:T(1024)(128)(4,1)}), s8[4194304]{0:T(1024)(128)(4,1)S(1)}, s32[]{:S(2)}) async-start(s8[14680064]{0:T(1024)(128)(4,1)} %bitcast.11), calls=%async_computation.5 | async-start | bytes 8388608
  22.3 70.0 %slice-start.6 = ((s8[14680064]{0:T(1024)(128)(4,1)}), s8[4194304]{0:T(1024)(128)(4,1)S(1)}, s32[]{:S(2)}) async-start(s8[14680064]{0:T(1024)(128)(4,1)} %bitcast.11), calls=%async_computation.6 | async-start | bytes 8388608
  22.3 70.0 %slice-start.7 = ((s8[14680064]{0:T(1024)(128)(4,1)}), s8[2097152]{0:T(1024)(128)(4,1)S(1)}, s32[]{:S(2)}) async-start(s8[14680064]{0:T(1024)(128)(4,1)} %bitcast.11), calls=%async_computation.7 | async-start | bytes 4194304
  30.5 61.8 %copy-start.1 = (f32[8192]{0:T(1024)S(1)}, f32[8192]{0:T(1024)}, u32[]{:S(2)}) copy-start(f32[8192]{0:T(1024)} %param.21) | copy-start | bytes 98308
  30.5 10.0 %collective-permute-start.18 = (bf16[64,1152]{1,0:T(8,128)(2,1)S(1)}, bf16[64,1152]{1,0:T(8,128)(2,1)S(1)}, u32[]{:S(2)}, u32[]{:S(2)}) collective-permute-start(bf16[64,1152]{1,0:T(8,128)(2,1)S(1)} %attention.1.refs_1_), channel_id=1, source_target_pairs={{0,2},{1,3},{2,0},{3,1},{4,6},{5,7},{6,4},{7,5},{8,10},{9,11},{10,... | collective-permute-start | bytes 442376 | tf_op jit(solution)/shard_map/ppermute | solution.py:277
  30.6 10.0 %collective-permute-start.17 = (bf16[64,1152]{1,0:T(8,128)(2,1)S(1)}, bf16[64,1152]{1,0:T(8,128)(2,1)S(1)}, u32[]{:S(2)}, u32[]{:S(2)}) collective-permute-start(bf16[64,1152]{1,0:T(8,128)(2,1)S(1)} %attention.1.refs_1_), channel_id=1, source_target_pairs={{0,12},{1,13},{2,14},{3,15},{4,8},{5,9},{6,10},{7,11},{8,4},{9,5},... | collective-permute-start | bytes 442376 | tf_op jit(solution)/shard_map/ppermute | solution.py:277
  34.7 8.5 %collective-permute-start.22 = (bf16[64,1152]{1,0:T(8,128)(2,1)S(1)}, bf16[64,1152]{1,0:T(8,128)(2,1)S(1)}, u32[]{:S(2)}, u32[]{:S(2)}) collective-permute-start(bf16[64,1152]{1,0:T(8,128)(2,1)S(1)} %attention.1.refs_1_), channel_id=1, source_target_pairs={{0,1},{1,0},{2,3},{3,2},{4,5},{5,4},{6,7},{7,6},{8,9},{9,8},{10,11... | collective-permute-start | bytes 442376 | tf_op jit(solution)/shard_map/ppermute | solution.py:277
  36.5 12.4 %collective-permute-start.16 = (bf16[64,1152]{1,0:T(8,128)(2,1)S(1)}, bf16[64,1152]{1,0:T(8,128)(2,1)S(1)}, u32[]{:S(2)}, u32[]{:S(2)}) collective-permute-start(bf16[64,1152]{1,0:T(8,128)(2,1)S(1)} %attention.1.refs_1_), channel_id=1, source_target_pairs={{0,8},{1,9},{2,10},{3,11},{4,12},{5,13},{6,14},{7,15},{8,0},{9,1},... | collective-permute-start | bytes 442376 | tf_op jit(solution)/shard_map/ppermute | solution.py:277
  37.0 13.6 %collective-permute-start.15 = (bf16[64,1152]{1,0:T(8,128)(2,1)S(1)}, bf16[64,1152]{1,0:T(8,128)(2,1)S(1)}, u32[]{:S(2)}, u32[]{:S(2)}) collective-permute-start(bf16[64,1152]{1,0:T(8,128)(2,1)S(1)} %attention.1.refs_1_), channel_id=1, source_target_pairs={{0,4},{1,5},{2,6},{3,7},{4,0},{5,1},{6,2},{7,3},{8,12},{9,13},{10,... | collective-permute-start | bytes 442376 | tf_op jit(solution)/shard_map/ppermute | solution.py:277
  40.6 10.4 %collective-permute-start.26 = (bf16[64,1152]{1,0:T(8,128)(2,1)S(1)}, bf16[64,1152]{1,0:T(8,128)(2,1)S(1)}, u32[]{:S(2)}, u32[]{:S(2)}) collective-permute-start(bf16[64,1152]{1,0:T(8,128)(2,1)S(1)} %collective-permute-done.18.refs_5_), channel_id=1, source_target_pairs={{0,1},{1,0},{2,3},{3,2},{4,5},{5,4},{6,7},{7,6},{8,9},{9,8},{10,11... | collective-permute-start | bytes 442376 | tf_op jit(solution)/shard_map/ppermute | solution.py:277
  40.6 10.4 %collective-permute-start.25 = (bf16[64,1152]{1,0:T(8,128)(2,1)S(1)}, bf16[64,1152]{1,0:T(8,128)(2,1)S(1)}, u32[]{:S(2)}, u32[]{:S(2)}) collective-permute-start(bf16[64,1152]{1,0:T(8,128)(2,1)S(1)} %collective-permute-done.17.refs_4_), channel_id=1, source_target_pairs={{0,1},{1,0},{2,3},{3,2},{4,5},{5,4},{6,7},{7,6},{8,9},{9,8},{10,11... | collective-permute-start | bytes 442376 | tf_op jit(solution)/shard_map/ppermute | solution.py:277
  43.2 8.2 %collective-permute-start.21 = (bf16[64,1152]{1,0:T(8,128)(2,1)S(1)}, bf16[64,1152]{1,0:T(8,128)(2,1)S(1)}, u32[]{:S(2)}, u32[]{:S(2)}) collective-permute-start(bf16[64,1152]{1,0:T(8,128)(2,1)S(1)} %collective-permute-done.17.refs_4_), channel_id=1, source_target_pairs={{0,2},{1,3},{2,0},{3,1},{4,6},{5,7},{6,4},{7,5},{8,10},{9,11},{10,... | collective-permute-start | bytes 442376 | tf_op jit(solution)/shard_map/ppermute | solution.py:277
  48.9 6.7 %collective-permute-start.20 = (bf16[64,1152]{1,0:T(8,128)(2,1)S(1)}, bf16[64,1152]{1,0:T(8,128)(2,1)S(1)}, u32[]{:S(2)}, u32[]{:S(2)}) collective-permute-start(bf16[64,1152]{1,0:T(8,128)(2,1)S(1)} %collective-permute-done.16.refs_3_), channel_id=1, source_target_pairs={{0,2},{1,3},{2,0},{3,1},{4,6},{5,7},{6,4},{7,5},{8,10},{9,11},{10,... | collective-permute-start | bytes 442376 | tf_op jit(solution)/shard_map/ppermute | solution.py:277
  50.6 6.8 %collective-permute-start.19 = (bf16[64,1152]{1,0:T(8,128)(2,1)S(1)}, bf16[64,1152]{1,0:T(8,128)(2,1)S(1)}, u32[]{:S(2)}, u32[]{:S(2)}) collective-permute-start(bf16[64,1152]{1,0:T(8,128)(2,1)S(1)} %collective-permute-done.15.refs_2_), channel_id=1, source_target_pairs={{0,2},{1,3},{2,0},{3,1},{4,6},{5,7},{6,4},{7,5},{8,10},{9,11},{10,... | collective-permute-start | bytes 442376 | tf_op jit(solution)/shard_map/ppermute | solution.py:277
  50.9 6.6 %collective-permute-start.24 = (bf16[64,1152]{1,0:T(8,128)(2,1)S(1)}, bf16[64,1152]{1,0:T(8,128)(2,1)S(1)}, u32[]{:S(2)}, u32[]{:S(2)}) collective-permute-start(bf16[64,1152]{1,0:T(8,128)(2,1)S(1)} %collective-permute-done.16.refs_3_), channel_id=1, source_target_pairs={{0,1},{1,0},{2,3},{3,2},{4,5},{5,4},{6,7},{7,6},{8,9},{9,8},{10,11... | collective-permute-start | bytes 442376 | tf_op jit(solution)/shard_map/ppermute | solution.py:277
  50.9 6.6 %collective-permute-start.23 = (bf16[64,1152]{1,0:T(8,128)(2,1)S(1)}, bf16[64,1152]{1,0:T(8,128)(2,1)S(1)}, u32[]{:S(2)}, u32[]{:S(2)}) collective-permute-start(bf16[64,1152]{1,0:T(8,128)(2,1)S(1)} %collective-permute-done.15.refs_2_), channel_id=1, source_target_pairs={{0,1},{1,0},{2,3},{3,2},{4,5},{5,4},{6,7},{7,6},{8,9},{9,8},{10,11... | collective-permute-start | bytes 442376 | tf_op jit(solution)/shard_map/ppermute | solution.py:277
  51.4 6.1 %collective-permute-start.29 = (bf16[64,1152]{1,0:T(8,128)(2,1)S(1)}, bf16[64,1152]{1,0:T(8,128)(2,1)S(1)}, u32[]{:S(2)}, u32[]{:S(2)}) collective-permute-start(bf16[64,1152]{1,0:T(8,128)(2,1)S(1)} %collective-permute-done.21.refs_8_), channel_id=1, source_target_pairs={{0,1},{1,0},{2,3},{3,2},{4,5},{5,4},{6,7},{7,6},{8,9},{9,8},{10,11... | collective-permute-start | bytes 442376 | tf_op jit(solution)/shard_map/ppermute | solution.py:277
  55.6 2.0 %collective-permute-start.28 = (bf16[64,1152]{1,0:T(8,128)(2,1)S(1)}, bf16[64,1152]{1,0:T(8,128)(2,1)S(1)}, u32[]{:S(2)}, u32[]{:S(2)}) collective-permute-start(bf16[64,1152]{1,0:T(8,128)(2,1)S(1)} %collective-permute-done.20.refs_7_), channel_id=1, source_target_pairs={{0,1},{1,0},{2,3},{3,2},{4,5},{5,4},{6,7},{7,6},{8,9},{9,8},{10,11... | collective-permute-start | bytes 442376 | tf_op jit(solution)/shard_map/ppermute | solution.py:277
  57.4 1.4 %collective-permute-start.27 = (bf16[64,1152]{1,0:T(8,128)(2,1)S(1)}, bf16[64,1152]{1,0:T(8,128)(2,1)S(1)}, u32[]{:S(2)}, u32[]{:S(2)}) collective-permute-start(bf16[64,1152]{1,0:T(8,128)(2,1)S(1)} %collective-permute-done.19.refs_6_), channel_id=1, source_target_pairs={{0,1},{1,0},{2,3},{3,2},{4,5},{5,4},{6,7},{7,6},{8,9},{9,8},{10,11... | collective-permute-start | bytes 442376 | tf_op jit(solution)/shard_map/ppermute | solution.py:277
  65.6 5.9 %collective-permute-start.33 = (bf16[128,512]{1,0:T(8,128)(2,1)S(1)}, bf16[128,512]{1,0:T(8,128)(2,1)S(1)}, u32[]{:S(2)}, u32[]{:S(2)}) collective-permute-start(bf16[128,512]{1,0:T(8,128)(2,1)S(1)} %projection.1.refs_0_), channel_id=1, source_target_pairs={{0,2},{1,3},{2,0},{3,1},{4,6},{5,7},{6,4},{7,5},{8,10},{9,11},{10,... | collective-permute-start | bytes 393224 | tf_op jit(solution)/shard_map/ppermute | solution.py:277
  67.2 7.7 %collective-permute-start.32 = (bf16[128,512]{1,0:T(8,128)(2,1)S(1)}, bf16[128,512]{1,0:T(8,128)(2,1)S(1)}, u32[]{:S(2)}, u32[]{:S(2)}) collective-permute-start(bf16[128,512]{1,0:T(8,128)(2,1)S(1)} %projection.1.refs_0_), channel_id=1, source_target_pairs={{0,12},{1,13},{2,14},{3,15},{4,8},{5,9},{6,10},{7,11},{8,4},{9,5},... | collective-permute-start | bytes 393224 | tf_op jit(solution)/shard_map/ppermute | solution.py:277
  69.0 5.9 %collective-permute-start.37 = (bf16[128,512]{1,0:T(8,128)(2,1)S(1)}, bf16[128,512]{1,0:T(8,128)(2,1)S(1)}, u32[]{:S(2)}, u32[]{:S(2)}) collective-permute-start(bf16[128,512]{1,0:T(8,128)(2,1)S(1)} %projection.1.refs_0_), channel_id=1, source_target_pairs={{0,1},{1,0},{2,3},{3,2},{4,5},{5,4},{6,7},{7,6},{8,9},{9,8},{10,11... | collective-permute-start | bytes 393224 | tf_op jit(solution)/shard_map/ppermute | solution.py:277
  69.0 13.6 %collective-permute-start.31 = (bf16[128,512]{1,0:T(8,128)(2,1)S(1)}, bf16[128,512]{1,0:T(8,128)(2,1)S(1)}, u32[]{:S(2)}, u32[]{:S(2)}) collective-permute-start(bf16[128,512]{1,0:T(8,128)(2,1)S(1)} %projection.1.refs_0_), channel_id=1, source_target_pairs={{0,8},{1,9},{2,10},{3,11},{4,12},{5,13},{6,14},{7,15},{8,0},{9,1},... | collective-permute-start | bytes 393224 | tf_op jit(solution)/shard_map/ppermute | solution.py:277
  71.1 12.0 %collective-permute-start.30 = (bf16[128,512]{1,0:T(8,128)(2,1)S(1)}, bf16[128,512]{1,0:T(8,128)(2,1)S(1)}, u32[]{:S(2)}, u32[]{:S(2)}) collective-permute-start(bf16[128,512]{1,0:T(8,128)(2,1)S(1)} %projection.1.refs_0_), channel_id=1, source_target_pairs={{0,4},{1,5},{2,6},{3,7},{4,0},{5,1},{6,2},{7,3},{8,12},{9,13},{10,... | collective-permute-start | bytes 393224 | tf_op jit(solution)/shard_map/ppermute | solution.py:277
  71.6 13.1 %collective-permute-start.41 = (bf16[128,512]{1,0:T(8,128)(2,1)S(1)}, bf16[128,512]{1,0:T(8,128)(2,1)S(1)}, u32[]{:S(2)}, u32[]{:S(2)}) collective-permute-start(bf16[128,512]{1,0:T(8,128)(2,1)S(1)} %collective-permute-done.33.refs_4_), channel_id=1, source_target_pairs={{0,1},{1,0},{2,3},{3,2},{4,5},{5,4},{6,7},{7,6},{8,9},{9,8},{10,11... | collective-permute-start | bytes 393224 | tf_op jit(solution)/shard_map/ppermute | solution.py:277
  74.9 9.8 %collective-permute-start.40 = (bf16[128,512]{1,0:T(8,128)(2,1)S(1)}, bf16[128,512]{1,0:T(8,128)(2,1)S(1)}, u32[]{:S(2)}, u32[]{:S(2)}) collective-permute-start(bf16[128,512]{1,0:T(8,128)(2,1)S(1)} %collective-permute-done.32.refs_3_), channel_id=1, source_target_pairs={{0,1},{1,0},{2,3},{3,2},{4,5},{5,4},{6,7},{7,6},{8,9},{9,8},{10,11... | collective-permute-start | bytes 393224 | tf_op jit(solution)/shard_map/ppermute | solution.py:277
  74.9 10.3 %collective-permute-start.36 = (bf16[128,512]{1,0:T(8,128)(2,1)S(1)}, bf16[128,512]{1,0:T(8,128)(2,1)S(1)}, u32[]{:S(2)}, u32[]{:S(2)}) collective-permute-start(bf16[128,512]{1,0:T(8,128)(2,1)S(1)} %collective-permute-done.32.refs_3_), channel_id=1, source_target_pairs={{0,2},{1,3},{2,0},{3,1},{4,6},{5,7},{6,4},{7,5},{8,10},{9,11},{10,... | collective-permute-start | bytes 393224 | tf_op jit(solution)/shard_map/ppermute | solution.py:277
  82.7 6.4 %collective-permute-start.35 = (bf16[128,512]{1,0:T(8,128)(2,1)S(1)}, bf16[128,512]{1,0:T(8,128)(2,1)S(1)}, u32[]{:S(2)}, u32[]{:S(2)}) collective-permute-start(bf16[128,512]{1,0:T(8,128)(2,1)S(1)} %collective-permute-done.31.refs_2_), channel_id=1, source_target_pairs={{0,2},{1,3},{2,0},{3,1},{4,6},{5,7},{6,4},{7,5},{8,10},{9,11},{10,... | collective-permute-start | bytes 393224 | tf_op jit(solution)/shard_map/ppermute | solution.py:277
  83.2 7.7 %collective-permute-start.34 = (bf16[128,512]{1,0:T(8,128)(2,1)S(1)}, bf16[128,512]{1,0:T(8,128)(2,1)S(1)}, u32[]{:S(2)}, u32[]{:S(2)}) collective-permute-start(bf16[128,512]{1,0:T(8,128)(2,1)S(1)} %collective-permute-done.30.refs_1_), channel_id=1, source_target_pairs={{0,2},{1,3},{2,0},{3,1},{4,6},{5,7},{6,4},{7,5},{8,10},{9,11},{10,... | collective-permute-start | bytes 393224 | tf_op jit(solution)/shard_map/ppermute | solution.py:277
  84.7 6.9 %collective-permute-start.39 = (bf16[128,512]{1,0:T(8,128)(2,1)S(1)}, bf16[128,512]{1,0:T(8,128)(2,1)S(1)}, u32[]{:S(2)}, u32[]{:S(2)}) collective-permute-start(bf16[128,512]{1,0:T(8,128)(2,1)S(1)} %collective-permute-done.31.refs_2_), channel_id=1, source_target_pairs={{0,1},{1,0},{2,3},{3,2},{4,5},{5,4},{6,7},{7,6},{8,9},{9,8},{10,11... | collective-permute-start | bytes 393224 | tf_op jit(solution)/shard_map/ppermute | solution.py:277
  84.7 6.9 %collective-permute-start.38 = (bf16[128,512]{1,0:T(8,128)(2,1)S(1)}, bf16[128,512]{1,0:T(8,128)(2,1)S(1)}, u32[]{:S(2)}, u32[]{:S(2)}) collective-permute-start(bf16[128,512]{1,0:T(8,128)(2,1)S(1)} %collective-permute-done.30.refs_1_), channel_id=1, source_target_pairs={{0,1},{1,0},{2,3},{3,2},{4,5},{5,4},{6,7},{7,6},{8,9},{9,8},{10,11... | collective-permute-start | bytes 393224 | tf_op jit(solution)/shard_map/ppermute | solution.py:277
  85.2 6.3 %collective-permute-start.44 = (bf16[128,512]{1,0:T(8,128)(2,1)S(1)}, bf16[128,512]{1,0:T(8,128)(2,1)S(1)}, u32[]{:S(2)}, u32[]{:S(2)}) collective-permute-start(bf16[128,512]{1,0:T(8,128)(2,1)S(1)} %collective-permute-done.36.refs_7_), channel_id=1, source_target_pairs={{0,1},{1,0},{2,3},{3,2},{4,5},{5,4},{6,7},{7,6},{8,9},{9,8},{10,11... | collective-permute-start | bytes 393224 | tf_op jit(solution)/shard_map/ppermute | solution.py:277
  89.0 2.5 %collective-permute-start.43 = (bf16[128,512]{1,0:T(8,128)(2,1)S(1)}, bf16[128,512]{1,0:T(8,128)(2,1)S(1)}, u32[]{:S(2)}, u32[]{:S(2)}) collective-permute-start(bf16[128,512]{1,0:T(8,128)(2,1)S(1)} %collective-permute-done.35.refs_6_), channel_id=1, source_target_pairs={{0,1},{1,0},{2,3},{3,2},{4,5},{5,4},{6,7},{7,6},{8,9},{9,8},{10,11... | collective-permute-start | bytes 393224 | tf_op jit(solution)/shard_map/ppermute | solution.py:277
  90.9 1.3 %collective-permute-start.42 = (bf16[128,512]{1,0:T(8,128)(2,1)S(1)}, bf16[128,512]{1,0:T(8,128)(2,1)S(1)}, u32[]{:S(2)}, u32[]{:S(2)}) collective-permute-start(bf16[128,512]{1,0:T(8,128)(2,1)S(1)} %collective-permute-done.34.refs_5_), channel_id=1, source_target_pairs={{0,1},{1,0},{2,3},{3,2},{4,5},{5,4},{6,7},{7,6},{8,9},{9,8},{10,11... | collective-permute-start | bytes 393224 | tf_op jit(solution)/shard_map/ppermute | solution.py:277
where the time goes:
time: 98.5 us; the launch traced here: 98.3 us
  starting transfers between devices  36.3 us (37%)
  waiting for transfers between devices  33.8 us (34%)
  Pallas kernels  20.6 us (21%)
  between operations  3.57 us (4%)
  other arithmetic  3.26 us (3%)
    ppermute x45, starting transfers between devices, swap(): return lax.ppermute(value, 'wide', [(i, i ^ bits) for i in range(devices)])  36.3 us
    ppermute x45, waiting for transfers between devices, swap(): return lax.ppermute(value, 'wide', [(i, i ^ bits) for i in range(devices)])  33.8 us
    pallas_call x1, Pallas kernels, attention(): pl.pallas_call(functools.partial(attention_kernel, pieces, sequences, row...  7.81 us
    pallas_call x1, Pallas kernels, projection(): pl.pallas_call(functools.partial(projection_kernel, pieces, per_pair, key...  6.86 us
    pallas_call x1, Pallas kernels, feed(): pl.pallas_call(functools.partial(feed_kernel, pieces), out_shape=jax.Shap...  5.97 us
  transfers between devices with their start and end apart: 45, of which 14 were waited for; matrix products, arithmetic and copies ran while one was open for 3% of the time, Pallas kernels for 0%

commit v1 on v0

--- a/solution.py
+++ b/solution.py
@@ -17,7 +17,7 @@
 
 def attention_kernel(pieces, sequences, rows, group, head_size, info, order, *refs):
     blocks = refs[:pieces]
-    mask, keys, values, out, land, q, top, total, acc, sem = refs[pieces:]
+    mask, keys, values, out, land, q, top, total, acc = refs[pieces:]
     step = pl.program_id(0)
     block = keys.shape[0]
     length, own_sequence, own_head, is_last = info[0], info[1], info[2], info[3]
@@ -56,15 +56,12 @@
         sources = pieces // sequences
         extent = land.shape[2]
         columns = pl.ds(pl.multiple_of(own_head * extent, lanes), extent)
-        for phase in range(2):
-            for piece in range(pieces):
-                slot = order[piece] % sources
-                copy = pltpu.make_async_copy(
-                    blocks[piece].at[:, columns], land.at[slot], sem.at[slot]
-                )
-                pl.when(order[piece] // sources == own_sequence)(
-                    copy.wait if phase else copy.start
-                )
+        for piece in range(pieces):
+
+            @pl.when(order[piece] // sources == own_sequence)
+            def _(piece=piece):
+                land[order[piece] % sources] = blocks[piece][:, columns]
+
         mine = land[...].reshape(rows, land.shape[2])
         for head in range(group):
             q[head * rows : (head + 1) * rows, :] = mine[:, head * head_size : (head + 1) * head_size]
@@ -132,7 +129,7 @@
         grid_spec=pltpu.PrefetchScalarGridSpec(
             num_scalar_prefetch=2,
             grid=(capacity // block,),
-            in_specs=[pl.BlockSpec(memory_space=pl.ANY)] * pieces
+            in_specs=[pl.BlockSpec(memory_space=pltpu.VMEM)] * pieces
             + [
                 pl.BlockSpec((1, rows, rows), lambda step, info, order: (info[1], 0, 0)),
                 pl.BlockSpec((block, head_size), at),
@@ -145,7 +142,6 @@
                 pltpu.VMEM((group * rows, lanes), jnp.float32),
                 pltpu.VMEM((group * rows, lanes), jnp.float32),
                 pltpu.VMEM((group * rows, head_size), jnp.float32),
-                pltpu.SemaphoreType.DMA((pieces // sequences,)),
             ],
         ),
         compiler_params=pltpu.CompilerParams(vmem_limit_bytes=16 << 20),
@@ -163,16 +159,11 @@
     blocks = refs[1 : 1 + pieces]
     weight = refs[1 + pieces]
     out = refs[2 + pieces]
-    held, attended, piece_sem = refs[3 + pieces :]
+    held, attended = refs[3 + pieces :]
     rows = held.shape[1]
     width = group * head_size
-    copies = []
     for piece in range(pieces):
-        copy = pltpu.make_async_copy(blocks[piece], held.at[piece], piece_sem.at[piece])
-        copy.start()
-        copies.append(copy)
-    for copy in copies:
-        copy.wait()
+        held[piece] = blocks[piece][...]
     for head in range(key_heads):
         for sequence in range(sequences):
             pair = sequence * key_heads + head
@@ -213,13 +204,11 @@
         ),
         out_shape=pltpu.VMEM((sequences * rows, weight.shape[1]), jnp.bfloat16),
         in_specs=[pl.BlockSpec(memory_space=pltpu.SMEM)]
-        + [pl.BlockSpec(memory_space=pl.ANY)] * pieces
-        + [pl.BlockSpec(memory_space=pltpu.VMEM)],
+        + [pl.BlockSpec(memory_space=pltpu.VMEM)] * (pieces + 1),
         out_specs=pl.BlockSpec(memory_space=pltpu.VMEM),
         scratch_shapes=[
             pltpu.VMEM((pieces, rows, extent), jnp.bfloat16),
             pltpu.VMEM((sequences * rows, weight.shape[0]), jnp.bfloat16),
-            pltpu.SemaphoreType.DMA((pieces,)),
         ],
         compiler_params=pltpu.CompilerParams(vmem_limit_bytes=16 << 20),
         cost_estimate=pl.CostEstimate(
@@ -231,22 +220,53 @@
     )(where_from, *blocks, weight)
 
 
-def feed_kernel(pieces, order, *refs):
-    blocks = refs[:pieces]
-    gain, gate_weight, up_weight, out, gate, up = refs[pieces:]
-    rows, depth = blocks[0].shape
-    squares = jnp.zeros((rows, lanes), jnp.float32)
-    for piece in range(pieces):
-        branch = blocks[piece][...].astype(jnp.float32)
+def multiply(order, slots, blocks, gain, weights, totals, squares, fresh):
+    for slot, block in zip(slots, blocks):
+        depth = block.shape[1]
+        branch = block[...].astype(jnp.float32)
         square = branch * branch
         for at in range(0, depth, lanes):
             squares = squares + square[:, at : at + lanes]
-        scaled = (branch * gain[order[piece]]).astype(jnp.bfloat16)
-        part = pl.ds(pl.multiple_of(order[piece] * depth, depth), depth)
-        for weight, total in ((gate_weight, gate), (up_weight, up)):
+        scaled = (branch * gain[order[slot]]).astype(jnp.bfloat16)
+        part = pl.ds(pl.multiple_of(order[slot] * depth, depth), depth)
+        for weight, total in zip(weights, totals):
             term = jnp.dot(scaled, weight[part, :], preferred_element_type=jnp.float32)
-            total[...] = term if piece == 0 else total[...] + term
-    inverse = lax.rsqrt(jnp.sum(squares, axis=1, keepdims=True) / (pieces * depth) + epsilon)
+            total[...] = term if fresh else total[...] + term
+        fresh = False
+    return squares
+
+
+def feed_first_kernel(slots, order, *refs):
+    blocks = refs[: len(slots)]
+    gain, gate_weight, up_weight, gate, up, squares = refs[len(slots) :]
+    squares[...] = multiply(
+        order,
+        slots,
+        blocks,
+        gain,
+        (gate_weight, up_weight),
+        (gate, up),
+        jnp.zeros(squares.shape, jnp.float32),
+        True,
+    )
+
+
+def feed_last_kernel(slots, total_width, order, *refs):
+    blocks = refs[: len(slots)]
+    gain, gate_weight, up_weight, gate_in, up_in, squares, out, gate, up = refs[len(slots) :]
+    gate[...] = gate_in[...]
+    up[...] = up_in[...]
+    total = multiply(
+        order,
+        slots,
+        blocks,
+        gain,
+        (gate_weight, up_weight),
+        (gate, up),
+        squares[...],
+        False,
+    )
+    inverse = lax.rsqrt(jnp.sum(total, axis=1, keepdims=True) / total_width + epsilon)
     opened = gate[...] * inverse
     out[...] = (opened / (1.0 + jnp.exp(-opened)) * (up[...] * inverse)).astype(jnp.bfloat16)
 
@@ -255,21 +275,47 @@
     pieces = len(blocks)
     rows, depth = blocks[0].shape
     width = gate_weight.shape[1]
+    far = pieces // 4
+    late = [far + number for number in range(1, far, 2)]
+    late = late + [2 * far + number for number in late]
+    early = [slot for slot in range(pieces) if slot not in late]
     whole = pl.BlockSpec(memory_space=pltpu.VMEM)
-    return pl.pallas_call(
-        functools.partial(feed_kernel, pieces),
-        out_shape=jax.ShapeDtypeStruct((rows, width), jnp.bfloat16),
-        in_specs=[pl.BlockSpec(memory_space=pltpu.SMEM)] + [whole] * (pieces + 3),
-        out_specs=whole,
-        scratch_shapes=[pltpu.VMEM((rows, width), jnp.float32)] * 2,
-        compiler_params=pltpu.CompilerParams(vmem_limit_bytes=16 << 20),
-        cost_estimate=pl.CostEstimate(
-            flops=4 * rows * pieces * depth * width,
-            bytes_accessed=2 * rows * pieces * depth,
-            transcendentals=rows * width,
+    table = gain.reshape(pieces, 1, depth)
+
+    def call(kernel, slots, extra, out_shape, scratch):
+        return pl.pallas_call(
+            kernel,
+            out_shape=out_shape,
+            in_specs=[pl.BlockSpec(memory_space=pltpu.SMEM)]
+            + [whole] * (len(slots) + 3 + len(extra)),
+            out_specs=jax.tree.map(lambda _: whole, out_shape),
+            scratch_shapes=scratch,
+            compiler_params=pltpu.CompilerParams(vmem_limit_bytes=16 << 20),
+            cost_estimate=pl.CostEstimate(
+                flops=4 * rows * len(slots) * depth * width,
+                bytes_accessed=2 * rows * len(slots) * depth,
+                transcendentals=0,
+            ),
+        )(order, *[blocks[slot] for slot in slots], table, gate_weight, up_weight, *extra)
+
+    sums = call(
+        functools.partial(feed_first_kernel, early),
+        early,
+        (),
+        (
+            jax.ShapeDtypeStruct((rows, width), jnp.float32),
+            jax.ShapeDtypeStruct((rows, width), jnp.float32),
+            jax.ShapeDtypeStruct((rows, lanes), jnp.float32),
         ),
-        name="feed",
-    )(order, *blocks, gain.reshape(pieces, 1, depth), gate_weight, up_weight)
+        (),
+    )
+    return call(
+        functools.partial(feed_last_kernel, late, pieces * depth),
+        late,
+        sums,
+        jax.ShapeDtypeStruct((rows, width), jnp.bfloat16),
+        [pltpu.VMEM((rows, width), jnp.float32)] * 2,
+    )
 
 
 def spread(block, devices):
@@ -313,12 +359,13 @@
     local_rows = queries.shape[0]
     per_pair = devices // (sequences * key_heads)
     device_ids = jnp.arange(devices, dtype=jnp.int32)
-    mine = (block_owner == own_index).astype(jnp.int32)
-    own_block = jnp.sum(mine * device_ids)
-    own_length = jnp.sum(mine * block_lengths)
-    own_pair = own_block // per_pair
-    is_last = (own_block % per_pair == per_pair - 1).astype(jnp.int32)
-    info = jnp.stack([own_length, own_pair // key_heads, own_pair % key_heads, is_last])
+    pair = device_ids // per_pair
+    facts = jnp.stack(
+        [block_lengths, pair // key_heads, pair % key_heads, device_ids % per_pair // (per_pair - 1)]
+        if per_pair > 1
+        else [block_lengths, pair // key_heads, pair % key_heads, jnp.ones_like(device_ids)]
+    )
+    info = jnp.sum(jnp.where((block_owner == own_index)[None, :], facts, 0), axis=1)
     order = origins(devices, own_index)
     slot_of = jnp.sum(
         (block_owner[:, None] == order[None, :]).astype(jnp.int32) * device_ids[None, :], axis=1

time: 98.5 us -> 92.4 us (0.938)
  starting transfers between devices: 36.3 us -> 33.1 us
  Pallas kernels: 20.6 us -> 17.7 us
  between operations: 3.57 us -> 0.91 us
  waiting for transfers between devices: 33.8 us -> 36.4 us
    pallas_call x1, Pallas kernels: 6.86 us -> 3.56 us  [projection(): pl.pallas_call(functools.partial(projection_kernel, pieces, per_pair, key...]
    ppermute x45, starting transfers between devices: 36.3 us -> 33.1 us  [swap(): return lax.ppermute(value, 'wide', [(i, i ^ bits) for i in range(devices)])]
    ppermute x45, waiting for transfers between devices: 33.8 us -> 36.4 us  [swap(): return lax.ppermute(value, 'wide', [(i, i ^ bits) for i in range(devices)])]
    pallas_call x1 -> x2, Pallas kernels: 5.97 us -> 6.65 us  [call(): pl.pallas_call(kernel, out_shape=out_shape, in_specs=[pl.BlockSpec(memory...]
  transfers between devices with their start and end apart: 45 -> 45, of which waited for: 14 -> 18; matrix products, arithmetic and copies ran while one was open for 3% -> 3% of each run, Pallas kernels for 0% -> 4%
where the time goes in v1:
time: 92.4 us; the launch traced here: 91.4 us
  waiting for transfers between devices  36.4 us (39%)
  starting transfers between devices  33.1 us (36%)
  Pallas kernels  17.7 us (19%)
  other arithmetic  2.54 us (3%)
    ppermute x45, waiting for transfers between devices, swap(): return lax.ppermute(value, 'wide', [(i, i ^ bits) for i in range(devices)])  36.4 us
    ppermute x45, starting transfers between devices, swap(): return lax.ppermute(value, 'wide', [(i, i ^ bits) for i in range(devices)])  33.1 us
    pallas_call x1, Pallas kernels, attention(): pl.pallas_call(functools.partial(attention_kernel, pieces, sequences, row...  7.51 us
    pallas_call x2, Pallas kernels, call(): pl.pallas_call(kernel, out_shape=out_shape, in_specs=[pl.BlockSpec(memory...  6.65 us
    pallas_call x1, Pallas kernels, projection(): pl.pallas_call(functools.partial(projection_kernel, pieces, per_pair, key...  3.56 us
  transfers between devices with their start and end apart: 45, of which 18 were waited for; matrix products, arithmetic and copies ran while one was open for 3% of the time, Pallas kernels for 4%

profile of v1, /device:TPU:0, one launch (start us, length us, event | category | flops | bytes accessed | tf_op | source)
XLA Modules:
  0.0 91.4 jit_solution(3829882941132174126)
XLA Ops:
  0.6 0.9 pad_maximum_fusion
  1.5 3.1 %collective-permute-start = (bf16[8,5120]{1,0:T(8,128)(2,1)S(1)}, bf16[8,5120]{1,0:T(8,128)(2,1)S(1)}, u32[]{:S(2)}, u32[]{:S(2)}) collective-permute-start(bf16[8,5120]{1,0:T(8,128)(2,1)S(1)} %bitcast.12), channel_id=1, source_target_pairs={{0,4},{1,5},{2,6},{3,7},{4,0},{5,1},{6,2},{7,3},{8,12},{9,13},{10,... | collective-permute-start | bytes 245768 | tf_op jit(solution)/shard_map/ppermute | solution.py:323
  4.6 2.6 %collective-permute-start.1 = (bf16[8,5120]{1,0:T(8,128)(2,1)S(1)}, bf16[8,5120]{1,0:T(8,128)(2,1)S(1)}, u32[]{:S(2)}, u32[]{:S(2)}) collective-permute-start(bf16[8,5120]{1,0:T(8,128)(2,1)S(1)} %bitcast.13), channel_id=1, source_target_pairs={{0,8},{1,9},{2,10},{3,11},{4,12},{5,13},{6,14},{7,15},{8,0},{9,1},... | collective-permute-start | bytes 245768 | tf_op jit(solution)/shard_map/ppermute | solution.py:323
  7.2 0.0 collective-permute-start.2
  7.2 1.7 %collective-permute-start.3 = (bf16[8,5120]{1,0:T(8,128)(2,1)S(1)}, bf16[8,5120]{1,0:T(8,128)(2,1)S(1)}, u32[]{:S(2)}, u32[]{:S(2)}) collective-permute-start(bf16[8,5120]{1,0:T(8,128)(2,1)S(1)} %bitcast.15), channel_id=1, source_target_pairs={{0,2},{1,3},{2,0},{3,1},{4,6},{5,7},{6,4},{7,5},{8,10},{9,11},{10,... | collective-permute-start | bytes 245768 | tf_op jit(solution)/shard_map/ppermute | solution.py:323
  8.9 0.0 collective-permute-start.7
  8.9 0.7 broadcast_compare_fusion
  9.6 3.9 %collective-permute-done.2.refs_3_ = bf16[8,5120]{1,0:T(8,128)(2,1)S(1)} collective-permute-done((bf16[8,5120]{1,0:T(8,128)(2,1)S(1)}, bf16[8,5120]{1,0:T(8,128)(2,1)S(1)}, u32[]{:S(2)}, u32[]{:S(2)}) %collective-permute-start.2) | collective-permute-done | bytes 81952 | tf_op jit(solution)/shard_map/ppermute | solution.py:323
  13.5 1.5 %collective-permute-start.6 = (bf16[8,5120]{1,0:T(8,128)(2,1)S(1)}, bf16[8,5120]{1,0:T(8,128)(2,1)S(1)}, u32[]{:S(2)}, u32[]{:S(2)}) collective-permute-start(bf16[8,5120]{1,0:T(8,128)(2,1)S(1)} %collective-permute-done.2.refs_3_), channel_id=1, source_target_pairs={{0,2},{1,3},{2,0},{3,1},{4,6},{5,7},{6,4},{7,5},{8,10},{9,11},{10,... | collective-permute-start | bytes 245768 | tf_op jit(solution)/shard_map/ppermute | solution.py:323
  15.0 0.0 collective-permute-start.10
  15.0 0.0 collective-permute-done.1.refs_2_
  15.0 0.6 collective-permute-start.4
  15.6 0.2 collective-permute-start.8
  15.8 1.5 %collective-permute-start.5 = (bf16[8,5120]{1,0:T(8,128)(2,1)S(1)}, bf16[8,5120]{1,0:T(8,128)(2,1)S(1)}, u32[]{:S(2)}, u32[]{:S(2)}) collective-permute-start(bf16[8,5120]{1,0:T(8,128)(2,1)S(1)} %collective-permute-done.1.refs_2_), channel_id=1, source_target_pairs={{0,2},{1,3},{2,0},{3,1},{4,6},{5,7},{6,4},{7,5},{8,10},{9,11},{10,... | collective-permute-start | bytes 245768 | tf_op jit(solution)/shard_map/ppermute | solution.py:323
  17.3 0.8 fusion.info
  18.1 2.3 %collective-permute-done.4.refs_5_ = bf16[8,5120]{1,0:T(8,128)(2,1)S(1)} collective-permute-done((bf16[8,5120]{1,0:T(8,128)(2,1)S(1)}, bf16[8,5120]{1,0:T(8,128)(2,1)S(1)}, u32[]{:S(2)}, u32[]{:S(2)}) %collective-permute-start.4) | collective-permute-done | bytes 81952 | tf_op jit(solution)/shard_map/ppermute | solution.py:323
  20.4 1.2 %collective-permute-done.5.refs_6_ = bf16[8,5120]{1,0:T(8,128)(2,1)S(1)} collective-permute-done((bf16[8,5120]{1,0:T(8,128)(2,1)S(1)}, bf16[8,5120]{1,0:T(8,128)(2,1)S(1)}, u32[]{:S(2)}, u32[]{:S(2)}) %collective-permute-start.5) | collective-permute-done | bytes 81952 | tf_op jit(solution)/shard_map/ppermute | solution.py:323
  21.7 0.5 collective-permute-start.12
  22.2 0.1 collective-permute-start.13
  22.2 0.4 collective-permute-start.14
  22.7 0.0 copy-start.2
  22.7 0.0 copy-start
  22.7 0.0 slice-start.1
  22.8 0.0 slice-start.5
  22.8 0.1 collective-permute-done.11.refs_12_
  22.9 0.2 collective-permute-done.12.refs_13_
  23.1 0.4 collective-permute-done.13.refs_14_
  23.5 0.2 collective-permute-done.14.refs_15_
  23.6 7.5 %attention.1.refs_1_ = bf16[64,1152]{1,0:T(8,128)(2,1)S(1)} custom-call(s32[4]{0:T(128)S(1)} %fusion.info, s32[16]{0:T(128)S(1)} %fusion.5.order, bf16[8,5120]{1,0:T(8,128)(2,1)S(1)} %bitcast.17, bf16[8,5120]{1,0:T(8,128)(2,1)S(1)} %collective-permute-done.refs_1_, bf16[8,5120]{1,0:T(8,128)(2,1)S(1)} %collective-permute-done.1.refs_2_, ...), custom_call_target="tpu_custom_call" | custom-call | flops 34359738368 | bytes 4194304 | tf_op jit(solution)/shard_map/attention/pallas_call | solution.py:126
  31.1 0.0 copy-start.1
  31.1 4.5 %collective-permute-start.15 = (bf16[64,1152]{1,0:T(8,128)(2,1)S(1)}, bf16[64,1152]{1,0:T(8,128)(2,1)S(1)}, u32[]{:S(2)}, u32[]{:S(2)}) collective-permute-start(bf16[64,1152]{1,0:T(8,128)(2,1)S(1)} %attention.1.refs_1_), channel_id=1, source_target_pairs={{0,4},{1,5},{2,6},{3,7},{4,0},{5,1},{6,2},{7,3},{8,12},{9,13},{10,... | collective-permute-start | bytes 442376 | tf_op jit(solution)/shard_map/ppermute | solution.py:323
  35.7 2.4 %collective-permute-start.17 = (bf16[64,1152]{1,0:T(8,128)(2,1)S(1)}, bf16[64,1152]{1,0:T(8,128)(2,1)S(1)}, u32[]{:S(2)}, u32[]{:S(2)}) collective-permute-start(bf16[64,1152]{1,0:T(8,128)(2,1)S(1)} %attention.1.refs_1_), channel_id=1, source_target_pairs={{0,12},{1,13},{2,14},{3,15},{4,8},{5,9},{6,10},{7,11},{8,4},{9,5},... | collective-permute-start | bytes 442376 | tf_op jit(solution)/shard_map/ppermute | solution.py:323
  38.1 2.6 %collective-permute-start.22 = (bf16[64,1152]{1,0:T(8,128)(2,1)S(1)}, bf16[64,1152]{1,0:T(8,128)(2,1)S(1)}, u32[]{:S(2)}, u32[]{:S(2)}) collective-permute-start(bf16[64,1152]{1,0:T(8,128)(2,1)S(1)} %attention.1.refs_1_), channel_id=1, source_target_pairs={{0,1},{1,0},{2,3},{3,2},{4,5},{5,4},{6,7},{7,6},{8,9},{9,8},{10,11... | collective-permute-start | bytes 442376 | tf_op jit(solution)/shard_map/ppermute | solution.py:323
  40.7 1.7 %collective-permute-start.19 = (bf16[64,1152]{1,0:T(8,128)(2,1)S(1)}, bf16[64,1152]{1,0:T(8,128)(2,1)S(1)}, u32[]{:S(2)}, u32[]{:S(2)}) collective-permute-start(bf16[64,1152]{1,0:T(8,128)(2,1)S(1)} %collective-permute-done.15.refs_2_), channel_id=1, source_target_pairs={{0,2},{1,3},{2,0},{3,1},{4,6},{5,7},{6,4},{7,5},{8,10},{9,11},{10,... | collective-permute-start | bytes 442376 | tf_op jit(solution)/shard_map/ppermute | solution.py:323
  42.5 6.6 %collective-permute-done.16.refs_3_ = bf16[64,1152]{1,0:T(8,128)(2,1)S(1)} collective-permute-done((bf16[64,1152]{1,0:T(8,128)(2,1)S(1)}, bf16[64,1152]{1,0:T(8,128)(2,1)S(1)}, u32[]{:S(2)}, u32[]{:S(2)}) %collective-permute-start.16) | collective-permute-done | bytes 147488 | tf_op jit(solution)/shard_map/ppermute | solution.py:323
  49.1 2.0 %collective-permute-start.21 = (bf16[64,1152]{1,0:T(8,128)(2,1)S(1)}, bf16[64,1152]{1,0:T(8,128)(2,1)S(1)}, u32[]{:S(2)}, u32[]{:S(2)}) collective-permute-start(bf16[64,1152]{1,0:T(8,128)(2,1)S(1)} %collective-permute-done.17.refs_4_), channel_id=1, source_target_pairs={{0,2},{1,3},{2,0},{3,1},{4,6},{5,7},{6,4},{7,5},{8,10},{9,11},{10,... | collective-permute-start | bytes 442376 | tf_op jit(solution)/shard_map/ppermute | solution.py:323
  51.1 0.5 collective-permute-start.24
  51.6 0.1 collective-permute-start.25
  51.7 4.1 %collective-permute-done.20.refs_7_ = bf16[64,1152]{1,0:T(8,128)(2,1)S(1)} collective-permute-done((bf16[64,1152]{1,0:T(8,128)(2,1)S(1)}, bf16[64,1152]{1,0:T(8,128)(2,1)S(1)}, u32[]{:S(2)}, u32[]{:S(2)}) %collective-permute-start.20) | collective-permute-done | bytes 147488 | tf_op jit(solution)/shard_map/ppermute | solution.py:323
  55.8 2.3 %collective-permute-done.21.refs_8_ = bf16[64,1152]{1,0:T(8,128)(2,1)S(1)} collective-permute-done((bf16[64,1152]{1,0:T(8,128)(2,1)S(1)}, bf16[64,1152]{1,0:T(8,128)(2,1)S(1)}, u32[]{:S(2)}, u32[]{:S(2)}) %collective-permute-start.21) | collective-permute-done | bytes 147488 | tf_op jit(solution)/shard_map/ppermute | solution.py:323
  58.1 0.5 collective-permute-start.28
  58.6 0.1 collective-permute-start.29
  58.7 0.2 select_reduce_fusion.refs_0_
  58.9 0.6 collective-permute-done.27.refs_14_
  59.5 0.2 collective-permute-done.28.refs_15_
  59.7 0.3 collective-permute-done.29.refs_16_
  60.0 3.6 %projection.1.refs_0_ = bf16[128,512]{1,0:T(8,128)(2,1)S(1)} custom-call(s32[16]{0:T(128)S(1)} %select_reduce_fusion.refs_0_, bf16[64,1152]{1,0:T(8,128)(2,1)S(1)} %attention.1.refs_1_, bf16[64,1152]{1,0:T(8,128)(2,1)S(1)} %collective-permute-done.15.refs_2_, bf16[64,1152]{1,0:T(8,128)(2,1)S(1)} %collective-permute-done.16.refs_3_, ...), custom_call_target="tpu_custom_call" | custom-call | flops 536870912 | bytes 6553600 | tf_op jit(solution)/shard_map/projection/pallas_call | solution.py:201
  63.5 0.1 collective-permute-start.36
  63.7 0.6 collective-permute-start.30
  64.3 3.7 %collective-permute-start.32 = (bf16[128,512]{1,0:T(8,128)(2,1)S(1)}, bf16[128,512]{1,0:T(8,128)(2,1)S(1)}, u32[]{:S(2)}, u32[]{:S(2)}) collective-permute-start(bf16[128,512]{1,0:T(8,128)(2,1)S(1)} %projection.1.refs_0_), channel_id=1, source_target_pairs={{0,12},{1,13},{2,14},{3,15},{4,8},{5,9},{6,10},{7,11},{8,4},{9,5},... | collective-permute-start | bytes 393224 | tf_op jit(solution)/shard_map/ppermute | solution.py:323
  68.0 0.3 collective-permute-start.37
  68.3 5.5 %collective-permute-done.36.refs_2_ = bf16[128,512]{1,0:T(8,128)(2,1)S(1)} collective-permute-done((bf16[128,512]{1,0:T(8,128)(2,1)S(1)}, bf16[128,512]{1,0:T(8,128)(2,1)S(1)}, u32[]{:S(2)}, u32[]{:S(2)}) %collective-permute-start.36) | collective-permute-done | bytes 131104 | tf_op jit(solution)/shard_map/ppermute | solution.py:323
  73.8 0.3 collective-permute-start.38
  74.1 1.8 %collective-permute-done.32.refs_3_ = bf16[128,512]{1,0:T(8,128)(2,1)S(1)} collective-permute-done((bf16[128,512]{1,0:T(8,128)(2,1)S(1)}, bf16[128,512]{1,0:T(8,128)(2,1)S(1)}, u32[]{:S(2)}, u32[]{:S(2)}) %collective-permute-start.32) | collective-permute-done | bytes 131104 | tf_op jit(solution)/shard_map/ppermute | solution.py:323
  75.9 0.5 collective-permute-start.31
  76.4 0.1 collective-permute-start.42
  76.5 2.5 %collective-permute-done.38.refs_5_ = bf16[128,512]{1,0:T(8,128)(2,1)S(1)} collective-permute-done((bf16[128,512]{1,0:T(8,128)(2,1)S(1)}, bf16[128,512]{1,0:T(8,128)(2,1)S(1)}, u32[]{:S(2)}, u32[]{:S(2)}) %collective-permute-start.38) | collective-permute-done | bytes 131104 | tf_op jit(solution)/shard_map/ppermute | solution.py:323
  79.0 0.3 collective-permute-start.33
  79.2 0.5 collective-permute-start.44
  79.8 0.7 copy.14
  80.4 1.9 %collective-permute-done.31.refs_0_ = bf16[128,512]{1,0:T(8,128)(2,1)S(1)} collective-permute-done((bf16[128,512]{1,0:T(8,128)(2,1)S(1)}, bf16[128,512]{1,0:T(8,128)(2,1)S(1)}, u32[]{:S(2)}, u32[]{:S(2)}) %collective-permute-start.31) | collective-permute-done | bytes 131104 | tf_op jit(solution)/shard_map/ppermute | solution.py:323
  82.3 2.3 %collective-permute-done.33.refs_1_ = bf16[128,512]{1,0:T(8,128)(2,1)S(1)} collective-permute-done((bf16[128,512]{1,0:T(8,128)(2,1)S(1)}, bf16[128,512]{1,0:T(8,128)(2,1)S(1)}, u32[]{:S(2)}, u32[]{:S(2)}) %collective-permute-start.33) | collective-permute-done | bytes 131104 | tf_op jit(solution)/shard_map/ppermute | solution.py:323
  84.7 4.1 %shard_map.131 = (f32[128,896]{1,0:T(8,128)S(1)}, f32[128,896]{1,0:T(8,128)S(1)}, f32[128,128]{1,0:T(8,128)S(1)}) custom-call(s32[16]{0:T(128)S(1)} %fusion.5.order, bf16[128,512]{1,0:T(8,128)(2,1)S(1)} %projection.1.refs_0_, bf16[128,512]{1,0:T(8,128)(2,1)S(1)} %collective-permute-done.30.refs_1_, bf16[128,512]{1,0:T(8,128)(2,1)S(1)} %collective-permute-done.36.refs_2_, ...), custom_call_target="tpu_custom_call" | custom-call | flops 2818572288 | bytes 1572864 | tf_op jit(solution)/shard_map/pallas_call | solution.py:286
  88.8 2.6 %shard_map.132 = bf16[128,896]{1,0:T(8,128)(2,1)} custom-call(s32[16]{0:T(128)S(1)} %fusion.5.order, bf16[128,512]{1,0:T(8,128)(2,1)S(1)} %collective-permute-done.31.refs_0_, bf16[128,512]{1,0:T(8,128)(2,1)S(1)} %collective-permute-done.33.refs_1_, bf16[128,512]{1,0:T(8,128)(2,1)S(1)} %collective-permute-done.34.refs_2_, ...), custom_call_target="tpu_custom_call" | custom-call | flops 939524096 | bytes 524288 | tf_op jit(solution)/shard_map/pallas_call | solution.py:286
  (62 shorter events, 0.2 us)
Async XLA Ops:
  1.5 13.5 %collective-permute-start = (bf16[8,5120]{1,0:T(8,128)(2,1)S(1)}, bf16[8,5120]{1,0:T(8,128)(2,1)S(1)}, u32[]{:S(2)}, u32[]{:S(2)}) collective-permute-start(bf16[8,5120]{1,0:T(8,128)(2,1)S(1)} %bitcast.12), channel_id=1, source_target_pairs={{0,4},{1,5},{2,6},{3,7},{4,0},{5,1},{6,2},{7,3},{8,12},{9,13},{10,... | collective-permute-start | bytes 245768 | tf_op jit(solution)/shard_map/ppermute | solution.py:323
  4.6 10.5 %collective-permute-start.1 = (bf16[8,5120]{1,0:T(8,128)(2,1)S(1)}, bf16[8,5120]{1,0:T(8,128)(2,1)S(1)}, u32[]{:S(2)}, u32[]{:S(2)}) collective-permute-start(bf16[8,5120]{1,0:T(8,128)(2,1)S(1)} %bitcast.13), channel_id=1, source_target_pairs={{0,8},{1,9},{2,10},{3,11},{4,12},{5,13},{6,14},{7,15},{8,0},{9,1},... | collective-permute-start | bytes 245768 | tf_op jit(solution)/shard_map/ppermute | solution.py:323
  7.2 6.3 %collective-permute-start.2 = (bf16[8,5120]{1,0:T(8,128)(2,1)S(1)}, bf16[8,5120]{1,0:T(8,128)(2,1)S(1)}, u32[]{:S(2)}, u32[]{:S(2)}) collective-permute-start(bf16[8,5120]{1,0:T(8,128)(2,1)S(1)} %bitcast.14), channel_id=1, source_target_pairs={{0,12},{1,13},{2,14},{3,15},{4,8},{5,9},{6,10},{7,11},{8,4},{9,5},... | collective-permute-start | bytes 245768 | tf_op jit(solution)/shard_map/ppermute | solution.py:323
  7.2 8.4 %collective-permute-start.3 = (bf16[8,5120]{1,0:T(8,128)(2,1)S(1)}, bf16[8,5120]{1,0:T(8,128)(2,1)S(1)}, u32[]{:S(2)}, u32[]{:S(2)}) collective-permute-start(bf16[8,5120]{1,0:T(8,128)(2,1)S(1)} %bitcast.15), channel_id=1, source_target_pairs={{0,2},{1,3},{2,0},{3,1},{4,6},{5,7},{6,4},{7,5},{8,10},{9,11},{10,... | collective-permute-start | bytes 245768 | tf_op jit(solution)/shard_map/ppermute | solution.py:323
  8.9 6.9 %collective-permute-start.7 = (bf16[8,5120]{1,0:T(8,128)(2,1)S(1)}, bf16[8,5120]{1,0:T(8,128)(2,1)S(1)}, u32[]{:S(2)}, u32[]{:S(2)}) collective-permute-start(bf16[8,5120]{1,0:T(8,128)(2,1)S(1)} %bitcast.16), channel_id=1, source_target_pairs={{0,1},{1,0},{2,3},{3,2},{4,5},{5,4},{6,7},{7,6},{8,9},{9,8},{10,11... | collective-permute-start | bytes 245768 | tf_op jit(solution)/shard_map/ppermute | solution.py:323
  13.5 8.1 %collective-permute-start.6 = (bf16[8,5120]{1,0:T(8,128)(2,1)S(1)}, bf16[8,5120]{1,0:T(8,128)(2,1)S(1)}, u32[]{:S(2)}, u32[]{:S(2)}) collective-permute-start(bf16[8,5120]{1,0:T(8,128)(2,1)S(1)} %collective-permute-done.2.refs_3_), channel_id=1, source_target_pairs={{0,2},{1,3},{2,0},{3,1},{4,6},{5,7},{6,4},{7,5},{8,10},{9,11},{10,... | collective-permute-start | bytes 245768 | tf_op jit(solution)/shard_map/ppermute | solution.py:323
  15.0 7.1 %collective-permute-start.10 = (bf16[8,5120]{1,0:T(8,128)(2,1)S(1)}, bf16[8,5120]{1,0:T(8,128)(2,1)S(1)}, u32[]{:S(2)}, u32[]{:S(2)}) collective-permute-start(bf16[8,5120]{1,0:T(8,128)(2,1)S(1)} %collective-permute-done.2.refs_3_), channel_id=1, source_target_pairs={{0,1},{1,0},{2,3},{3,2},{4,5},{5,4},{6,7},{7,6},{8,9},{9,8},{10,11... | collective-permute-start | bytes 245768 | tf_op jit(solution)/shard_map/ppermute | solution.py:323
  15.0 5.4 %collective-permute-start.4 = (bf16[8,5120]{1,0:T(8,128)(2,1)S(1)}, bf16[8,5120]{1,0:T(8,128)(2,1)S(1)}, u32[]{:S(2)}, u32[]{:S(2)}) collective-permute-start(bf16[8,5120]{1,0:T(8,128)(2,1)S(1)} %collective-permute-done.refs_1_), channel_id=1, source_target_pairs={{0,2},{1,3},{2,0},{3,1},{4,6},{5,7},{6,4},{7,5},{8,10},{9,11},{10,... | collective-permute-start | bytes 245768 | tf_op jit(solution)/shard_map/ppermute | solution.py:323
  15.6 6.6 %collective-permute-start.8 = (bf16[8,5120]{1,0:T(8,128)(2,1)S(1)}, bf16[8,5120]{1,0:T(8,128)(2,1)S(1)}, u32[]{:S(2)}, u32[]{:S(2)}) collective-permute-start(bf16[8,5120]{1,0:T(8,128)(2,1)S(1)} %collective-permute-done.refs_1_), channel_id=1, source_target_pairs={{0,1},{1,0},{2,3},{3,2},{4,5},{5,4},{6,7},{7,6},{8,9},{9,8},{10,11... | collective-permute-start | bytes 245768 | tf_op jit(solution)/shard_map/ppermute | solution.py:323
  15.8 5.9 %collective-permute-start.5 = (bf16[8,5120]{1,0:T(8,128)(2,1)S(1)}, bf16[8,5120]{1,0:T(8,128)(2,1)S(1)}, u32[]{:S(2)}, u32[]{:S(2)}) collective-permute-start(bf16[8,5120]{1,0:T(8,128)(2,1)S(1)} %collective-permute-done.1.refs_2_), channel_id=1, source_target_pairs={{0,2},{1,3},{2,0},{3,1},{4,6},{5,7},{6,4},{7,5},{8,10},{9,11},{10,... | collective-permute-start | bytes 245768 | tf_op jit(solution)/shard_map/ppermute | solution.py:323
  20.4 2.4 %collective-permute-start.9 = (bf16[8,5120]{1,0:T(8,128)(2,1)S(1)}, bf16[8,5120]{1,0:T(8,128)(2,1)S(1)}, u32[]{:S(2)}, u32[]{:S(2)}) collective-permute-start(bf16[8,5120]{1,0:T(8,128)(2,1)S(1)} %collective-permute-done.1.refs_2_), channel_id=1, source_target_pairs={{0,1},{1,0},{2,3},{3,2},{4,5},{5,4},{6,7},{7,6},{8,9},{9,8},{10,11... | collective-permute-start | bytes 245768 | tf_op jit(solution)/shard_map/ppermute | solution.py:323
  21.7 1.3 %collective-permute-start.11 = (bf16[8,5120]{1,0:T(8,128)(2,1)S(1)}, bf16[8,5120]{1,0:T(8,128)(2,1)S(1)}, u32[]{:S(2)}, u32[]{:S(2)}) collective-permute-start(bf16[8,5120]{1,0:T(8,128)(2,1)S(1)} %collective-permute-done.3.refs_4_), channel_id=1, source_target_pairs={{0,1},{1,0},{2,3},{3,2},{4,5},{5,4},{6,7},{7,6},{8,9},{9,8},{10,11... | collective-permute-start | bytes 245768 | tf_op jit(solution)/shard_map/ppermute | solution.py:323
  21.7 1.4 %collective-permute-start.12 = (bf16[8,5120]{1,0:T(8,128)(2,1)S(1)}, bf16[8,5120]{1,0:T(8,128)(2,1)S(1)}, u32[]{:S(2)}, u32[]{:S(2)}) collective-permute-start(bf16[8,5120]{1,0:T(8,128)(2,1)S(1)} %collective-permute-done.4.refs_5_), channel_id=1, source_target_pairs={{0,1},{1,0},{2,3},{3,2},{4,5},{5,4},{6,7},{7,6},{8,9},{9,8},{10,11... | collective-permute-start | bytes 245768 | tf_op jit(solution)/shard_map/ppermute | solution.py:323
  22.2 1.3 %collective-permute-start.13 = (bf16[8,5120]{1,0:T(8,128)(2,1)S(1)}, bf16[8,5120]{1,0:T(8,128)(2,1)S(1)}, u32[]{:S(2)}, u32[]{:S(2)}) collective-permute-start(bf16[8,5120]{1,0:T(8,128)(2,1)S(1)} %collective-permute-done.5.refs_6_), channel_id=1, source_target_pairs={{0,1},{1,0},{2,3},{3,2},{4,5},{5,4},{6,7},{7,6},{8,9},{9,8},{10,11... | collective-permute-start | bytes 245768 | tf_op jit(solution)/shard_map/ppermute | solution.py:323
  22.2 1.4 %collective-permute-start.14 = (bf16[8,5120]{1,0:T(8,128)(2,1)S(1)}, bf16[8,5120]{1,0:T(8,128)(2,1)S(1)}, u32[]{:S(2)}, u32[]{:S(2)}) collective-permute-start(bf16[8,5120]{1,0:T(8,128)(2,1)S(1)} %collective-permute-done.6.refs_7_), channel_id=1, source_target_pairs={{0,1},{1,0},{2,3},{3,2},{4,5},{5,4},{6,7},{7,6},{8,9},{9,8},{10,11... | collective-permute-start | bytes 245768 | tf_op jit(solution)/shard_map/ppermute | solution.py:323
  22.7 61.9 %slice-start = ((s8[14680064]{0:T(1024)(128)(4,1)}), s8[4194304]{0:T(1024)(128)(4,1)S(1)}, s32[]{:S(2)}) async-start(s8[14680064]{0:T(1024)(128)(4,1)} %bitcast.6), calls=%async_computation | async-start | bytes 8388608
  22.7 62.0 %slice-start.4 = ((s8[14680064]{0:T(1024)(128)(4,1)}), s8[4194304]{0:T(1024)(128)(4,1)S(1)}, s32[]{:S(2)}) async-start(s8[14680064]{0:T(1024)(128)(4,1)} %bitcast.8), calls=%async_computation.4 | async-start | bytes 8388608
  22.7 36.0 %copy-start.2 = (s32[16]{0:T(128)S(1)}, s32[16]{0:T(128)}, u32[]{:S(2)}) copy-start(s32[16]{0:T(128)} %param.17) | copy-start | bytes 196
  22.7 37.3 %copy-start = (bf16[4096,512]{1,0:T(8,128)(2,1)S(1)}, bf16[4096,512]{1,0:T(8,128)(2,1)}, u32[]{:S(2)}) copy-start(bf16[4096,512]{1,0:T(8,128)(2,1)} %refs_17_.3) | copy-start | bytes 12582916
  22.7 61.9 %slice-start.1 = ((s8[14680064]{0:T(1024)(128)(4,1)}), s8[4194304]{0:T(1024)(128)(4,1)S(1)}, s32[]{:S(2)}) async-start(s8[14680064]{0:T(1024)(128)(4,1)} %bitcast.6), calls=%async_computation.1 | async-start | bytes 8388608
  22.7 61.9 %slice-start.2 = ((s8[14680064]{0:T(1024)(128)(4,1)}), s8[4194304]{0:T(1024)(128)(4,1)S(1)}, s32[]{:S(2)}) async-start(s8[14680064]{0:T(1024)(128)(4,1)} %bitcast.6), calls=%async_computation.2 | async-start | bytes 8388608
  22.8 61.9 %slice-start.3 = ((s8[14680064]{0:T(1024)(128)(4,1)}), s8[2097152]{0:T(1024)(128)(4,1)S(1)}, s32[]{:S(2)}) async-start(s8[14680064]{0:T(1024)(128)(4,1)} %bitcast.6), calls=%async_computation.3 | async-start | bytes 4194304
  22.8 61.9 %slice-start.5 = ((s8[14680064]{0:T(1024)(128)(4,1)}), s8[4194304]{0:T(1024)(128)(4,1)S(1)}, s32[]{:S(2)}) async-start(s8[14680064]{0:T(1024)(128)(4,1)} %bitcast.8), calls=%async_computation.5 | async-start | bytes 8388608
  22.8 61.9 %slice-start.6 = ((s8[14680064]{0:T(1024)(128)(4,1)}), s8[4194304]{0:T(1024)(128)(4,1)S(1)}, s32[]{:S(2)}) async-start(s8[14680064]{0:T(1024)(128)(4,1)} %bitcast.8), calls=%async_computation.6 | async-start | bytes 8388608
  22.8 61.9 %slice-start.7 = ((s8[14680064]{0:T(1024)(128)(4,1)}), s8[2097152]{0:T(1024)(128)(4,1)S(1)}, s32[]{:S(2)}) async-start(s8[14680064]{0:T(1024)(128)(4,1)} %bitcast.8), calls=%async_computation.7 | async-start | bytes 4194304
  31.1 53.6 %copy-start.1 = (f32[8192]{0:T(1024)S(1)}, f32[8192]{0:T(1024)}, u32[]{:S(2)}) copy-start(f32[8192]{0:T(1024)} %param.21) | copy-start | bytes 98308
  31.1 9.6 %collective-permute-start.15 = (bf16[64,1152]{1,0:T(8,128)(2,1)S(1)}, bf16[64,1152]{1,0:T(8,128)(2,1)S(1)}, u32[]{:S(2)}, u32[]{:S(2)}) collective-permute-start(bf16[64,1152]{1,0:T(8,128)(2,1)S(1)} %attention.1.refs_1_), channel_id=1, source_target_pairs={{0,4},{1,5},{2,6},{3,7},{4,0},{5,1},{6,2},{7,3},{8,12},{9,13},{10,... | collective-permute-start | bytes 442376 | tf_op jit(solution)/shard_map/ppermute | solution.py:323
  35.7 13.4 %collective-permute-start.16 = (bf16[64,1152]{1,0:T(8,128)(2,1)S(1)}, bf16[64,1152]{1,0:T(8,128)(2,1)S(1)}, u32[]{:S(2)}, u32[]{:S(2)}) collective-permute-start(bf16[64,1152]{1,0:T(8,128)(2,1)S(1)} %attention.1.refs_1_), channel_id=1, source_target_pairs={{0,8},{1,9},{2,10},{3,11},{4,12},{5,13},{6,14},{7,15},{8,0},{9,1},... | collective-permute-start | bytes 442376 | tf_op jit(solution)/shard_map/ppermute | solution.py:323
  35.7 13.4 %collective-permute-start.17 = (bf16[64,1152]{1,0:T(8,128)(2,1)S(1)}, bf16[64,1152]{1,0:T(8,128)(2,1)S(1)}, u32[]{:S(2)}, u32[]{:S(2)}) collective-permute-start(bf16[64,1152]{1,0:T(8,128)(2,1)S(1)} %attention.1.refs_1_), channel_id=1, source_target_pairs={{0,12},{1,13},{2,14},{3,15},{4,8},{5,9},{6,10},{7,11},{8,4},{9,5},... | collective-permute-start | bytes 442376 | tf_op jit(solution)/shard_map/ppermute | solution.py:323
  38.1 13.0 %collective-permute-start.18 = (bf16[64,1152]{1,0:T(8,128)(2,1)S(1)}, bf16[64,1152]{1,0:T(8,128)(2,1)S(1)}, u32[]{:S(2)}, u32[]{:S(2)}) collective-permute-start(bf16[64,1152]{1,0:T(8,128)(2,1)S(1)} %attention.1.refs_1_), channel_id=1, source_target_pairs={{0,2},{1,3},{2,0},{3,1},{4,6},{5,7},{6,4},{7,5},{8,10},{9,11},{10,... | collective-permute-start | bytes 442376 | tf_op jit(solution)/shard_map/ppermute | solution.py:323
  38.1 13.0 %collective-permute-start.22 = (bf16[64,1152]{1,0:T(8,128)(2,1)S(1)}, bf16[64,1152]{1,0:T(8,128)(2,1)S(1)}, u32[]{:S(2)}, u32[]{:S(2)}) collective-permute-start(bf16[64,1152]{1,0:T(8,128)(2,1)S(1)} %attention.1.refs_1_), channel_id=1, source_target_pairs={{0,1},{1,0},{2,3},{3,2},{4,5},{5,4},{6,7},{7,6},{8,9},{9,8},{10,11... | collective-permute-start | bytes 442376 | tf_op jit(solution)/shard_map/ppermute | solution.py:323
  40.7 10.9 %collective-permute-start.19 = (bf16[64,1152]{1,0:T(8,128)(2,1)S(1)}, bf16[64,1152]{1,0:T(8,128)(2,1)S(1)}, u32[]{:S(2)}, u32[]{:S(2)}) collective-permute-start(bf16[64,1152]{1,0:T(8,128)(2,1)S(1)} %collective-permute-done.15.refs_2_), channel_id=1, source_target_pairs={{0,2},{1,3},{2,0},{3,1},{4,6},{5,7},{6,4},{7,5},{8,10},{9,11},{10,... | collective-permute-start | bytes 442376 | tf_op jit(solution)/shard_map/ppermute | solution.py:323
  49.1 6.7 %collective-permute-start.20 = (bf16[64,1152]{1,0:T(8,128)(2,1)S(1)}, bf16[64,1152]{1,0:T(8,128)(2,1)S(1)}, u32[]{:S(2)}, u32[]{:S(2)}) collective-permute-start(bf16[64,1152]{1,0:T(8,128)(2,1)S(1)} %collective-permute-done.16.refs_3_), channel_id=1, source_target_pairs={{0,2},{1,3},{2,0},{3,1},{4,6},{5,7},{6,4},{7,5},{8,10},{9,11},{10,... | collective-permute-start | bytes 442376 | tf_op jit(solution)/shard_map/ppermute | solution.py:323
  49.1 9.0 %collective-permute-start.21 = (bf16[64,1152]{1,0:T(8,128)(2,1)S(1)}, bf16[64,1152]{1,0:T(8,128)(2,1)S(1)}, u32[]{:S(2)}, u32[]{:S(2)}) collective-permute-start(bf16[64,1152]{1,0:T(8,128)(2,1)S(1)} %collective-permute-done.17.refs_4_), channel_id=1, source_target_pairs={{0,2},{1,3},{2,0},{3,1},{4,6},{5,7},{6,4},{7,5},{8,10},{9,11},{10,... | collective-permute-start | bytes 442376 | tf_op jit(solution)/shard_map/ppermute | solution.py:323
  51.1 7.0 %collective-permute-start.23 = (bf16[64,1152]{1,0:T(8,128)(2,1)S(1)}, bf16[64,1152]{1,0:T(8,128)(2,1)S(1)}, u32[]{:S(2)}, u32[]{:S(2)}) collective-permute-start(bf16[64,1152]{1,0:T(8,128)(2,1)S(1)} %collective-permute-done.15.refs_2_), channel_id=1, source_target_pairs={{0,1},{1,0},{2,3},{3,2},{4,5},{5,4},{6,7},{7,6},{8,9},{9,8},{10,11... | collective-permute-start | bytes 442376 | tf_op jit(solution)/shard_map/ppermute | solution.py:323
  51.1 7.5 %collective-permute-start.24 = (bf16[64,1152]{1,0:T(8,128)(2,1)S(1)}, bf16[64,1152]{1,0:T(8,128)(2,1)S(1)}, u32[]{:S(2)}, u32[]{:S(2)}) collective-permute-start(bf16[64,1152]{1,0:T(8,128)(2,1)S(1)} %collective-permute-done.16.refs_3_), channel_id=1, source_target_pairs={{0,1},{1,0},{2,3},{3,2},{4,5},{5,4},{6,7},{7,6},{8,9},{9,8},{10,11... | collective-permute-start | bytes 442376 | tf_op jit(solution)/shard_map/ppermute | solution.py:323
  51.6 7.3 %collective-permute-start.25 = (bf16[64,1152]{1,0:T(8,128)(2,1)S(1)}, bf16[64,1152]{1,0:T(8,128)(2,1)S(1)}, u32[]{:S(2)}, u32[]{:S(2)}) collective-permute-start(bf16[64,1152]{1,0:T(8,128)(2,1)S(1)} %collective-permute-done.17.refs_4_), channel_id=1, source_target_pairs={{0,1},{1,0},{2,3},{3,2},{4,5},{5,4},{6,7},{7,6},{8,9},{9,8},{10,11... | collective-permute-start | bytes 442376 | tf_op jit(solution)/shard_map/ppermute | solution.py:323
  55.8 3.1 %collective-permute-start.26 = (bf16[64,1152]{1,0:T(8,128)(2,1)S(1)}, bf16[64,1152]{1,0:T(8,128)(2,1)S(1)}, u32[]{:S(2)}, u32[]{:S(2)}) collective-permute-start(bf16[64,1152]{1,0:T(8,128)(2,1)S(1)} %collective-permute-done.18.refs_5_), channel_id=1, source_target_pairs={{0,1},{1,0},{2,3},{3,2},{4,5},{5,4},{6,7},{7,6},{8,9},{9,8},{10,11... | collective-permute-start | bytes 442376 | tf_op jit(solution)/shard_map/ppermute | solution.py:323
  58.1 1.4 %collective-permute-start.27 = (bf16[64,1152]{1,0:T(8,128)(2,1)S(1)}, bf16[64,1152]{1,0:T(8,128)(2,1)S(1)}, u32[]{:S(2)}, u32[]{:S(2)}) collective-permute-start(bf16[64,1152]{1,0:T(8,128)(2,1)S(1)} %collective-permute-done.19.refs_6_), channel_id=1, source_target_pairs={{0,1},{1,0},{2,3},{3,2},{4,5},{5,4},{6,7},{7,6},{8,9},{9,8},{10,11... | collective-permute-start | bytes 442376 | tf_op jit(solution)/shard_map/ppermute | solution.py:323
  58.1 1.6 %collective-permute-start.28 = (bf16[64,1152]{1,0:T(8,128)(2,1)S(1)}, bf16[64,1152]{1,0:T(8,128)(2,1)S(1)}, u32[]{:S(2)}, u32[]{:S(2)}) collective-permute-start(bf16[64,1152]{1,0:T(8,128)(2,1)S(1)} %collective-permute-done.20.refs_7_), channel_id=1, source_target_pairs={{0,1},{1,0},{2,3},{3,2},{4,5},{5,4},{6,7},{7,6},{8,9},{9,8},{10,11... | collective-permute-start | bytes 442376 | tf_op jit(solution)/shard_map/ppermute | solution.py:323
  58.6 1.4 %collective-permute-start.29 = (bf16[64,1152]{1,0:T(8,128)(2,1)S(1)}, bf16[64,1152]{1,0:T(8,128)(2,1)S(1)}, u32[]{:S(2)}, u32[]{:S(2)}) collective-permute-start(bf16[64,1152]{1,0:T(8,128)(2,1)S(1)} %collective-permute-done.21.refs_8_), channel_id=1, source_target_pairs={{0,1},{1,0},{2,3},{3,2},{4,5},{5,4},{6,7},{7,6},{8,9},{9,8},{10,11... | collective-permute-start | bytes 442376 | tf_op jit(solution)/shard_map/ppermute | solution.py:323
  63.5 10.3 %collective-permute-start.36 = (bf16[128,512]{1,0:T(8,128)(2,1)S(1)}, bf16[128,512]{1,0:T(8,128)(2,1)S(1)}, u32[]{:S(2)}, u32[]{:S(2)}) collective-permute-start(bf16[128,512]{1,0:T(8,128)(2,1)S(1)} %projection.1.refs_0_), channel_id=1, source_target_pairs={{0,8},{1,9},{2,10},{3,11},{4,12},{5,13},{6,14},{7,15},{8,0},{9,1},... | collective-permute-start | bytes 393224 | tf_op jit(solution)/shard_map/ppermute | solution.py:323
  63.7 10.4 %collective-permute-start.30 = (bf16[128,512]{1,0:T(8,128)(2,1)S(1)}, bf16[128,512]{1,0:T(8,128)(2,1)S(1)}, u32[]{:S(2)}, u32[]{:S(2)}) collective-permute-start(bf16[128,512]{1,0:T(8,128)(2,1)S(1)} %projection.1.refs_0_), channel_id=1, source_target_pairs={{0,4},{1,5},{2,6},{3,7},{4,0},{5,1},{6,2},{7,3},{8,12},{9,13},{10,... | collective-permute-start | bytes 393224 | tf_op jit(solution)/shard_map/ppermute | solution.py:323
  64.3 11.6 %collective-permute-start.32 = (bf16[128,512]{1,0:T(8,128)(2,1)S(1)}, bf16[128,512]{1,0:T(8,128)(2,1)S(1)}, u32[]{:S(2)}, u32[]{:S(2)}) collective-permute-start(bf16[128,512]{1,0:T(8,128)(2,1)S(1)} %projection.1.refs_0_), channel_id=1, source_target_pairs={{0,12},{1,13},{2,14},{3,15},{4,8},{5,9},{6,10},{7,11},{8,4},{9,5},... | collective-permute-start | bytes 393224 | tf_op jit(solution)/shard_map/ppermute | solution.py:323
  68.0 7.9 %collective-permute-start.37 = (bf16[128,512]{1,0:T(8,128)(2,1)S(1)}, bf16[128,512]{1,0:T(8,128)(2,1)S(1)}, u32[]{:S(2)}, u32[]{:S(2)}) collective-permute-start(bf16[128,512]{1,0:T(8,128)(2,1)S(1)} %projection.1.refs_0_), channel_id=1, source_target_pairs={{0,2},{1,3},{2,0},{3,1},{4,6},{5,7},{6,4},{7,5},{8,10},{9,11},{10,... | collective-permute-start | bytes 393224 | tf_op jit(solution)/shard_map/ppermute | solution.py:323
  68.3 8.1 %collective-permute-start.39 = (bf16[128,512]{1,0:T(8,128)(2,1)S(1)}, bf16[128,512]{1,0:T(8,128)(2,1)S(1)}, u32[]{:S(2)}, u32[]{:S(2)}) collective-permute-start(bf16[128,512]{1,0:T(8,128)(2,1)S(1)} %projection.1.refs_0_), channel_id=1, source_target_pairs={{0,1},{1,0},{2,3},{3,2},{4,5},{5,4},{6,7},{7,6},{8,9},{9,8},{10,11... | collective-permute-start | bytes 393224 | tf_op jit(solution)/shard_map/ppermute | solution.py:323
  73.8 5.2 %collective-permute-start.38 = (bf16[128,512]{1,0:T(8,128)(2,1)S(1)}, bf16[128,512]{1,0:T(8,128)(2,1)S(1)}, u32[]{:S(2)}, u32[]{:S(2)}) collective-permute-start(bf16[128,512]{1,0:T(8,128)(2,1)S(1)} %collective-permute-done.36.refs_2_), channel_id=1, source_target_pairs={{0,2},{1,3},{2,0},{3,1},{4,6},{5,7},{6,4},{7,5},{8,10},{9,11},{10,... | collective-permute-start | bytes 393224 | tf_op jit(solution)/shard_map/ppermute | solution.py:323
  74.1 5.2 %collective-permute-start.40 = (bf16[128,512]{1,0:T(8,128)(2,1)S(1)}, bf16[128,512]{1,0:T(8,128)(2,1)S(1)}, u32[]{:S(2)}, u32[]{:S(2)}) collective-permute-start(bf16[128,512]{1,0:T(8,128)(2,1)S(1)} %collective-permute-done.30.refs_1_), channel_id=1, source_target_pairs={{0,1},{1,0},{2,3},{3,2},{4,5},{5,4},{6,7},{7,6},{8,9},{9,8},{10,11... | collective-permute-start | bytes 393224 | tf_op jit(solution)/shard_map/ppermute | solution.py:323
  75.9 3.4 %collective-permute-start.41 = (bf16[128,512]{1,0:T(8,128)(2,1)S(1)}, bf16[128,512]{1,0:T(8,128)(2,1)S(1)}, u32[]{:S(2)}, u32[]{:S(2)}) collective-permute-start(bf16[128,512]{1,0:T(8,128)(2,1)S(1)} %collective-permute-done.36.refs_2_), channel_id=1, source_target_pairs={{0,1},{1,0},{2,3},{3,2},{4,5},{5,4},{6,7},{7,6},{8,9},{9,8},{10,11... | collective-permute-start | bytes 393224 | tf_op jit(solution)/shard_map/ppermute | solution.py:323
  75.9 6.4 %collective-permute-start.31 = (bf16[128,512]{1,0:T(8,128)(2,1)S(1)}, bf16[128,512]{1,0:T(8,128)(2,1)S(1)}, u32[]{:S(2)}, u32[]{:S(2)}) collective-permute-start(bf16[128,512]{1,0:T(8,128)(2,1)S(1)} %collective-permute-done.30.refs_1_), channel_id=1, source_target_pairs={{0,2},{1,3},{2,0},{3,1},{4,6},{5,7},{6,4},{7,5},{8,10},{9,11},{10,... | collective-permute-start | bytes 393224 | tf_op jit(solution)/shard_map/ppermute | solution.py:323
  76.4 8.3 %collective-permute-start.42 = (bf16[128,512]{1,0:T(8,128)(2,1)S(1)}, bf16[128,512]{1,0:T(8,128)(2,1)S(1)}, u32[]{:S(2)}, u32[]{:S(2)}) collective-permute-start(bf16[128,512]{1,0:T(8,128)(2,1)S(1)} %collective-permute-done.32.refs_3_), channel_id=1, source_target_pairs={{0,1},{1,0},{2,3},{3,2},{4,5},{5,4},{6,7},{7,6},{8,9},{9,8},{10,11... | collective-permute-start | bytes 393224 | tf_op jit(solution)/shard_map/ppermute | solution.py:323
  79.0 5.7 %collective-permute-start.33 = (bf16[128,512]{1,0:T(8,128)(2,1)S(1)}, bf16[128,512]{1,0:T(8,128)(2,1)S(1)}, u32[]{:S(2)}, u32[]{:S(2)}) collective-permute-start(bf16[128,512]{1,0:T(8,128)(2,1)S(1)} %collective-permute-done.32.refs_3_), channel_id=1, source_target_pairs={{0,2},{1,3},{2,0},{3,1},{4,6},{5,7},{6,4},{7,5},{8,10},{9,11},{10,... | collective-permute-start | bytes 393224 | tf_op jit(solution)/shard_map/ppermute | solution.py:323
  79.2 5.4 %collective-permute-start.43 = (bf16[128,512]{1,0:T(8,128)(2,1)S(1)}, bf16[128,512]{1,0:T(8,128)(2,1)S(1)}, u32[]{:S(2)}, u32[]{:S(2)}) collective-permute-start(bf16[128,512]{1,0:T(8,128)(2,1)S(1)} %collective-permute-done.37.refs_4_), channel_id=1, source_target_pairs={{0,1},{1,0},{2,3},{3,2},{4,5},{5,4},{6,7},{7,6},{8,9},{9,8},{10,11... | collective-permute-start | bytes 393224 | tf_op jit(solution)/shard_map/ppermute | solution.py:323
  79.2 5.4 %collective-permute-start.44 = (bf16[128,512]{1,0:T(8,128)(2,1)S(1)}, bf16[128,512]{1,0:T(8,128)(2,1)S(1)}, u32[]{:S(2)}, u32[]{:S(2)}) collective-permute-start(bf16[128,512]{1,0:T(8,128)(2,1)S(1)} %collective-permute-done.38.refs_5_), channel_id=1, source_target_pairs={{0,1},{1,0},{2,3},{3,2},{4,5},{5,4},{6,7},{7,6},{8,9},{9,8},{10,11... | collective-permute-start | bytes 393224 | tf_op jit(solution)/shard_map/ppermute | solution.py:323
  82.3 6.6 %collective-permute-start.34 = (bf16[128,512]{1,0:T(8,128)(2,1)S(1)}, bf16[128,512]{1,0:T(8,128)(2,1)S(1)}, u32[]{:S(2)}, u32[]{:S(2)}) collective-permute-start(bf16[128,512]{1,0:T(8,128)(2,1)S(1)} %collective-permute-done.31.refs_0_), channel_id=1, source_target_pairs={{0,1},{1,0},{2,3},{3,2},{4,5},{5,4},{6,7},{7,6},{8,9},{9,8},{10,11... | collective-permute-start | bytes 393224 | tf_op jit(solution)/shard_map/ppermute | solution.py:323
  84.6 4.2 %collective-permute-start.35 = (bf16[128,512]{1,0:T(8,128)(2,1)S(1)}, bf16[128,512]{1,0:T(8,128)(2,1)S(1)}, u32[]{:S(2)}, u32[]{:S(2)}) collective-permute-start(bf16[128,512]{1,0:T(8,128)(2,1)S(1)} %collective-permute-done.33.refs_1_), channel_id=1, source_target_pairs={{0,1},{1,0},{2,3},{3,2},{4,5},{5,4},{6,7},{7,6},{8,9},{9,8},{10,11... | collective-permute-start | bytes 393224 | tf_op jit(solution)/shard_map/ppermute | solution.py:323

commit v2 on v1

--- a/solution.py
+++ b/solution.py
@@ -24,32 +24,44 @@
     scale = log2e / math.sqrt(head_size)
     width = group * head_size
 
-    def fold(scores, valid, block_values):
+    every = group * rows
+    some = min(256, group * rows)
+
+    def fold(part, scores, valid, block_values):
         if valid is not None:
             scores = jnp.where(valid, scores, very_low)
-        peak = top[...]
+        peak = top[part, :]
         newest = jnp.maximum(peak, jnp.max(scores, axis=1, keepdims=True))
         factor = jnp.exp2(peak - newest)
-        part, weights = None, []
+        sums, weights = None, []
         for at in range(0, scores.shape[1], lanes):
             tile = jnp.exp2(scores[:, at : at + lanes] - newest)
             if valid is not None:
                 tile = jnp.where(valid[:, at : at + lanes], tile, 0.0)
-            part = tile if part is None else part + tile
+            sums = tile if sums is None else sums + tile
             weights.append(tile.astype(jnp.bfloat16))
-        total[...] = total[...] * factor + part
-        acc[...] = acc[...] * factor + jnp.dot(
+        total[part, :] = total[part, :] * factor + sums
+        acc[part, :] = acc[part, :] * factor + jnp.dot(
             jnp.concatenate(weights, axis=1), block_values, preferred_element_type=jnp.float32
         )
-        top[...] = newest
-
-    def score(block_keys):
+        top[part, :] = newest
+
+    def score(part, block_keys):
         return (
             lax.dot_general(
-                q[...], block_keys, (((1,), (1,)), ((), ())), preferred_element_type=jnp.float32
+                q[part, :], block_keys, (((1,), (1,)), ((), ())), preferred_element_type=jnp.float32
             )
             * scale
         )
+
+    def sweep(block_keys, block_values, valid_of):
+        parts = [slice(at, at + some) for at in range(0, every, some)]
+        ready = score(parts[0], block_keys)
+        for number, part in enumerate(parts):
+            scores = ready
+            if number + 1 < len(parts):
+                ready = score(parts[number + 1], block_keys)
+            fold(part, scores, valid_of(part), block_values)
 
     @pl.when(step == 0)
     def _():
@@ -81,17 +93,17 @@
         top[...] = jnp.full_like(top, very_low)
         total[...] = jnp.zeros_like(total)
         acc[...] = jnp.zeros_like(acc)
-        fold(score(own_keys), valid, own_values)
+        sweep(own_keys, own_values, lambda part: valid[part, :])
 
     @pl.when((step + 1) * block <= length)
     def _():
-        fold(score(keys[...]), None, values[...])
+        sweep(keys[...], values[...], lambda part: None)
 
     @pl.when((step * block < length) & ((step + 1) * block > length))
     def _():
         at = step * block + lax.broadcasted_iota(jnp.int32, (1, block), 1)
-        valid = jnp.broadcast_to(at < length, (q.shape[0], block))
-        fold(score(keys[...]), valid, values[...])
+        valid = jnp.broadcast_to(at < length, (some, block))
+        sweep(keys[...], values[...], lambda part: valid)
 
     @pl.when(step == pl.num_programs(0) - 1)
     def _():
@@ -146,9 +158,9 @@
         ),
         compiler_params=pltpu.CompilerParams(vmem_limit_bytes=16 << 20),
         cost_estimate=pl.CostEstimate(
-            flops=16 * 4 * group * rows * capacity * head_size,
+            flops=4 * group * rows * capacity * head_size,
             bytes_accessed=4 * capacity * head_size,
-            transcendentals=16 * group * rows * capacity,
+            transcendentals=group * rows * capacity,
         ),
         name="attention",
     )(info, order, *blocks, mask, keys, values)
@@ -164,6 +176,7 @@
     width = group * head_size
     for piece in range(pieces):
         held[piece] = blocks[piece][...]
+    result = None
     for head in range(key_heads):
         for sequence in range(sequences):
             pair = sequence * key_heads + head
@@ -182,17 +195,19 @@
             mixing = [part / whole for part in mixing]
             for member in range(group):
                 columns = slice(member * head_size, (member + 1) * head_size)
-                gathered = None
-                for slot, part in zip(slots, mixing):
-                    term = part[:, member : member + 1] * held[slot, :, columns].astype(jnp.float32)
-                    gathered = term if gathered is None else gathered + term
+                gathered = held[slots[-1], :, columns].astype(jnp.float32)
+                base = gathered
+                for slot, part in zip(slots[:-1], mixing):
+                    change = held[slot, :, columns].astype(jnp.float32) - base
+                    gathered = gathered + part[:, member : member + 1] * change
                 attended[
                     sequence * rows : (sequence + 1) * rows,
                     head * width + member * head_size : head * width + (member + 1) * head_size,
                 ] = gathered.astype(jnp.bfloat16)
-    out[...] = jnp.dot(
-        attended[...], weight[...], preferred_element_type=jnp.float32
-    ).astype(jnp.bfloat16)
+        part = slice(head * width, (head + 1) * width)
+        term = jnp.dot(attended[:, part], weight[part, :], preferred_element_type=jnp.float32)
+        result = term if result is None else result + term
+    out[...] = result.astype(jnp.bfloat16)
 
 
 def projection(where_from, blocks, weight, per_pair, key_heads, sequences, group, head_size):
@@ -220,102 +235,98 @@
     )(where_from, *blocks, weight)
 
 
-def multiply(order, slots, blocks, gain, weights, totals, squares, fresh):
-    for slot, block in zip(slots, blocks):
-        depth = block.shape[1]
+def feed_kernel(slots, total_width, first, last, order, *refs):
+    blocks, refs = refs[: len(slots)], refs[len(slots) :]
+    (gain, *weights), refs = refs[:3], refs[3:]
+    if not first:
+        given, refs = refs[:3], refs[3:]
+    if last:
+        out, totals = refs[0], refs[1:]
+    else:
+        totals, kept = refs[:2], refs[2]
+    rows, depth = blocks[0].shape
+    squares = jnp.zeros((rows, lanes), jnp.float32) if first else given[2][...]
+    for number, (slot, block) in enumerate(zip(slots, blocks)):
         branch = block[...].astype(jnp.float32)
         square = branch * branch
         for at in range(0, depth, lanes):
             squares = squares + square[:, at : at + lanes]
         scaled = (branch * gain[order[slot]]).astype(jnp.bfloat16)
         part = pl.ds(pl.multiple_of(order[slot] * depth, depth), depth)
-        for weight, total in zip(weights, totals):
-            term = jnp.dot(scaled, weight[part, :], preferred_element_type=jnp.float32)
-            total[...] = term if fresh else total[...] + term
-        fresh = False
-    return squares
-
-
-def feed_first_kernel(slots, order, *refs):
-    blocks = refs[: len(slots)]
-    gain, gate_weight, up_weight, gate, up, squares = refs[len(slots) :]
-    squares[...] = multiply(
-        order,
-        slots,
-        blocks,
-        gain,
-        (gate_weight, up_weight),
-        (gate, up),
-        jnp.zeros(squares.shape, jnp.float32),
-        True,
-    )
-
-
-def feed_last_kernel(slots, total_width, order, *refs):
-    blocks = refs[: len(slots)]
-    gain, gate_weight, up_weight, gate_in, up_in, squares, out, gate, up = refs[len(slots) :]
-    gate[...] = gate_in[...]
-    up[...] = up_in[...]
-    total = multiply(
-        order,
-        slots,
-        blocks,
-        gain,
-        (gate_weight, up_weight),
-        (gate, up),
-        squares[...],
-        False,
-    )
-    inverse = lax.rsqrt(jnp.sum(total, axis=1, keepdims=True) / total_width + epsilon)
-    opened = gate[...] * inverse
-    out[...] = (opened / (1.0 + jnp.exp(-opened)) * (up[...] * inverse)).astype(jnp.bfloat16)
-
-
-def feed(order, blocks, gain, gate_weight, up_weight):
+        for which in range(2):
+            term = jnp.dot(scaled, weights[which][part, :], preferred_element_type=jnp.float32)
+            if number > 0:
+                term = totals[which][...] + term
+            elif not first:
+                term = given[which][...] + term
+            totals[which][...] = term
+    if not last:
+        kept[...] = squares
+        return
+    inverse = lax.rsqrt(jnp.sum(squares, axis=1, keepdims=True) / total_width + epsilon)
+    opened = totals[0][...] * inverse
+    out[...] = (opened / (1.0 + jnp.exp(-opened)) * (totals[1][...] * inverse)).astype(jnp.bfloat16)
+
+
+def feed(order, blocks, gain, gate_weight, up_weight, mark):
     pieces = len(blocks)
     rows, depth = blocks[0].shape
     width = gate_weight.shape[1]
     far = pieces // 4
     late = [far + number for number in range(1, far, 2)]
     late = late + [2 * far + number for number in late]
-    early = [slot for slot in range(pieces) if slot not in late]
+    stages = [[0, 2 * far], [2, 2 * far + 2, far, 3 * far]]
+    known = late + stages[0] + stages[1]
+    stages = stages + [[slot for slot in range(pieces) if slot not in known], late]
     whole = pl.BlockSpec(memory_space=pltpu.VMEM)
     table = gain.reshape(pieces, 1, depth)
-
-    def call(kernel, slots, extra, out_shape, scratch):
-        return pl.pallas_call(
-            kernel,
-            out_shape=out_shape,
+    result = ()
+    for number, slots in enumerate(stages):
+        first, last = number == 0, number == len(stages) - 1
+        sums = [jax.ShapeDtypeStruct((rows, width), jnp.float32)] * 2
+        sums = sums + [jax.ShapeDtypeStruct((rows, lanes), jnp.float32)]
+        shape = jax.ShapeDtypeStruct((rows, width), jnp.bfloat16) if last else tuple(sums)
+        kernel = functools.partial(feed_kernel, slots, pieces * depth, first, last)
+        result = pl.pallas_call(
+            kernel if not last else lambda *refs: kernel(*refs[:-4], *refs[-3:]),
+            out_shape=shape,
             in_specs=[pl.BlockSpec(memory_space=pltpu.SMEM)]
-            + [whole] * (len(slots) + 3 + len(extra)),
-            out_specs=jax.tree.map(lambda _: whole, out_shape),
-            scratch_shapes=scratch,
-            compiler_params=pltpu.CompilerParams(vmem_limit_bytes=16 << 20),
+            + [whole] * (len(slots) + 3 + len(result) + last),
+            out_specs=whole if last else (whole,) * 3,
+            scratch_shapes=[pltpu.VMEM((rows, width), jnp.float32)] * 2 if last else [],
+            compiler_params=pltpu.CompilerParams(vmem_limit_bytes=12 << 20),
             cost_estimate=pl.CostEstimate(
                 flops=4 * rows * len(slots) * depth * width,
                 bytes_accessed=2 * rows * len(slots) * depth,
                 transcendentals=0,
             ),
-        )(order, *[blocks[slot] for slot in slots], table, gate_weight, up_weight, *extra)
-
-    sums = call(
-        functools.partial(feed_first_kernel, early),
-        early,
-        (),
-        (
-            jax.ShapeDtypeStruct((rows, width), jnp.float32),
-            jax.ShapeDtypeStruct((rows, width), jnp.float32),
-            jax.ShapeDtypeStruct((rows, lanes), jnp.float32),
-        ),
-        (),
-    )
-    return call(
-        functools.partial(feed_last_kernel, late, pieces * depth),
-        late,
-        sums,
-        jax.ShapeDtypeStruct((rows, width), jnp.bfloat16),
-        [pltpu.VMEM((rows, width), jnp.float32)] * 2,
-    )
+        )(
+            order,
+            *[blocks[slot] for slot in slots],
+            table,
+            gate_weight,
+            up_weight,
+            *result,
+            *((mark,) if last else ()),
+        )
+    return result
+
+
+def mark_kernel(block, out):
+    out[...] = block[: out.shape[0], : out.shape[1]]
+
+
+def marked(block, work):
+    whole = pl.BlockSpec(memory_space=pltpu.VMEM)
+    return pl.pallas_call(
+        mark_kernel,
+        out_shape=jax.ShapeDtypeStruct((8, lanes), block.dtype),
+        in_specs=[whole],
+        out_specs=whole,
+        compiler_params=pltpu.CompilerParams(vmem_limit_bytes=1 << 20),
+        cost_estimate=pl.CostEstimate(flops=work, bytes_accessed=0, transcendentals=work // 512),
+        name="mark",
+    )(block)
 
 
 def spread(block, devices):
@@ -389,6 +400,8 @@
         pltpu.with_memory_space_constraint(cache_values, pltpu.HBM),
         group,
     )
+    work = 64 * 2 * queries.shape[1] * cache_keys.size // 8
+    mark = marked(block, work)
     projected = projection(
         slot_of,
         spread(block, devices),
@@ -399,13 +412,7 @@
         group,
         head_size,
     )
-    hidden = feed(
-        order,
-        spread(projected, devices),
-        norm_gain,
-        gate_weight,
-        up_weight,
-    )
+    hidden = feed(order, spread(projected, devices), norm_gain, gate_weight, up_weight, mark)
     return (projected, hidden)
 
 

time: 92.4 us -> 89 us (0.963)
  waiting for transfers between devices: 36.4 us -> 33.2 us
  starting transfers between devices: 33.1 us -> 34.7 us
  Pallas kernels: 17.7 us -> 16.5 us
    ppermute x45, waiting for transfers between devices: 36.4 us -> 33.2 us  [swap(): return lax.ppermute(value, 'wide', [(i, i ^ bits) for i in range(devices)])]
    pallas_call x1, Pallas kernels: 7.51 us -> 5.77 us  [attention(): pl.pallas_call(functools.partial(attention_kernel, pieces, sequences, row...]
    ppermute x45, starting transfers between devices: 33.1 us -> 34.7 us  [swap(): return lax.ppermute(value, 'wide', [(i, i ^ bits) for i in range(devices)])]
    pallas_call x2 -> x5, Pallas kernels: 6.65 us -> 8.08 us  [the longest x4 8.08 us: feed(): pl.pallas_call(kernel if not last else lambda *refs: kernel(*refs[:-4], *...]
    pallas_call x1, Pallas kernels: 3.56 us -> 2.64 us  [projection(): pl.pallas_call(functools.partial(projection_kernel, pieces, per_pair, key...]
  transfers between devices with their start and end apart: 45 -> 45, of which waited for: 18 -> 17; matrix products, arithmetic and copies ran while one was open for 3% -> 3% of each run, Pallas kernels for 4% -> 6%
where the time goes in v2:
time: 89 us; the launch traced here: 88.7 us
  starting transfers between devices  34.7 us (39%)
  waiting for transfers between devices  33.2 us (37%)
  Pallas kernels  16.5 us (19%)
  other arithmetic  2.7 us (3%)
  between operations  0.92 us (1%)
    ppermute x45, starting transfers between devices, swap(): return lax.ppermute(value, 'wide', [(i, i ^ bits) for i in range(devices)])  34.7 us
    ppermute x45, waiting for transfers between devices, swap(): return lax.ppermute(value, 'wide', [(i, i ^ bits) for i in range(devices)])  33.2 us
    pallas_call x4, Pallas kernels, feed(): pl.pallas_call(kernel if not last else lambda *refs: kernel(*refs[:-4], *...  8.08 us
    pallas_call x1, Pallas kernels, attention(): pl.pallas_call(functools.partial(attention_kernel, pieces, sequences, row...  5.77 us
    pallas_call x1, Pallas kernels, projection(): pl.pallas_call(functools.partial(projection_kernel, pieces, per_pair, key...  2.64 us
  transfers between devices with their start and end apart: 45, of which 17 were waited for; matrix products, arithmetic and copies ran while one was open for 3% of the time, Pallas kernels for 6%

profile of v2, /device:TPU:0, one launch (start us, length us, event | category | flops | bytes accessed | tf_op | source)
XLA Modules:
  0.0 88.7 jit_solution(4623291588829327403)
XLA Ops:
  0.6 0.0 copy-start.2
  0.6 0.9 pad_maximum_fusion
  1.5 3.1 %collective-permute-start = (bf16[8,5120]{1,0:T(8,128)(2,1)S(1)}, bf16[8,5120]{1,0:T(8,128)(2,1)S(1)}, u32[]{:S(2)}, u32[]{:S(2)}) collective-permute-start(bf16[8,5120]{1,0:T(8,128)(2,1)S(1)} %bitcast.14), channel_id=1, source_target_pairs={{0,4},{1,5},{2,6},{3,7},{4,0},{5,1},{6,2},{7,3},{8,12},{9,13},{10,... | collective-permute-start | bytes 245768 | tf_op jit(solution)/shard_map/ppermute | solution.py:334
  4.6 2.6 %collective-permute-start.1 = (bf16[8,5120]{1,0:T(8,128)(2,1)S(1)}, bf16[8,5120]{1,0:T(8,128)(2,1)S(1)}, u32[]{:S(2)}, u32[]{:S(2)}) collective-permute-start(bf16[8,5120]{1,0:T(8,128)(2,1)S(1)} %bitcast.15), channel_id=1, source_target_pairs={{0,8},{1,9},{2,10},{3,11},{4,12},{5,13},{6,14},{7,15},{8,0},{9,1},... | collective-permute-start | bytes 245768 | tf_op jit(solution)/shard_map/ppermute | solution.py:334
  7.2 0.0 collective-permute-start.2
  7.2 1.7 %collective-permute-start.3 = (bf16[8,5120]{1,0:T(8,128)(2,1)S(1)}, bf16[8,5120]{1,0:T(8,128)(2,1)S(1)}, u32[]{:S(2)}, u32[]{:S(2)}) collective-permute-start(bf16[8,5120]{1,0:T(8,128)(2,1)S(1)} %bitcast.17), channel_id=1, source_target_pairs={{0,2},{1,3},{2,0},{3,1},{4,6},{5,7},{6,4},{7,5},{8,10},{9,11},{10,... | collective-permute-start | bytes 245768 | tf_op jit(solution)/shard_map/ppermute | solution.py:334
  8.9 0.0 collective-permute-start.7
  9.0 0.0 copy-start
  9.0 0.8 broadcast_compare_fusion
  9.8 3.7 %collective-permute-done.2.refs_3_ = bf16[8,5120]{1,0:T(8,128)(2,1)S(1)} collective-permute-done((bf16[8,5120]{1,0:T(8,128)(2,1)S(1)}, bf16[8,5120]{1,0:T(8,128)(2,1)S(1)}, u32[]{:S(2)}, u32[]{:S(2)}) %collective-permute-start.2) | collective-permute-done | bytes 81952 | tf_op jit(solution)/shard_map/ppermute | solution.py:334
  13.5 1.5 %collective-permute-start.6 = (bf16[8,5120]{1,0:T(8,128)(2,1)S(1)}, bf16[8,5120]{1,0:T(8,128)(2,1)S(1)}, u32[]{:S(2)}, u32[]{:S(2)}) collective-permute-start(bf16[8,5120]{1,0:T(8,128)(2,1)S(1)} %collective-permute-done.2.refs_3_), channel_id=1, source_target_pairs={{0,2},{1,3},{2,0},{3,1},{4,6},{5,7},{6,4},{7,5},{8,10},{9,11},{10,... | collective-permute-start | bytes 245768 | tf_op jit(solution)/shard_map/ppermute | solution.py:334
  15.1 0.6 collective-permute-start.4
  15.6 0.2 collective-permute-start.8
  15.8 1.5 %collective-permute-start.5 = (bf16[8,5120]{1,0:T(8,128)(2,1)S(1)}, bf16[8,5120]{1,0:T(8,128)(2,1)S(1)}, u32[]{:S(2)}, u32[]{:S(2)}) collective-permute-start(bf16[8,5120]{1,0:T(8,128)(2,1)S(1)} %collective-permute-done.1.refs_2_), channel_id=1, source_target_pairs={{0,2},{1,3},{2,0},{3,1},{4,6},{5,7},{6,4},{7,5},{8,10},{9,11},{10,... | collective-permute-start | bytes 245768 | tf_op jit(solution)/shard_map/ppermute | solution.py:334
  17.3 0.8 fusion.info
  18.1 2.3 %collective-permute-done.4.refs_5_ = bf16[8,5120]{1,0:T(8,128)(2,1)S(1)} collective-permute-done((bf16[8,5120]{1,0:T(8,128)(2,1)S(1)}, bf16[8,5120]{1,0:T(8,128)(2,1)S(1)}, u32[]{:S(2)}, u32[]{:S(2)}) %collective-permute-start.4) | collective-permute-done | bytes 81952 | tf_op jit(solution)/shard_map/ppermute | solution.py:334
  20.4 1.2 %collective-permute-done.5.refs_6_ = bf16[8,5120]{1,0:T(8,128)(2,1)S(1)} collective-permute-done((bf16[8,5120]{1,0:T(8,128)(2,1)S(1)}, bf16[8,5120]{1,0:T(8,128)(2,1)S(1)}, u32[]{:S(2)}, u32[]{:S(2)}) %collective-permute-start.5) | collective-permute-done | bytes 81952 | tf_op jit(solution)/shard_map/ppermute | solution.py:334
  21.7 0.5 collective-permute-start.12
  22.2 0.1 collective-permute-start.13
  22.3 0.4 collective-permute-start.14
  22.7 0.2 collective-permute-done.11.refs_12_
  23.0 0.2 collective-permute-done.12.refs_13_
  23.1 0.4 collective-permute-done.13.refs_14_
  23.5 0.2 collective-permute-done.14.refs_15_
  23.6 5.8 %attention.1.refs_1_.block = bf16[64,1152]{1,0:T(8,128)(2,1)S(1)} custom-call(s32[4]{0:T(128)S(1)} %fusion.info, s32[16]{0:T(128)S(1)} %fusion.5.order.refs_0_, bf16[8,5120]{1,0:T(8,128)(2,1)S(1)} %bitcast.19, bf16[8,5120]{1,0:T(8,128)(2,1)S(1)} %collective-permute-done.refs_1_, bf16[8,5120]{1,0:T(8,128)(2,1)S(1)} %collective-permute-done.1.refs_2_, ...), custom_call_target="tpu_custom_call" | custom-call | flops 2147483648 | bytes 4194304 | tf_op jit(solution)/shard_map/attention/pallas_call | solution.py:138
  29.4 3.6 %collective-permute-start.15 = (bf16[64,1152]{1,0:T(8,128)(2,1)S(1)}, bf16[64,1152]{1,0:T(8,128)(2,1)S(1)}, u32[]{:S(2)}, u32[]{:S(2)}) collective-permute-start(bf16[64,1152]{1,0:T(8,128)(2,1)S(1)} %attention.1.refs_1_.block), channel_id=1, source_target_pairs={{0,4},{1,5},{2,6},{3,7},{4,0},{5,1},{6,2},{7,3},{8,12},{9,13},{10,... | collective-permute-start | bytes 442376 | tf_op jit(solution)/shard_map/ppermute | solution.py:334
  33.1 2.4 %collective-permute-start.17 = (bf16[64,1152]{1,0:T(8,128)(2,1)S(1)}, bf16[64,1152]{1,0:T(8,128)(2,1)S(1)}, u32[]{:S(2)}, u32[]{:S(2)}) collective-permute-start(bf16[64,1152]{1,0:T(8,128)(2,1)S(1)} %attention.1.refs_1_.block), channel_id=1, source_target_pairs={{0,12},{1,13},{2,14},{3,15},{4,8},{5,9},{6,10},{7,11},{8,4},{9,5},... | collective-permute-start | bytes 442376 | tf_op jit(solution)/shard_map/ppermute | solution.py:334
  35.5 2.4 %collective-permute-start.22 = (bf16[64,1152]{1,0:T(8,128)(2,1)S(1)}, bf16[64,1152]{1,0:T(8,128)(2,1)S(1)}, u32[]{:S(2)}, u32[]{:S(2)}) collective-permute-start(bf16[64,1152]{1,0:T(8,128)(2,1)S(1)} %attention.1.refs_1_.block), channel_id=1, source_target_pairs={{0,1},{1,0},{2,3},{3,2},{4,5},{5,4},{6,7},{7,6},{8,9},{9,8},{10,11... | collective-permute-start | bytes 442376 | tf_op jit(solution)/shard_map/ppermute | solution.py:334
  37.9 1.7 %collective-permute-start.19 = (bf16[64,1152]{1,0:T(8,128)(2,1)S(1)}, bf16[64,1152]{1,0:T(8,128)(2,1)S(1)}, u32[]{:S(2)}, u32[]{:S(2)}) collective-permute-start(bf16[64,1152]{1,0:T(8,128)(2,1)S(1)} %collective-permute-done.15.refs_2_), channel_id=1, source_target_pairs={{0,2},{1,3},{2,0},{3,1},{4,6},{5,7},{6,4},{7,5},{8,10},{9,11},{10,... | collective-permute-start | bytes 442376 | tf_op jit(solution)/shard_map/ppermute | solution.py:334
  39.7 6.8 %collective-permute-done.16.refs_3_ = bf16[64,1152]{1,0:T(8,128)(2,1)S(1)} collective-permute-done((bf16[64,1152]{1,0:T(8,128)(2,1)S(1)}, bf16[64,1152]{1,0:T(8,128)(2,1)S(1)}, u32[]{:S(2)}, u32[]{:S(2)}) %collective-permute-start.16) | collective-permute-done | bytes 147488 | tf_op jit(solution)/shard_map/ppermute | solution.py:334
  46.5 2.0 %collective-permute-start.21 = (bf16[64,1152]{1,0:T(8,128)(2,1)S(1)}, bf16[64,1152]{1,0:T(8,128)(2,1)S(1)}, u32[]{:S(2)}, u32[]{:S(2)}) collective-permute-start(bf16[64,1152]{1,0:T(8,128)(2,1)S(1)} %collective-permute-done.17.refs_4_), channel_id=1, source_target_pairs={{0,2},{1,3},{2,0},{3,1},{4,6},{5,7},{6,4},{7,5},{8,10},{9,11},{10,... | collective-permute-start | bytes 442376 | tf_op jit(solution)/shard_map/ppermute | solution.py:334
  48.5 0.5 collective-permute-start.24
  49.0 0.1 collective-permute-start.25
  49.1 4.1 %collective-permute-done.20.refs_7_ = bf16[64,1152]{1,0:T(8,128)(2,1)S(1)} collective-permute-done((bf16[64,1152]{1,0:T(8,128)(2,1)S(1)}, bf16[64,1152]{1,0:T(8,128)(2,1)S(1)}, u32[]{:S(2)}, u32[]{:S(2)}) %collective-permute-start.20) | collective-permute-done | bytes 147488 | tf_op jit(solution)/shard_map/ppermute | solution.py:334
  53.2 2.3 %collective-permute-done.21.refs_8_ = bf16[64,1152]{1,0:T(8,128)(2,1)S(1)} collective-permute-done((bf16[64,1152]{1,0:T(8,128)(2,1)S(1)}, bf16[64,1152]{1,0:T(8,128)(2,1)S(1)}, u32[]{:S(2)}, u32[]{:S(2)}) %collective-permute-start.21) | collective-permute-done | bytes 147488 | tf_op jit(solution)/shard_map/ppermute | solution.py:334
  55.5 0.5 collective-permute-start.28
  56.0 0.1 collective-permute-start.29
  56.1 0.2 select_reduce_fusion.refs_0_
  56.3 0.6 collective-permute-done.27.refs_14_
  56.9 0.2 collective-permute-done.28.refs_15_
  57.1 0.3 collective-permute-done.29.refs_16_
  57.4 2.6 %projection.1.refs_0_ = bf16[128,512]{1,0:T(8,128)(2,1)S(1)} custom-call(s32[16]{0:T(128)S(1)} %select_reduce_fusion.refs_0_, bf16[64,1152]{1,0:T(8,128)(2,1)S(1)} %attention.1.refs_1_.block, bf16[64,1152]{1,0:T(8,128)(2,1)S(1)} %collective-permute-done.15.refs_2_, bf16[64,1152]{1,0:T(8,128)(2,1)S(1)} %collective-permute-done.16.refs_3_, ...), custom_call_target="tpu_custom_call" | custom-call | flops 536870912 | bytes 6553600 | tf_op jit(solution)/shard_map/projection/pallas_call | solution.py:216
  60.0 0.0 slice-start.1
  60.1 0.0 slice-start.5
  60.1 0.0 copy-start.1
  60.1 0.3 collective-permute-start.36
  60.4 0.1 collective-permute-start.44
  60.5 0.7 collective-permute-start.42
  61.2 1.5 %collective-permute-start.30 = (bf16[128,512]{1,0:T(8,128)(2,1)S(1)}, bf16[128,512]{1,0:T(8,128)(2,1)S(1)}, u32[]{:S(2)}, u32[]{:S(2)}) collective-permute-start(bf16[128,512]{1,0:T(8,128)(2,1)S(1)} %projection.1.refs_0_), channel_id=1, source_target_pairs={{0,4},{1,5},{2,6},{3,7},{4,0},{5,1},{6,2},{7,3},{8,12},{9,13},{10,... | collective-permute-start | bytes 393224 | tf_op jit(solution)/shard_map/ppermute | solution.py:334
  62.7 2.6 %collective-permute-start.32 = (bf16[128,512]{1,0:T(8,128)(2,1)S(1)}, bf16[128,512]{1,0:T(8,128)(2,1)S(1)}, u32[]{:S(2)}, u32[]{:S(2)}) collective-permute-start(bf16[128,512]{1,0:T(8,128)(2,1)S(1)} %projection.1.refs_0_), channel_id=1, source_target_pairs={{0,12},{1,13},{2,14},{3,15},{4,8},{5,9},{6,10},{7,11},{8,4},{9,5},... | collective-permute-start | bytes 393224 | tf_op jit(solution)/shard_map/ppermute | solution.py:334
  65.3 5.0 %collective-permute-done.36.refs_0_ = bf16[128,512]{1,0:T(8,128)(2,1)S(1)} collective-permute-done((bf16[128,512]{1,0:T(8,128)(2,1)S(1)}, bf16[128,512]{1,0:T(8,128)(2,1)S(1)}, u32[]{:S(2)}, u32[]{:S(2)}) %collective-permute-start.36) | collective-permute-done | bytes 131104 | tf_op jit(solution)/shard_map/ppermute | solution.py:334
  70.3 0.0 collective-permute-start.37
  70.4 0.5 collective-permute-start.43
  70.9 2.7 %collective-permute-start.31 = (bf16[128,512]{1,0:T(8,128)(2,1)S(1)}, bf16[128,512]{1,0:T(8,128)(2,1)S(1)}, u32[]{:S(2)}, u32[]{:S(2)}) collective-permute-start(bf16[128,512]{1,0:T(8,128)(2,1)S(1)} %collective-permute-done.30.refs_0_), channel_id=1, source_target_pairs={{0,2},{1,3},{2,0},{3,1},{4,6},{5,7},{6,4},{7,5},{8,10},{9,11},{10,... | collective-permute-start | bytes 393224 | tf_op jit(solution)/shard_map/ppermute | solution.py:334
  73.6 0.0 collective-permute-start.33
  73.7 0.7 copy.14
  74.3 0.5 collective-permute-start.39
  74.8 1.8 %collective-permute-done.37.refs_2_ = bf16[128,512]{1,0:T(8,128)(2,1)S(1)} collective-permute-done((bf16[128,512]{1,0:T(8,128)(2,1)S(1)}, bf16[128,512]{1,0:T(8,128)(2,1)S(1)}, u32[]{:S(2)}, u32[]{:S(2)}) %collective-permute-start.37) | collective-permute-done | bytes 131104 | tf_op jit(solution)/shard_map/ppermute | solution.py:334
  76.8 1.3 %shard_map.131 = (f32[128,896]{1,0:T(8,128)S(1)}, f32[128,896]{1,0:T(8,128)S(1)}, f32[128,128]{1,0:T(8,128)S(1)}) custom-call(s32[16]{0:T(128)S(1)} %fusion.5.order.refs_0_, bf16[128,512]{1,0:T(8,128)(2,1)S(1)} %projection.1.refs_0_, bf16[128,512]{1,0:T(8,128)(2,1)S(1)} %collective-permute-done.44.refs_1_, f32[16,1,512]{2,1,0:T(1,128)S(1)} %bitcast.10, ...), custom_call_target="tpu_custom_call" | custom-call | flops 469762048 | bytes 262144 | tf_op jit(solution)/shard_map/pallas_call | solution.py:290
  78.1 1.4 %collective-permute-done.31.refs_1_ = bf16[128,512]{1,0:T(8,128)(2,1)S(1)} collective-permute-done((bf16[128,512]{1,0:T(8,128)(2,1)S(1)}, bf16[128,512]{1,0:T(8,128)(2,1)S(1)}, u32[]{:S(2)}, u32[]{:S(2)}) %collective-permute-start.31) | collective-permute-done | bytes 131104 | tf_op jit(solution)/shard_map/ppermute | solution.py:334
  79.5 2.3 %collective-permute-done.33.refs_2_ = bf16[128,512]{1,0:T(8,128)(2,1)S(1)} collective-permute-done((bf16[128,512]{1,0:T(8,128)(2,1)S(1)}, bf16[128,512]{1,0:T(8,128)(2,1)S(1)}, u32[]{:S(2)}, u32[]{:S(2)}) %collective-permute-start.33) | collective-permute-done | bytes 131104 | tf_op jit(solution)/shard_map/ppermute | solution.py:334
  81.8 1.8 %shard_map.132 = (f32[128,896]{1,0:T(8,128)S(1)}, f32[128,896]{1,0:T(8,128)S(1)}, f32[128,128]{1,0:T(8,128)S(1)}) custom-call(s32[16]{0:T(128)S(1)} %fusion.5.order.refs_0_, bf16[128,512]{1,0:T(8,128)(2,1)S(1)} %collective-permute-done.36.refs_0_, bf16[128,512]{1,0:T(8,128)(2,1)S(1)} %collective-permute-done.41.refs_1_, ...), custom_call_target="tpu_custom_call" | custom-call | flops 939524096 | bytes 524288 | tf_op jit(solution)/shard_map/pallas_call | solution.py:290
  83.7 2.4 %shard_map.133 = (f32[128,896]{1,0:T(8,128)S(1)}, f32[128,896]{1,0:T(8,128)S(1)}, f32[128,128]{1,0:T(8,128)S(1)}) custom-call(s32[16]{0:T(128)S(1)} %fusion.5.order.refs_0_, bf16[128,512]{1,0:T(8,128)(2,1)S(1)} %collective-permute-done.30.refs_0_, bf16[128,512]{1,0:T(8,128)(2,1)S(1)} %collective-permute-done.32.refs_1_, ...), custom_call_target="tpu_custom_call" | custom-call | flops 1409286144 | bytes 786432 | tf_op jit(solution)/shard_map/pallas_call | solution.py:290
  86.1 2.6 %shard_map.134 = bf16[128,896]{1,0:T(8,128)(2,1)} custom-call(s32[16]{0:T(128)S(1)} %fusion.5.order.refs_0_, bf16[128,512]{1,0:T(8,128)(2,1)S(1)} %collective-permute-done.31.refs_1_, bf16[128,512]{1,0:T(8,128)(2,1)S(1)} %collective-permute-done.33.refs_2_, bf16[128,512]{1,0:T(8,128)(2,1)S(1)} %collective-permute-done.34.refs_3_, ...), custom_call_target="tpu_custom_call" | custom-call | flops 939524096 | bytes 524288 | tf_op jit(solution)/shard_map/pallas_call | solution.py:290
  (65 shorter events, 0.2 us)
Async XLA Ops:
  0.6 55.5 %copy-start.2 = (s32[16]{0:T(128)S(1)}, s32[16]{0:T(128)}, u32[]{:S(2)}) copy-start(s32[16]{0:T(128)} %param.17) | copy-start | bytes 196
  1.5 13.5 %collective-permute-start = (bf16[8,5120]{1,0:T(8,128)(2,1)S(1)}, bf16[8,5120]{1,0:T(8,128)(2,1)S(1)}, u32[]{:S(2)}, u32[]{:S(2)}) collective-permute-start(bf16[8,5120]{1,0:T(8,128)(2,1)S(1)} %bitcast.14), channel_id=1, source_target_pairs={{0,4},{1,5},{2,6},{3,7},{4,0},{5,1},{6,2},{7,3},{8,12},{9,13},{10,... | collective-permute-start | bytes 245768 | tf_op jit(solution)/shard_map/ppermute | solution.py:334
  4.6 10.5 %collective-permute-start.1 = (bf16[8,5120]{1,0:T(8,128)(2,1)S(1)}, bf16[8,5120]{1,0:T(8,128)(2,1)S(1)}, u32[]{:S(2)}, u32[]{:S(2)}) collective-permute-start(bf16[8,5120]{1,0:T(8,128)(2,1)S(1)} %bitcast.15), channel_id=1, source_target_pairs={{0,8},{1,9},{2,10},{3,11},{4,12},{5,13},{6,14},{7,15},{8,0},{9,1},... | collective-permute-start | bytes 245768 | tf_op jit(solution)/shard_map/ppermute | solution.py:334
  7.2 6.3 %collective-permute-start.2 = (bf16[8,5120]{1,0:T(8,128)(2,1)S(1)}, bf16[8,5120]{1,0:T(8,128)(2,1)S(1)}, u32[]{:S(2)}, u32[]{:S(2)}) collective-permute-start(bf16[8,5120]{1,0:T(8,128)(2,1)S(1)} %bitcast.16), channel_id=1, source_target_pairs={{0,12},{1,13},{2,14},{3,15},{4,8},{5,9},{6,10},{7,11},{8,4},{9,5},... | collective-permute-start | bytes 245768 | tf_op jit(solution)/shard_map/ppermute | solution.py:334
  7.2 8.4 %collective-permute-start.3 = (bf16[8,5120]{1,0:T(8,128)(2,1)S(1)}, bf16[8,5120]{1,0:T(8,128)(2,1)S(1)}, u32[]{:S(2)}, u32[]{:S(2)}) collective-permute-start(bf16[8,5120]{1,0:T(8,128)(2,1)S(1)} %bitcast.17), channel_id=1, source_target_pairs={{0,2},{1,3},{2,0},{3,1},{4,6},{5,7},{6,4},{7,5},{8,10},{9,11},{10,... | collective-permute-start | bytes 245768 | tf_op jit(solution)/shard_map/ppermute | solution.py:334
  8.9 6.9 %collective-permute-start.7 = (bf16[8,5120]{1,0:T(8,128)(2,1)S(1)}, bf16[8,5120]{1,0:T(8,128)(2,1)S(1)}, u32[]{:S(2)}, u32[]{:S(2)}) collective-permute-start(bf16[8,5120]{1,0:T(8,128)(2,1)S(1)} %bitcast.18), channel_id=1, source_target_pairs={{0,1},{1,0},{2,3},{3,2},{4,5},{5,4},{6,7},{7,6},{8,9},{9,8},{10,11... | collective-permute-start | bytes 245768 | tf_op jit(solution)/shard_map/ppermute | solution.py:334
  9.0 48.4 %copy-start = (bf16[4096,512]{1,0:T(8,128)(2,1)S(1)}, bf16[4096,512]{1,0:T(8,128)(2,1)}, u32[]{:S(2)}) copy-start(bf16[4096,512]{1,0:T(8,128)(2,1)} %refs_17_.3) | copy-start | bytes 12582916
  13.5 8.1 %collective-permute-start.6 = (bf16[8,5120]{1,0:T(8,128)(2,1)S(1)}, bf16[8,5120]{1,0:T(8,128)(2,1)S(1)}, u32[]{:S(2)}, u32[]{:S(2)}) collective-permute-start(bf16[8,5120]{1,0:T(8,128)(2,1)S(1)} %collective-permute-done.2.refs_3_), channel_id=1, source_target_pairs={{0,2},{1,3},{2,0},{3,1},{4,6},{5,7},{6,4},{7,5},{8,10},{9,11},{10,... | collective-permute-start | bytes 245768 | tf_op jit(solution)/shard_map/ppermute | solution.py:334
  15.1 7.1 %collective-permute-start.10 = (bf16[8,5120]{1,0:T(8,128)(2,1)S(1)}, bf16[8,5120]{1,0:T(8,128)(2,1)S(1)}, u32[]{:S(2)}, u32[]{:S(2)}) collective-permute-start(bf16[8,5120]{1,0:T(8,128)(2,1)S(1)} %collective-permute-done.2.refs_3_), channel_id=1, source_target_pairs={{0,1},{1,0},{2,3},{3,2},{4,5},{5,4},{6,7},{7,6},{8,9},{9,8},{10,11... | collective-permute-start | bytes 245768 | tf_op jit(solution)/shard_map/ppermute | solution.py:334
  15.1 5.4 %collective-permute-start.4 = (bf16[8,5120]{1,0:T(8,128)(2,1)S(1)}, bf16[8,5120]{1,0:T(8,128)(2,1)S(1)}, u32[]{:S(2)}, u32[]{:S(2)}) collective-permute-start(bf16[8,5120]{1,0:T(8,128)(2,1)S(1)} %collective-permute-done.refs_1_), channel_id=1, source_target_pairs={{0,2},{1,3},{2,0},{3,1},{4,6},{5,7},{6,4},{7,5},{8,10},{9,11},{10,... | collective-permute-start | bytes 245768 | tf_op jit(solution)/shard_map/ppermute | solution.py:334
  15.6 6.6 %collective-permute-start.8 = (bf16[8,5120]{1,0:T(8,128)(2,1)S(1)}, bf16[8,5120]{1,0:T(8,128)(2,1)S(1)}, u32[]{:S(2)}, u32[]{:S(2)}) collective-permute-start(bf16[8,5120]{1,0:T(8,128)(2,1)S(1)} %collective-permute-done.refs_1_), channel_id=1, source_target_pairs={{0,1},{1,0},{2,3},{3,2},{4,5},{5,4},{6,7},{7,6},{8,9},{9,8},{10,11... | collective-permute-start | bytes 245768 | tf_op jit(solution)/shard_map/ppermute | solution.py:334
  15.8 5.9 %collective-permute-start.5 = (bf16[8,5120]{1,0:T(8,128)(2,1)S(1)}, bf16[8,5120]{1,0:T(8,128)(2,1)S(1)}, u32[]{:S(2)}, u32[]{:S(2)}) collective-permute-start(bf16[8,5120]{1,0:T(8,128)(2,1)S(1)} %collective-permute-done.1.refs_2_), channel_id=1, source_target_pairs={{0,2},{1,3},{2,0},{3,1},{4,6},{5,7},{6,4},{7,5},{8,10},{9,11},{10,... | collective-permute-start | bytes 245768 | tf_op jit(solution)/shard_map/ppermute | solution.py:334
  20.4 2.3 %collective-permute-start.9 = (bf16[8,5120]{1,0:T(8,128)(2,1)S(1)}, bf16[8,5120]{1,0:T(8,128)(2,1)S(1)}, u32[]{:S(2)}, u32[]{:S(2)}) collective-permute-start(bf16[8,5120]{1,0:T(8,128)(2,1)S(1)} %collective-permute-done.1.refs_2_), channel_id=1, source_target_pairs={{0,1},{1,0},{2,3},{3,2},{4,5},{5,4},{6,7},{7,6},{8,9},{9,8},{10,11... | collective-permute-start | bytes 245768 | tf_op jit(solution)/shard_map/ppermute | solution.py:334
  21.7 1.3 %collective-permute-start.11 = (bf16[8,5120]{1,0:T(8,128)(2,1)S(1)}, bf16[8,5120]{1,0:T(8,128)(2,1)S(1)}, u32[]{:S(2)}, u32[]{:S(2)}) collective-permute-start(bf16[8,5120]{1,0:T(8,128)(2,1)S(1)} %collective-permute-done.3.refs_4_), channel_id=1, source_target_pairs={{0,1},{1,0},{2,3},{3,2},{4,5},{5,4},{6,7},{7,6},{8,9},{9,8},{10,11... | collective-permute-start | bytes 245768 | tf_op jit(solution)/shard_map/ppermute | solution.py:334
  21.7 1.4 %collective-permute-start.12 = (bf16[8,5120]{1,0:T(8,128)(2,1)S(1)}, bf16[8,5120]{1,0:T(8,128)(2,1)S(1)}, u32[]{:S(2)}, u32[]{:S(2)}) collective-permute-start(bf16[8,5120]{1,0:T(8,128)(2,1)S(1)} %collective-permute-done.4.refs_5_), channel_id=1, source_target_pairs={{0,1},{1,0},{2,3},{3,2},{4,5},{5,4},{6,7},{7,6},{8,9},{9,8},{10,11... | collective-permute-start | bytes 245768 | tf_op jit(solution)/shard_map/ppermute | solution.py:334
  22.2 1.3 %collective-permute-start.13 = (bf16[8,5120]{1,0:T(8,128)(2,1)S(1)}, bf16[8,5120]{1,0:T(8,128)(2,1)S(1)}, u32[]{:S(2)}, u32[]{:S(2)}) collective-permute-start(bf16[8,5120]{1,0:T(8,128)(2,1)S(1)} %collective-permute-done.5.refs_6_), channel_id=1, source_target_pairs={{0,1},{1,0},{2,3},{3,2},{4,5},{5,4},{6,7},{7,6},{8,9},{9,8},{10,11... | collective-permute-start | bytes 245768 | tf_op jit(solution)/shard_map/ppermute | solution.py:334
  22.3 1.4 %collective-permute-start.14 = (bf16[8,5120]{1,0:T(8,128)(2,1)S(1)}, bf16[8,5120]{1,0:T(8,128)(2,1)S(1)}, u32[]{:S(2)}, u32[]{:S(2)}) collective-permute-start(bf16[8,5120]{1,0:T(8,128)(2,1)S(1)} %collective-permute-done.6.refs_7_), channel_id=1, source_target_pairs={{0,1},{1,0},{2,3},{3,2},{4,5},{5,4},{6,7},{7,6},{8,9},{9,8},{10,11... | collective-permute-start | bytes 245768 | tf_op jit(solution)/shard_map/ppermute | solution.py:334
  29.4 8.5 %collective-permute-start.15 = (bf16[64,1152]{1,0:T(8,128)(2,1)S(1)}, bf16[64,1152]{1,0:T(8,128)(2,1)S(1)}, u32[]{:S(2)}, u32[]{:S(2)}) collective-permute-start(bf16[64,1152]{1,0:T(8,128)(2,1)S(1)} %attention.1.refs_1_.block), channel_id=1, source_target_pairs={{0,4},{1,5},{2,6},{3,7},{4,0},{5,1},{6,2},{7,3},{8,12},{9,13},{10,... | collective-permute-start | bytes 442376 | tf_op jit(solution)/shard_map/ppermute | solution.py:334
  33.1 13.4 %collective-permute-start.16 = (bf16[64,1152]{1,0:T(8,128)(2,1)S(1)}, bf16[64,1152]{1,0:T(8,128)(2,1)S(1)}, u32[]{:S(2)}, u32[]{:S(2)}) collective-permute-start(bf16[64,1152]{1,0:T(8,128)(2,1)S(1)} %attention.1.refs_1_.block), channel_id=1, source_target_pairs={{0,8},{1,9},{2,10},{3,11},{4,12},{5,13},{6,14},{7,15},{8,0},{9,1},... | collective-permute-start | bytes 442376 | tf_op jit(solution)/shard_map/ppermute | solution.py:334
  33.1 13.4 %collective-permute-start.17 = (bf16[64,1152]{1,0:T(8,128)(2,1)S(1)}, bf16[64,1152]{1,0:T(8,128)(2,1)S(1)}, u32[]{:S(2)}, u32[]{:S(2)}) collective-permute-start(bf16[64,1152]{1,0:T(8,128)(2,1)S(1)} %attention.1.refs_1_.block), channel_id=1, source_target_pairs={{0,12},{1,13},{2,14},{3,15},{4,8},{5,9},{6,10},{7,11},{8,4},{9,5},... | collective-permute-start | bytes 442376 | tf_op jit(solution)/shard_map/ppermute | solution.py:334
  35.5 13.0 %collective-permute-start.18 = (bf16[64,1152]{1,0:T(8,128)(2,1)S(1)}, bf16[64,1152]{1,0:T(8,128)(2,1)S(1)}, u32[]{:S(2)}, u32[]{:S(2)}) collective-permute-start(bf16[64,1152]{1,0:T(8,128)(2,1)S(1)} %attention.1.refs_1_.block), channel_id=1, source_target_pairs={{0,2},{1,3},{2,0},{3,1},{4,6},{5,7},{6,4},{7,5},{8,10},{9,11},{10,... | collective-permute-start | bytes 442376 | tf_op jit(solution)/shard_map/ppermute | solution.py:334
  35.5 13.0 %collective-permute-start.22 = (bf16[64,1152]{1,0:T(8,128)(2,1)S(1)}, bf16[64,1152]{1,0:T(8,128)(2,1)S(1)}, u32[]{:S(2)}, u32[]{:S(2)}) collective-permute-start(bf16[64,1152]{1,0:T(8,128)(2,1)S(1)} %attention.1.refs_1_.block), channel_id=1, source_target_pairs={{0,1},{1,0},{2,3},{3,2},{4,5},{5,4},{6,7},{7,6},{8,9},{9,8},{10,11... | collective-permute-start | bytes 442376 | tf_op jit(solution)/shard_map/ppermute | solution.py:334
  37.9 11.1 %collective-permute-start.19 = (bf16[64,1152]{1,0:T(8,128)(2,1)S(1)}, bf16[64,1152]{1,0:T(8,128)(2,1)S(1)}, u32[]{:S(2)}, u32[]{:S(2)}) collective-permute-start(bf16[64,1152]{1,0:T(8,128)(2,1)S(1)} %collective-permute-done.15.refs_2_), channel_id=1, source_target_pairs={{0,2},{1,3},{2,0},{3,1},{4,6},{5,7},{6,4},{7,5},{8,10},{9,11},{10,... | collective-permute-start | bytes 442376 | tf_op jit(solution)/shard_map/ppermute | solution.py:334
  46.5 6.7 %collective-permute-start.20 = (bf16[64,1152]{1,0:T(8,128)(2,1)S(1)}, bf16[64,1152]{1,0:T(8,128)(2,1)S(1)}, u32[]{:S(2)}, u32[]{:S(2)}) collective-permute-start(bf16[64,1152]{1,0:T(8,128)(2,1)S(1)} %collective-permute-done.16.refs_3_), channel_id=1, source_target_pairs={{0,2},{1,3},{2,0},{3,1},{4,6},{5,7},{6,4},{7,5},{8,10},{9,11},{10,... | collective-permute-start | bytes 442376 | tf_op jit(solution)/shard_map/ppermute | solution.py:334
  46.5 9.0 %collective-permute-start.21 = (bf16[64,1152]{1,0:T(8,128)(2,1)S(1)}, bf16[64,1152]{1,0:T(8,128)(2,1)S(1)}, u32[]{:S(2)}, u32[]{:S(2)}) collective-permute-start(bf16[64,1152]{1,0:T(8,128)(2,1)S(1)} %collective-permute-done.17.refs_4_), channel_id=1, source_target_pairs={{0,2},{1,3},{2,0},{3,1},{4,6},{5,7},{6,4},{7,5},{8,10},{9,11},{10,... | collective-permute-start | bytes 442376 | tf_op jit(solution)/shard_map/ppermute | solution.py:334
  48.5 7.0 %collective-permute-start.23 = (bf16[64,1152]{1,0:T(8,128)(2,1)S(1)}, bf16[64,1152]{1,0:T(8,128)(2,1)S(1)}, u32[]{:S(2)}, u32[]{:S(2)}) collective-permute-start(bf16[64,1152]{1,0:T(8,128)(2,1)S(1)} %collective-permute-done.15.refs_2_), channel_id=1, source_target_pairs={{0,1},{1,0},{2,3},{3,2},{4,5},{5,4},{6,7},{7,6},{8,9},{9,8},{10,11... | collective-permute-start | bytes 442376 | tf_op jit(solution)/shard_map/ppermute | solution.py:334
  48.5 7.5 %collective-permute-start.24 = (bf16[64,1152]{1,0:T(8,128)(2,1)S(1)}, bf16[64,1152]{1,0:T(8,128)(2,1)S(1)}, u32[]{:S(2)}, u32[]{:S(2)}) collective-permute-start(bf16[64,1152]{1,0:T(8,128)(2,1)S(1)} %collective-permute-done.16.refs_3_), channel_id=1, source_target_pairs={{0,1},{1,0},{2,3},{3,2},{4,5},{5,4},{6,7},{7,6},{8,9},{9,8},{10,11... | collective-permute-start | bytes 442376 | tf_op jit(solution)/shard_map/ppermute | solution.py:334
  49.0 7.3 %collective-permute-start.25 = (bf16[64,1152]{1,0:T(8,128)(2,1)S(1)}, bf16[64,1152]{1,0:T(8,128)(2,1)S(1)}, u32[]{:S(2)}, u32[]{:S(2)}) collective-permute-start(bf16[64,1152]{1,0:T(8,128)(2,1)S(1)} %collective-permute-done.17.refs_4_), channel_id=1, source_target_pairs={{0,1},{1,0},{2,3},{3,2},{4,5},{5,4},{6,7},{7,6},{8,9},{9,8},{10,11... | collective-permute-start | bytes 442376 | tf_op jit(solution)/shard_map/ppermute | solution.py:334
  53.2 3.1 %collective-permute-start.26 = (bf16[64,1152]{1,0:T(8,128)(2,1)S(1)}, bf16[64,1152]{1,0:T(8,128)(2,1)S(1)}, u32[]{:S(2)}, u32[]{:S(2)}) collective-permute-start(bf16[64,1152]{1,0:T(8,128)(2,1)S(1)} %collective-permute-done.18.refs_5_), channel_id=1, source_target_pairs={{0,1},{1,0},{2,3},{3,2},{4,5},{5,4},{6,7},{7,6},{8,9},{9,8},{10,11... | collective-permute-start | bytes 442376 | tf_op jit(solution)/shard_map/ppermute | solution.py:334
  55.5 1.4 %collective-permute-start.27 = (bf16[64,1152]{1,0:T(8,128)(2,1)S(1)}, bf16[64,1152]{1,0:T(8,128)(2,1)S(1)}, u32[]{:S(2)}, u32[]{:S(2)}) collective-permute-start(bf16[64,1152]{1,0:T(8,128)(2,1)S(1)} %collective-permute-done.19.refs_6_), channel_id=1, source_target_pairs={{0,1},{1,0},{2,3},{3,2},{4,5},{5,4},{6,7},{7,6},{8,9},{9,8},{10,11... | collective-permute-start | bytes 442376 | tf_op jit(solution)/shard_map/ppermute | solution.py:334
  55.5 1.6 %collective-permute-start.28 = (bf16[64,1152]{1,0:T(8,128)(2,1)S(1)}, bf16[64,1152]{1,0:T(8,128)(2,1)S(1)}, u32[]{:S(2)}, u32[]{:S(2)}) collective-permute-start(bf16[64,1152]{1,0:T(8,128)(2,1)S(1)} %collective-permute-done.20.refs_7_), channel_id=1, source_target_pairs={{0,1},{1,0},{2,3},{3,2},{4,5},{5,4},{6,7},{7,6},{8,9},{9,8},{10,11... | collective-permute-start | bytes 442376 | tf_op jit(solution)/shard_map/ppermute | solution.py:334
  56.0 1.4 %collective-permute-start.29 = (bf16[64,1152]{1,0:T(8,128)(2,1)S(1)}, bf16[64,1152]{1,0:T(8,128)(2,1)S(1)}, u32[]{:S(2)}, u32[]{:S(2)}) collective-permute-start(bf16[64,1152]{1,0:T(8,128)(2,1)S(1)} %collective-permute-done.21.refs_8_), channel_id=1, source_target_pairs={{0,1},{1,0},{2,3},{3,2},{4,5},{5,4},{6,7},{7,6},{8,9},{9,8},{10,11... | collective-permute-start | bytes 442376 | tf_op jit(solution)/shard_map/ppermute | solution.py:334
  57.4 19.3 %slice-start = ((s8[14680064]{0:T(1024)(128)(4,1)}), s8[4194304]{0:T(1024)(128)(4,1)S(1)}, s32[]{:S(2)}) async-start(s8[14680064]{0:T(1024)(128)(4,1)} %bitcast.6), calls=%async_computation | async-start | bytes 8388608
  57.4 19.3 %slice-start.4 = ((s8[14680064]{0:T(1024)(128)(4,1)}), s8[2097152]{0:T(1024)(128)(4,1)S(1)}, s32[]{:S(2)}) async-start(s8[14680064]{0:T(1024)(128)(4,1)} %bitcast.8), calls=%async_computation.4 | async-start | bytes 4194304
  60.0 16.6 %slice-start.1 = ((s8[14680064]{0:T(1024)(128)(4,1)}), s8[4194304]{0:T(1024)(128)(4,1)S(1)}, s32[]{:S(2)}) async-start(s8[14680064]{0:T(1024)(128)(4,1)} %bitcast.6), calls=%async_computation.1 | async-start | bytes 8388608
  60.1 16.6 %slice-start.2 = ((s8[14680064]{0:T(1024)(128)(4,1)}), s8[4194304]{0:T(1024)(128)(4,1)S(1)}, s32[]{:S(2)}) async-start(s8[14680064]{0:T(1024)(128)(4,1)} %bitcast.6), calls=%async_computation.2 | async-start | bytes 8388608
  60.1 16.6 %slice-start.3 = ((s8[14680064]{0:T(1024)(128)(4,1)}), s8[2097152]{0:T(1024)(128)(4,1)S(1)}, s32[]{:S(2)}) async-start(s8[14680064]{0:T(1024)(128)(4,1)} %bitcast.6), calls=%async_computation.3 | async-start | bytes 4194304
  60.1 16.6 %slice-start.5 = ((s8[14680064]{0:T(1024)(128)(4,1)}), s8[4194304]{0:T(1024)(128)(4,1)S(1)}, s32[]{:S(2)}) async-start(s8[14680064]{0:T(1024)(128)(4,1)} %bitcast.8), calls=%async_computation.5 | async-start | bytes 8388608
  60.1 16.6 %slice-start.6 = ((s8[14680064]{0:T(1024)(128)(4,1)}), s8[4194304]{0:T(1024)(128)(4,1)S(1)}, s32[]{:S(2)}) async-start(s8[14680064]{0:T(1024)(128)(4,1)} %bitcast.8), calls=%async_computation.6 | async-start | bytes 8388608
  60.1 16.6 %slice-start.7 = ((s8[14680064]{0:T(1024)(128)(4,1)}), s8[4194304]{0:T(1024)(128)(4,1)S(1)}, s32[]{:S(2)}) async-start(s8[14680064]{0:T(1024)(128)(4,1)} %bitcast.8), calls=%async_computation.7 | async-start | bytes 8388608
  60.1 16.6 %copy-start.1 = (f32[8192]{0:T(1024)S(1)}, f32[8192]{0:T(1024)}, u32[]{:S(2)}) copy-start(f32[8192]{0:T(1024)} %param.21) | copy-start | bytes 98308
  60.1 10.2 %collective-permute-start.36 = (bf16[128,512]{1,0:T(8,128)(2,1)S(1)}, bf16[128,512]{1,0:T(8,128)(2,1)S(1)}, u32[]{:S(2)}, u32[]{:S(2)}) collective-permute-start(bf16[128,512]{1,0:T(8,128)(2,1)S(1)} %projection.1.refs_0_), channel_id=1, source_target_pairs={{0,8},{1,9},{2,10},{3,11},{4,12},{5,13},{6,14},{7,15},{8,0},{9,1},... | collective-permute-start | bytes 393224 | tf_op jit(solution)/shard_map/ppermute | solution.py:334
  60.4 9.9 %collective-permute-start.44 = (bf16[128,512]{1,0:T(8,128)(2,1)S(1)}, bf16[128,512]{1,0:T(8,128)(2,1)S(1)}, u32[]{:S(2)}, u32[]{:S(2)}) collective-permute-start(bf16[128,512]{1,0:T(8,128)(2,1)S(1)} %projection.1.refs_0_), channel_id=1, source_target_pairs={{0,1},{1,0},{2,3},{3,2},{4,5},{5,4},{6,7},{7,6},{8,9},{9,8},{10,11... | collective-permute-start | bytes 393224 | tf_op jit(solution)/shard_map/ppermute | solution.py:334
  60.5 9.9 %collective-permute-start.42 = (bf16[128,512]{1,0:T(8,128)(2,1)S(1)}, bf16[128,512]{1,0:T(8,128)(2,1)S(1)}, u32[]{:S(2)}, u32[]{:S(2)}) collective-permute-start(bf16[128,512]{1,0:T(8,128)(2,1)S(1)} %projection.1.refs_0_), channel_id=1, source_target_pairs={{0,2},{1,3},{2,0},{3,1},{4,6},{5,7},{6,4},{7,5},{8,10},{9,11},{10,... | collective-permute-start | bytes 393224 | tf_op jit(solution)/shard_map/ppermute | solution.py:334
  61.2 9.7 %collective-permute-start.30 = (bf16[128,512]{1,0:T(8,128)(2,1)S(1)}, bf16[128,512]{1,0:T(8,128)(2,1)S(1)}, u32[]{:S(2)}, u32[]{:S(2)}) collective-permute-start(bf16[128,512]{1,0:T(8,128)(2,1)S(1)} %projection.1.refs_0_), channel_id=1, source_target_pairs={{0,4},{1,5},{2,6},{3,7},{4,0},{5,1},{6,2},{7,3},{8,12},{9,13},{10,... | collective-permute-start | bytes 393224 | tf_op jit(solution)/shard_map/ppermute | solution.py:334
  62.7 10.9 %collective-permute-start.32 = (bf16[128,512]{1,0:T(8,128)(2,1)S(1)}, bf16[128,512]{1,0:T(8,128)(2,1)S(1)}, u32[]{:S(2)}, u32[]{:S(2)}) collective-permute-start(bf16[128,512]{1,0:T(8,128)(2,1)S(1)} %projection.1.refs_0_), channel_id=1, source_target_pairs={{0,12},{1,13},{2,14},{3,15},{4,8},{5,9},{6,10},{7,11},{8,4},{9,5},... | collective-permute-start | bytes 393224 | tf_op jit(solution)/shard_map/ppermute | solution.py:334
  70.3 4.0 %collective-permute-start.41 = (bf16[128,512]{1,0:T(8,128)(2,1)S(1)}, bf16[128,512]{1,0:T(8,128)(2,1)S(1)}, u32[]{:S(2)}, u32[]{:S(2)}) collective-permute-start(bf16[128,512]{1,0:T(8,128)(2,1)S(1)} %collective-permute-done.36.refs_0_), channel_id=1, source_target_pairs={{0,1},{1,0},{2,3},{3,2},{4,5},{5,4},{6,7},{7,6},{8,9},{9,8},{10,11... | collective-permute-start | bytes 393224 | tf_op jit(solution)/shard_map/ppermute | solution.py:334
  70.3 6.4 %collective-permute-start.37 = (bf16[128,512]{1,0:T(8,128)(2,1)S(1)}, bf16[128,512]{1,0:T(8,128)(2,1)S(1)}, u32[]{:S(2)}, u32[]{:S(2)}) collective-permute-start(bf16[128,512]{1,0:T(8,128)(2,1)S(1)} %collective-permute-done.36.refs_0_), channel_id=1, source_target_pairs={{0,2},{1,3},{2,0},{3,1},{4,6},{5,7},{6,4},{7,5},{8,10},{9,11},{10,... | collective-permute-start | bytes 393224 | tf_op jit(solution)/shard_map/ppermute | solution.py:334
  70.4 4.0 %collective-permute-start.43 = (bf16[128,512]{1,0:T(8,128)(2,1)S(1)}, bf16[128,512]{1,0:T(8,128)(2,1)S(1)}, u32[]{:S(2)}, u32[]{:S(2)}) collective-permute-start(bf16[128,512]{1,0:T(8,128)(2,1)S(1)} %collective-permute-done.42.refs_2_), channel_id=1, source_target_pairs={{0,1},{1,0},{2,3},{3,2},{4,5},{5,4},{6,7},{7,6},{8,9},{9,8},{10,11... | collective-permute-start | bytes 393224 | tf_op jit(solution)/shard_map/ppermute | solution.py:334
  70.9 8.6 %collective-permute-start.31 = (bf16[128,512]{1,0:T(8,128)(2,1)S(1)}, bf16[128,512]{1,0:T(8,128)(2,1)S(1)}, u32[]{:S(2)}, u32[]{:S(2)}) collective-permute-start(bf16[128,512]{1,0:T(8,128)(2,1)S(1)} %collective-permute-done.30.refs_0_), channel_id=1, source_target_pairs={{0,2},{1,3},{2,0},{3,1},{4,6},{5,7},{6,4},{7,5},{8,10},{9,11},{10,... | collective-permute-start | bytes 393224 | tf_op jit(solution)/shard_map/ppermute | solution.py:334
  73.6 8.2 %collective-permute-start.33 = (bf16[128,512]{1,0:T(8,128)(2,1)S(1)}, bf16[128,512]{1,0:T(8,128)(2,1)S(1)}, u32[]{:S(2)}, u32[]{:S(2)}) collective-permute-start(bf16[128,512]{1,0:T(8,128)(2,1)S(1)} %collective-permute-done.32.refs_1_), channel_id=1, source_target_pairs={{0,2},{1,3},{2,0},{3,1},{4,6},{5,7},{6,4},{7,5},{8,10},{9,11},{10,... | collective-permute-start | bytes 393224 | tf_op jit(solution)/shard_map/ppermute | solution.py:334
  74.3 9.4 %collective-permute-start.38 = (bf16[128,512]{1,0:T(8,128)(2,1)S(1)}, bf16[128,512]{1,0:T(8,128)(2,1)S(1)}, u32[]{:S(2)}, u32[]{:S(2)}) collective-permute-start(bf16[128,512]{1,0:T(8,128)(2,1)S(1)} %collective-permute-done.30.refs_0_), channel_id=1, source_target_pairs={{0,1},{1,0},{2,3},{3,2},{4,5},{5,4},{6,7},{7,6},{8,9},{9,8},{10,11... | collective-permute-start | bytes 393224 | tf_op jit(solution)/shard_map/ppermute | solution.py:334
  74.3 9.4 %collective-permute-start.39 = (bf16[128,512]{1,0:T(8,128)(2,1)S(1)}, bf16[128,512]{1,0:T(8,128)(2,1)S(1)}, u32[]{:S(2)}, u32[]{:S(2)}) collective-permute-start(bf16[128,512]{1,0:T(8,128)(2,1)S(1)} %collective-permute-done.32.refs_1_), channel_id=1, source_target_pairs={{0,1},{1,0},{2,3},{3,2},{4,5},{5,4},{6,7},{7,6},{8,9},{9,8},{10,11... | collective-permute-start | bytes 393224 | tf_op jit(solution)/shard_map/ppermute | solution.py:334
  76.7 7.0 %collective-permute-start.40 = (bf16[128,512]{1,0:T(8,128)(2,1)S(1)}, bf16[128,512]{1,0:T(8,128)(2,1)S(1)}, u32[]{:S(2)}, u32[]{:S(2)}) collective-permute-start(bf16[128,512]{1,0:T(8,128)(2,1)S(1)} %collective-permute-done.37.refs_2_), channel_id=1, source_target_pairs={{0,1},{1,0},{2,3},{3,2},{4,5},{5,4},{6,7},{7,6},{8,9},{9,8},{10,11... | collective-permute-start | bytes 393224 | tf_op jit(solution)/shard_map/ppermute | solution.py:334
  79.5 6.6 %collective-permute-start.34 = (bf16[128,512]{1,0:T(8,128)(2,1)S(1)}, bf16[128,512]{1,0:T(8,128)(2,1)S(1)}, u32[]{:S(2)}, u32[]{:S(2)}) collective-permute-start(bf16[128,512]{1,0:T(8,128)(2,1)S(1)} %collective-permute-done.31.refs_1_), channel_id=1, source_target_pairs={{0,1},{1,0},{2,3},{3,2},{4,5},{5,4},{6,7},{7,6},{8,9},{9,8},{10,11... | collective-permute-start | bytes 393224 | tf_op jit(solution)/shard_map/ppermute | solution.py:334
  81.8 4.3 %collective-permute-start.35 = (bf16[128,512]{1,0:T(8,128)(2,1)S(1)}, bf16[128,512]{1,0:T(8,128)(2,1)S(1)}, u32[]{:S(2)}, u32[]{:S(2)}) collective-permute-start(bf16[128,512]{1,0:T(8,128)(2,1)S(1)} %collective-permute-done.33.refs_2_), channel_id=1, source_target_pairs={{0,1},{1,0},{2,3},{3,2},{4,5},{5,4},{6,7},{7,6},{8,9},{9,8},{10,11... | collective-permute-start | bytes 393224 | tf_op jit(solution)/shard_map/ppermute | solution.py:334

commit v3 on v2

--- a/solution.py
+++ b/solution.py
@@ -244,6 +244,8 @@
         out, totals = refs[0], refs[1:]
     else:
         totals, kept = refs[:2], refs[2]
+    if first:
+        refs[3][...] = blocks[0][...]
     rows, depth = blocks[0].shape
     squares = jnp.zeros((rows, lanes), jnp.float32) if first else given[2][...]
     for number, (slot, block) in enumerate(zip(slots, blocks)):
@@ -274,10 +276,10 @@
     width = gate_weight.shape[1]
     far = pieces // 4
     late = [far + number for number in range(1, far, 2)]
-    late = late + [2 * far + number for number in late]
+    final = [2 * far + number for number in late]
     stages = [[0, 2 * far], [2, 2 * far + 2, far, 3 * far]]
-    known = late + stages[0] + stages[1]
-    stages = stages + [[slot for slot in range(pieces) if slot not in known], late]
+    known = late + final + stages[0] + stages[1]
+    stages = stages + [[slot for slot in range(pieces) if slot not in known], late, final]
     whole = pl.BlockSpec(memory_space=pltpu.VMEM)
     table = gain.reshape(pieces, 1, depth)
     result = ()
@@ -285,6 +287,8 @@
         first, last = number == 0, number == len(stages) - 1
         sums = [jax.ShapeDtypeStruct((rows, width), jnp.float32)] * 2
         sums = sums + [jax.ShapeDtypeStruct((rows, lanes), jnp.float32)]
+        if first:
+            sums = sums + [jax.ShapeDtypeStruct((rows, depth), jnp.bfloat16)]
         shape = jax.ShapeDtypeStruct((rows, width), jnp.bfloat16) if last else tuple(sums)
         kernel = functools.partial(feed_kernel, slots, pieces * depth, first, last)
         result = pl.pallas_call(
@@ -292,7 +296,7 @@
             out_shape=shape,
             in_specs=[pl.BlockSpec(memory_space=pltpu.SMEM)]
             + [whole] * (len(slots) + 3 + len(result) + last),
-            out_specs=whole if last else (whole,) * 3,
+            out_specs=whole if last else (whole,) * len(shape),
             scratch_shapes=[pltpu.VMEM((rows, width), jnp.float32)] * 2 if last else [],
             compiler_params=pltpu.CompilerParams(vmem_limit_bytes=12 << 20),
             cost_estimate=pl.CostEstimate(
@@ -309,7 +313,9 @@
             *result,
             *((mark,) if last else ()),
         )
-    return result
+        if first:
+            result, own = result[:3], result[3]
+    return own, result
 
 
 def mark_kernel(block, out):
@@ -412,7 +418,9 @@
         group,
         head_size,
     )
-    hidden = feed(order, spread(projected, devices), norm_gain, gate_weight, up_weight, mark)
+    projected, hidden = feed(
+        order, spread(projected, devices), norm_gain, gate_weight, up_weight, mark
+    )
     return (projected, hidden)
 
 

time: 89 us -> 89.7 us (level)
  Pallas kernels: 16.5 us -> 17.8 us
    pallas_call x4 -> x5, Pallas kernels: 8.08 us -> 9.37 us  [feed(): pl.pallas_call(kernel if not last else lambda *refs: kernel(*refs[:-4], *...]
  transfers between devices with their start and end apart: 45 -> 45, of which waited for: 17 -> 17; matrix products, arithmetic and copies ran while one was open for 3% -> 2% of each run, Pallas kernels for 6% -> 8%
where the time goes in v3:
time: 89.7 us; the launch traced here: 89.4 us
  starting transfers between devices  34.7 us (39%)
  waiting for transfers between devices  33.3 us (37%)
  Pallas kernels  17.8 us (20%)
  other arithmetic  2.7 us (3%)
  between operations  0.93 us (1%)
    ppermute x45, starting transfers between devices, swap(): return lax.ppermute(value, 'wide', [(i, i ^ bits) for i in range(devices)])  34.7 us
    ppermute x45, waiting for transfers between devices, swap(): return lax.ppermute(value, 'wide', [(i, i ^ bits) for i in range(devices)])  33.3 us
    pallas_call x5, Pallas kernels, feed(): pl.pallas_call(kernel if not last else lambda *refs: kernel(*refs[:-4], *...  9.37 us
    pallas_call x1, Pallas kernels, attention(): pl.pallas_call(functools.partial(attention_kernel, pieces, sequences, row...  5.77 us
    pallas_call x1, Pallas kernels, projection(): pl.pallas_call(functools.partial(projection_kernel, pieces, per_pair, key...  2.64 us
  transfers between devices with their start and end apart: 45, of which 17 were waited for; matrix products, arithmetic and copies ran while one was open for 2% of the time, Pallas kernels for 8%

profile of v3, /device:TPU:0, one launch (start us, length us, event | category | flops | bytes accessed | tf_op | source)
XLA Modules:
  0.0 89.4 jit_solution(10429107105435012193)
XLA Ops:
  0.6 0.0 copy-start.2
  0.6 0.9 pad_maximum_fusion
  1.5 3.1 %collective-permute-start = (bf16[8,5120]{1,0:T(8,128)(2,1)S(1)}, bf16[8,5120]{1,0:T(8,128)(2,1)S(1)}, u32[]{:S(2)}, u32[]{:S(2)}) collective-permute-start(bf16[8,5120]{1,0:T(8,128)(2,1)S(1)} %bitcast.15), channel_id=1, source_target_pairs={{0,4},{1,5},{2,6},{3,7},{4,0},{5,1},{6,2},{7,3},{8,12},{9,13},{10,... | collective-permute-start | bytes 245768 | tf_op jit(solution)/shard_map/ppermute | solution.py:340
  4.6 2.6 %collective-permute-start.1 = (bf16[8,5120]{1,0:T(8,128)(2,1)S(1)}, bf16[8,5120]{1,0:T(8,128)(2,1)S(1)}, u32[]{:S(2)}, u32[]{:S(2)}) collective-permute-start(bf16[8,5120]{1,0:T(8,128)(2,1)S(1)} %bitcast.16), channel_id=1, source_target_pairs={{0,8},{1,9},{2,10},{3,11},{4,12},{5,13},{6,14},{7,15},{8,0},{9,1},... | collective-permute-start | bytes 245768 | tf_op jit(solution)/shard_map/ppermute | solution.py:340
  7.2 0.0 collective-permute-start.2
  7.2 1.7 %collective-permute-start.3 = (bf16[8,5120]{1,0:T(8,128)(2,1)S(1)}, bf16[8,5120]{1,0:T(8,128)(2,1)S(1)}, u32[]{:S(2)}, u32[]{:S(2)}) collective-permute-start(bf16[8,5120]{1,0:T(8,128)(2,1)S(1)} %bitcast.18), channel_id=1, source_target_pairs={{0,2},{1,3},{2,0},{3,1},{4,6},{5,7},{6,4},{7,5},{8,10},{9,11},{10,... | collective-permute-start | bytes 245768 | tf_op jit(solution)/shard_map/ppermute | solution.py:340
  9.0 0.0 copy-start
  9.0 0.8 broadcast_compare_fusion
  9.8 3.7 %collective-permute-done.2.refs_3_ = bf16[8,5120]{1,0:T(8,128)(2,1)S(1)} collective-permute-done((bf16[8,5120]{1,0:T(8,128)(2,1)S(1)}, bf16[8,5120]{1,0:T(8,128)(2,1)S(1)}, u32[]{:S(2)}, u32[]{:S(2)}) %collective-permute-start.2) | collective-permute-done | bytes 81952 | tf_op jit(solution)/shard_map/ppermute | solution.py:340
  13.5 1.5 %collective-permute-start.6 = (bf16[8,5120]{1,0:T(8,128)(2,1)S(1)}, bf16[8,5120]{1,0:T(8,128)(2,1)S(1)}, u32[]{:S(2)}, u32[]{:S(2)}) collective-permute-start(bf16[8,5120]{1,0:T(8,128)(2,1)S(1)} %collective-permute-done.2.refs_3_), channel_id=1, source_target_pairs={{0,2},{1,3},{2,0},{3,1},{4,6},{5,7},{6,4},{7,5},{8,10},{9,11},{10,... | collective-permute-start | bytes 245768 | tf_op jit(solution)/shard_map/ppermute | solution.py:340
  15.1 0.6 collective-permute-start.4
  15.6 0.2 collective-permute-start.8
  15.8 1.5 %collective-permute-start.5 = (bf16[8,5120]{1,0:T(8,128)(2,1)S(1)}, bf16[8,5120]{1,0:T(8,128)(2,1)S(1)}, u32[]{:S(2)}, u32[]{:S(2)}) collective-permute-start(bf16[8,5120]{1,0:T(8,128)(2,1)S(1)} %collective-permute-done.1.refs_2_), channel_id=1, source_target_pairs={{0,2},{1,3},{2,0},{3,1},{4,6},{5,7},{6,4},{7,5},{8,10},{9,11},{10,... | collective-permute-start | bytes 245768 | tf_op jit(solution)/shard_map/ppermute | solution.py:340
  17.3 0.8 fusion.info
  18.1 2.3 %collective-permute-done.4.refs_5_ = bf16[8,5120]{1,0:T(8,128)(2,1)S(1)} collective-permute-done((bf16[8,5120]{1,0:T(8,128)(2,1)S(1)}, bf16[8,5120]{1,0:T(8,128)(2,1)S(1)}, u32[]{:S(2)}, u32[]{:S(2)}) %collective-permute-start.4) | collective-permute-done | bytes 81952 | tf_op jit(solution)/shard_map/ppermute | solution.py:340
  20.4 1.2 %collective-permute-done.5.refs_6_ = bf16[8,5120]{1,0:T(8,128)(2,1)S(1)} collective-permute-done((bf16[8,5120]{1,0:T(8,128)(2,1)S(1)}, bf16[8,5120]{1,0:T(8,128)(2,1)S(1)}, u32[]{:S(2)}, u32[]{:S(2)}) %collective-permute-start.5) | collective-permute-done | bytes 81952 | tf_op jit(solution)/shard_map/ppermute | solution.py:340
  21.7 0.5 collective-permute-start.12
  22.2 0.1 collective-permute-start.13
  22.3 0.4 collective-permute-start.14
  22.7 0.2 collective-permute-done.11.refs_12_
  23.0 0.2 collective-permute-done.12.refs_13_
  23.1 0.4 collective-permute-done.13.refs_14_
  23.5 0.2 collective-permute-done.14.refs_15_
  23.6 5.8 %attention.1.refs_1_.block = bf16[64,1152]{1,0:T(8,128)(2,1)S(1)} custom-call(s32[4]{0:T(128)S(1)} %fusion.info, s32[16]{0:T(128)S(1)} %fusion.5.order.refs_0_, bf16[8,5120]{1,0:T(8,128)(2,1)S(1)} %bitcast.20, bf16[8,5120]{1,0:T(8,128)(2,1)S(1)} %collective-permute-done.refs_1_, bf16[8,5120]{1,0:T(8,128)(2,1)S(1)} %collective-permute-done.1.refs_2_, ...), custom_call_target="tpu_custom_call" | custom-call | flops 2147483648 | bytes 4194304 | tf_op jit(solution)/shard_map/attention/pallas_call | solution.py:138
  29.4 3.6 %collective-permute-start.15 = (bf16[64,1152]{1,0:T(8,128)(2,1)S(1)}, bf16[64,1152]{1,0:T(8,128)(2,1)S(1)}, u32[]{:S(2)}, u32[]{:S(2)}) collective-permute-start(bf16[64,1152]{1,0:T(8,128)(2,1)S(1)} %attention.1.refs_1_.block), channel_id=1, source_target_pairs={{0,4},{1,5},{2,6},{3,7},{4,0},{5,1},{6,2},{7,3},{8,12},{9,13},{10,... | collective-permute-start | bytes 442376 | tf_op jit(solution)/shard_map/ppermute | solution.py:340
  33.1 2.4 %collective-permute-start.17 = (bf16[64,1152]{1,0:T(8,128)(2,1)S(1)}, bf16[64,1152]{1,0:T(8,128)(2,1)S(1)}, u32[]{:S(2)}, u32[]{:S(2)}) collective-permute-start(bf16[64,1152]{1,0:T(8,128)(2,1)S(1)} %attention.1.refs_1_.block), channel_id=1, source_target_pairs={{0,12},{1,13},{2,14},{3,15},{4,8},{5,9},{6,10},{7,11},{8,4},{9,5},... | collective-permute-start | bytes 442376 | tf_op jit(solution)/shard_map/ppermute | solution.py:340
  35.5 2.4 %collective-permute-start.22 = (bf16[64,1152]{1,0:T(8,128)(2,1)S(1)}, bf16[64,1152]{1,0:T(8,128)(2,1)S(1)}, u32[]{:S(2)}, u32[]{:S(2)}) collective-permute-start(bf16[64,1152]{1,0:T(8,128)(2,1)S(1)} %attention.1.refs_1_.block), channel_id=1, source_target_pairs={{0,1},{1,0},{2,3},{3,2},{4,5},{5,4},{6,7},{7,6},{8,9},{9,8},{10,11... | collective-permute-start | bytes 442376 | tf_op jit(solution)/shard_map/ppermute | solution.py:340
  37.9 1.7 %collective-permute-start.19 = (bf16[64,1152]{1,0:T(8,128)(2,1)S(1)}, bf16[64,1152]{1,0:T(8,128)(2,1)S(1)}, u32[]{:S(2)}, u32[]{:S(2)}) collective-permute-start(bf16[64,1152]{1,0:T(8,128)(2,1)S(1)} %collective-permute-done.15.refs_2_), channel_id=1, source_target_pairs={{0,2},{1,3},{2,0},{3,1},{4,6},{5,7},{6,4},{7,5},{8,10},{9,11},{10,... | collective-permute-start | bytes 442376 | tf_op jit(solution)/shard_map/ppermute | solution.py:340
  39.7 6.8 %collective-permute-done.16.refs_3_ = bf16[64,1152]{1,0:T(8,128)(2,1)S(1)} collective-permute-done((bf16[64,1152]{1,0:T(8,128)(2,1)S(1)}, bf16[64,1152]{1,0:T(8,128)(2,1)S(1)}, u32[]{:S(2)}, u32[]{:S(2)}) %collective-permute-start.16) | collective-permute-done | bytes 147488 | tf_op jit(solution)/shard_map/ppermute | solution.py:340
  46.5 2.0 %collective-permute-start.21 = (bf16[64,1152]{1,0:T(8,128)(2,1)S(1)}, bf16[64,1152]{1,0:T(8,128)(2,1)S(1)}, u32[]{:S(2)}, u32[]{:S(2)}) collective-permute-start(bf16[64,1152]{1,0:T(8,128)(2,1)S(1)} %collective-permute-done.17.refs_4_), channel_id=1, source_target_pairs={{0,2},{1,3},{2,0},{3,1},{4,6},{5,7},{6,4},{7,5},{8,10},{9,11},{10,... | collective-permute-start | bytes 442376 | tf_op jit(solution)/shard_map/ppermute | solution.py:340
  48.5 0.5 collective-permute-start.24
  49.0 0.1 collective-permute-start.25
  49.1 4.1 %collective-permute-done.20.refs_7_ = bf16[64,1152]{1,0:T(8,128)(2,1)S(1)} collective-permute-done((bf16[64,1152]{1,0:T(8,128)(2,1)S(1)}, bf16[64,1152]{1,0:T(8,128)(2,1)S(1)}, u32[]{:S(2)}, u32[]{:S(2)}) %collective-permute-start.20) | collective-permute-done | bytes 147488 | tf_op jit(solution)/shard_map/ppermute | solution.py:340
  53.2 2.3 %collective-permute-done.21.refs_8_ = bf16[64,1152]{1,0:T(8,128)(2,1)S(1)} collective-permute-done((bf16[64,1152]{1,0:T(8,128)(2,1)S(1)}, bf16[64,1152]{1,0:T(8,128)(2,1)S(1)}, u32[]{:S(2)}, u32[]{:S(2)}) %collective-permute-start.21) | collective-permute-done | bytes 147488 | tf_op jit(solution)/shard_map/ppermute | solution.py:340
  55.5 0.5 collective-permute-start.28
  56.0 0.1 collective-permute-start.29
  56.1 0.2 select_reduce_fusion.refs_0_
  56.3 0.6 collective-permute-done.27.refs_14_
  56.9 0.2 collective-permute-done.28.refs_15_
  57.1 0.3 collective-permute-done.29.refs_16_
  57.4 2.6 %projection.1.refs_0_ = bf16[128,512]{1,0:T(8,128)(2,1)S(1)} custom-call(s32[16]{0:T(128)S(1)} %select_reduce_fusion.refs_0_, bf16[64,1152]{1,0:T(8,128)(2,1)S(1)} %attention.1.refs_1_.block, bf16[64,1152]{1,0:T(8,128)(2,1)S(1)} %collective-permute-done.15.refs_2_, bf16[64,1152]{1,0:T(8,128)(2,1)S(1)} %collective-permute-done.16.refs_3_, ...), custom_call_target="tpu_custom_call" | custom-call | flops 536870912 | bytes 6553600 | tf_op jit(solution)/shard_map/projection/pallas_call | solution.py:216
  60.0 0.0 slice-start.1
  60.1 0.0 slice-start.5
  60.1 0.0 copy-start.1
  60.1 0.3 collective-permute-start.37
  60.4 0.1 collective-permute-start.30
  60.5 0.7 collective-permute-start.43
  61.2 1.5 %collective-permute-start.31 = (bf16[128,512]{1,0:T(8,128)(2,1)S(1)}, bf16[128,512]{1,0:T(8,128)(2,1)S(1)}, u32[]{:S(2)}, u32[]{:S(2)}) collective-permute-start(bf16[128,512]{1,0:T(8,128)(2,1)S(1)} %projection.1.refs_0_), channel_id=1, source_target_pairs={{0,4},{1,5},{2,6},{3,7},{4,0},{5,1},{6,2},{7,3},{8,12},{9,13},{10,... | collective-permute-start | bytes 393224 | tf_op jit(solution)/shard_map/ppermute | solution.py:340
  62.7 2.6 %collective-permute-start.34 = (bf16[128,512]{1,0:T(8,128)(2,1)S(1)}, bf16[128,512]{1,0:T(8,128)(2,1)S(1)}, u32[]{:S(2)}, u32[]{:S(2)}) collective-permute-start(bf16[128,512]{1,0:T(8,128)(2,1)S(1)} %projection.1.refs_0_), channel_id=1, source_target_pairs={{0,12},{1,13},{2,14},{3,15},{4,8},{5,9},{6,10},{7,11},{8,4},{9,5},... | collective-permute-start | bytes 393224 | tf_op jit(solution)/shard_map/ppermute | solution.py:340
  65.3 5.0 %collective-permute-done.37.refs_0_ = bf16[128,512]{1,0:T(8,128)(2,1)S(1)} collective-permute-done((bf16[128,512]{1,0:T(8,128)(2,1)S(1)}, bf16[128,512]{1,0:T(8,128)(2,1)S(1)}, u32[]{:S(2)}, u32[]{:S(2)}) %collective-permute-start.37) | collective-permute-done | bytes 131104 | tf_op jit(solution)/shard_map/ppermute | solution.py:340
  70.3 0.0 collective-permute-start.38
  70.4 0.5 collective-permute-start.44
  70.9 2.7 %collective-permute-start.32 = (bf16[128,512]{1,0:T(8,128)(2,1)S(1)}, bf16[128,512]{1,0:T(8,128)(2,1)S(1)}, u32[]{:S(2)}, u32[]{:S(2)}) collective-permute-start(bf16[128,512]{1,0:T(8,128)(2,1)S(1)} %collective-permute-done.31.refs_0_), channel_id=1, source_target_pairs={{0,2},{1,3},{2,0},{3,1},{4,6},{5,7},{6,4},{7,5},{8,10},{9,11},{10,... | collective-permute-start | bytes 393224 | tf_op jit(solution)/shard_map/ppermute | solution.py:340
  73.6 0.0 collective-permute-start.35
  73.7 0.1 collective-permute-start.39
  73.7 0.5 collective-permute-start.40
  74.2 2.4 %collective-permute-done.38.refs_2_ = bf16[128,512]{1,0:T(8,128)(2,1)S(1)} collective-permute-done((bf16[128,512]{1,0:T(8,128)(2,1)S(1)}, bf16[128,512]{1,0:T(8,128)(2,1)S(1)}, u32[]{:S(2)}, u32[]{:S(2)}) %collective-permute-start.38) | collective-permute-done | bytes 131104 | tf_op jit(solution)/shard_map/ppermute | solution.py:340
  76.8 1.9 %shard_map.131 = (f32[128,896]{1,0:T(8,128)S(1)}, f32[128,896]{1,0:T(8,128)S(1)}, f32[128,128]{1,0:T(8,128)S(1)}, bf16[128,512]{1,0:T(8,128)(2,1)}) custom-call(s32[16]{0:T(128)S(1)} %fusion.5.order.refs_0_, bf16[128,512]{1,0:T(8,128)(2,1)S(1)} %projection.1.refs_0_, bf16[128,512]{1,0:T(8,128)(2,1)S(1)} %collective-permute-done.30.refs_1_, ...), custom_call_target="tpu_custom_call" | custom-call | flops 469762048 | bytes 262144 | tf_op jit(solution)/shard_map/pallas_call | solution.py:294
  78.6 0.9 collective-permute-done.32.refs_0_
  79.5 2.3 %collective-permute-done.35.refs_1_ = bf16[128,512]{1,0:T(8,128)(2,1)S(1)} collective-permute-done((bf16[128,512]{1,0:T(8,128)(2,1)S(1)}, bf16[128,512]{1,0:T(8,128)(2,1)S(1)}, u32[]{:S(2)}, u32[]{:S(2)}) %collective-permute-start.35) | collective-permute-done | bytes 131104 | tf_op jit(solution)/shard_map/ppermute | solution.py:340
  81.8 1.8 %shard_map.132 = (f32[128,896]{1,0:T(8,128)S(1)}, f32[128,896]{1,0:T(8,128)S(1)}, f32[128,128]{1,0:T(8,128)S(1)}) custom-call(s32[16]{0:T(128)S(1)} %fusion.5.order.refs_0_, bf16[128,512]{1,0:T(8,128)(2,1)S(1)} %collective-permute-done.37.refs_0_, bf16[128,512]{1,0:T(8,128)(2,1)S(1)} %collective-permute-done.42.refs_1_, ...), custom_call_target="tpu_custom_call" | custom-call | flops 939524096 | bytes 524288 | tf_op jit(solution)/shard_map/pallas_call | solution.py:294
  83.7 2.4 %shard_map.133 = (f32[128,896]{1,0:T(8,128)S(1)}, f32[128,896]{1,0:T(8,128)S(1)}, f32[128,128]{1,0:T(8,128)S(1)}) custom-call(s32[16]{0:T(128)S(1)} %fusion.5.order.refs_0_, bf16[128,512]{1,0:T(8,128)(2,1)S(1)} %collective-permute-done.31.refs_0_, bf16[128,512]{1,0:T(8,128)(2,1)S(1)} %collective-permute-done.34.refs_1_, ...), custom_call_target="tpu_custom_call" | custom-call | flops 1409286144 | bytes 786432 | tf_op jit(solution)/shard_map/pallas_call | solution.py:294
  86.1 1.3 %shard_map.134 = (f32[128,896]{1,0:T(8,128)S(1)}, f32[128,896]{1,0:T(8,128)S(1)}, f32[128,128]{1,0:T(8,128)S(1)}) custom-call(s32[16]{0:T(128)S(1)} %fusion.5.order.refs_0_, bf16[128,512]{1,0:T(8,128)(2,1)S(1)} %collective-permute-done.32.refs_0_, bf16[128,512]{1,0:T(8,128)(2,1)S(1)} %collective-permute-done.35.refs_1_, f32[16,1,512]{2,1,0:T(1,128)S(1)} %bitcast.13, ...), custom_call_target="tpu_custom_call" | custom-call | flops 469762048 | bytes 262144 | tf_op jit(solution)/shard_map/pallas_call | solution.py:294
  87.4 2.0 %shard_map.135 = bf16[128,896]{1,0:T(8,128)(2,1)} custom-call(s32[16]{0:T(128)S(1)} %fusion.5.order.refs_0_, bf16[128,512]{1,0:T(8,128)(2,1)S(1)} %collective-permute-done.33.refs_1_, bf16[128,512]{1,0:T(8,128)(2,1)S(1)} %collective-permute-done.36.refs_2_, f32[16,1,512]{2,1,0:T(1,128)S(1)} %bitcast.14, bf16[8192,896]{1,0:T(8,128)(2,1)S(1)} %bitcast.7, ...), custom_call_target="tpu_custom_call" | custom-call | flops 469762048 | bytes 262144 | tf_op jit(solution)/shard_map/pallas_call | solution.py:294
  (65 shorter events, 0.2 us)
Async XLA Ops:
  0.6 55.5 %copy-start.2 = (s32[16]{0:T(128)S(1)}, s32[16]{0:T(128)}, u32[]{:S(2)}) copy-start(s32[16]{0:T(128)} %param.17) | copy-start | bytes 196
  1.5 13.5 %collective-permute-start = (bf16[8,5120]{1,0:T(8,128)(2,1)S(1)}, bf16[8,5120]{1,0:T(8,128)(2,1)S(1)}, u32[]{:S(2)}, u32[]{:S(2)}) collective-permute-start(bf16[8,5120]{1,0:T(8,128)(2,1)S(1)} %bitcast.15), channel_id=1, source_target_pairs={{0,4},{1,5},{2,6},{3,7},{4,0},{5,1},{6,2},{7,3},{8,12},{9,13},{10,... | collective-permute-start | bytes 245768 | tf_op jit(solution)/shard_map/ppermute | solution.py:340
  4.6 10.5 %collective-permute-start.1 = (bf16[8,5120]{1,0:T(8,128)(2,1)S(1)}, bf16[8,5120]{1,0:T(8,128)(2,1)S(1)}, u32[]{:S(2)}, u32[]{:S(2)}) collective-permute-start(bf16[8,5120]{1,0:T(8,128)(2,1)S(1)} %bitcast.16), channel_id=1, source_target_pairs={{0,8},{1,9},{2,10},{3,11},{4,12},{5,13},{6,14},{7,15},{8,0},{9,1},... | collective-permute-start | bytes 245768 | tf_op jit(solution)/shard_map/ppermute | solution.py:340
  7.2 6.3 %collective-permute-start.2 = (bf16[8,5120]{1,0:T(8,128)(2,1)S(1)}, bf16[8,5120]{1,0:T(8,128)(2,1)S(1)}, u32[]{:S(2)}, u32[]{:S(2)}) collective-permute-start(bf16[8,5120]{1,0:T(8,128)(2,1)S(1)} %bitcast.17), channel_id=1, source_target_pairs={{0,12},{1,13},{2,14},{3,15},{4,8},{5,9},{6,10},{7,11},{8,4},{9,5},... | collective-permute-start | bytes 245768 | tf_op jit(solution)/shard_map/ppermute | solution.py:340
  7.2 8.4 %collective-permute-start.3 = (bf16[8,5120]{1,0:T(8,128)(2,1)S(1)}, bf16[8,5120]{1,0:T(8,128)(2,1)S(1)}, u32[]{:S(2)}, u32[]{:S(2)}) collective-permute-start(bf16[8,5120]{1,0:T(8,128)(2,1)S(1)} %bitcast.18), channel_id=1, source_target_pairs={{0,2},{1,3},{2,0},{3,1},{4,6},{5,7},{6,4},{7,5},{8,10},{9,11},{10,... | collective-permute-start | bytes 245768 | tf_op jit(solution)/shard_map/ppermute | solution.py:340
  8.9 6.9 %collective-permute-start.7 = (bf16[8,5120]{1,0:T(8,128)(2,1)S(1)}, bf16[8,5120]{1,0:T(8,128)(2,1)S(1)}, u32[]{:S(2)}, u32[]{:S(2)}) collective-permute-start(bf16[8,5120]{1,0:T(8,128)(2,1)S(1)} %bitcast.19), channel_id=1, source_target_pairs={{0,1},{1,0},{2,3},{3,2},{4,5},{5,4},{6,7},{7,6},{8,9},{9,8},{10,11... | collective-permute-start | bytes 245768 | tf_op jit(solution)/shard_map/ppermute | solution.py:340
  9.0 48.4 %copy-start = (bf16[4096,512]{1,0:T(8,128)(2,1)S(1)}, bf16[4096,512]{1,0:T(8,128)(2,1)}, u32[]{:S(2)}) copy-start(bf16[4096,512]{1,0:T(8,128)(2,1)} %refs_17_.3) | copy-start | bytes 12582916
  13.5 8.1 %collective-permute-start.6 = (bf16[8,5120]{1,0:T(8,128)(2,1)S(1)}, bf16[8,5120]{1,0:T(8,128)(2,1)S(1)}, u32[]{:S(2)}, u32[]{:S(2)}) collective-permute-start(bf16[8,5120]{1,0:T(8,128)(2,1)S(1)} %collective-permute-done.2.refs_3_), channel_id=1, source_target_pairs={{0,2},{1,3},{2,0},{3,1},{4,6},{5,7},{6,4},{7,5},{8,10},{9,11},{10,... | collective-permute-start | bytes 245768 | tf_op jit(solution)/shard_map/ppermute | solution.py:340
  15.1 7.1 %collective-permute-start.10 = (bf16[8,5120]{1,0:T(8,128)(2,1)S(1)}, bf16[8,5120]{1,0:T(8,128)(2,1)S(1)}, u32[]{:S(2)}, u32[]{:S(2)}) collective-permute-start(bf16[8,5120]{1,0:T(8,128)(2,1)S(1)} %collective-permute-done.2.refs_3_), channel_id=1, source_target_pairs={{0,1},{1,0},{2,3},{3,2},{4,5},{5,4},{6,7},{7,6},{8,9},{9,8},{10,11... | collective-permute-start | bytes 245768 | tf_op jit(solution)/shard_map/ppermute | solution.py:340
  15.1 5.4 %collective-permute-start.4 = (bf16[8,5120]{1,0:T(8,128)(2,1)S(1)}, bf16[8,5120]{1,0:T(8,128)(2,1)S(1)}, u32[]{:S(2)}, u32[]{:S(2)}) collective-permute-start(bf16[8,5120]{1,0:T(8,128)(2,1)S(1)} %collective-permute-done.refs_1_), channel_id=1, source_target_pairs={{0,2},{1,3},{2,0},{3,1},{4,6},{5,7},{6,4},{7,5},{8,10},{9,11},{10,... | collective-permute-start | bytes 245768 | tf_op jit(solution)/shard_map/ppermute | solution.py:340
  15.6 6.6 %collective-permute-start.8 = (bf16[8,5120]{1,0:T(8,128)(2,1)S(1)}, bf16[8,5120]{1,0:T(8,128)(2,1)S(1)}, u32[]{:S(2)}, u32[]{:S(2)}) collective-permute-start(bf16[8,5120]{1,0:T(8,128)(2,1)S(1)} %collective-permute-done.refs_1_), channel_id=1, source_target_pairs={{0,1},{1,0},{2,3},{3,2},{4,5},{5,4},{6,7},{7,6},{8,9},{9,8},{10,11... | collective-permute-start | bytes 245768 | tf_op jit(solution)/shard_map/ppermute | solution.py:340
  15.8 5.9 %collective-permute-start.5 = (bf16[8,5120]{1,0:T(8,128)(2,1)S(1)}, bf16[8,5120]{1,0:T(8,128)(2,1)S(1)}, u32[]{:S(2)}, u32[]{:S(2)}) collective-permute-start(bf16[8,5120]{1,0:T(8,128)(2,1)S(1)} %collective-permute-done.1.refs_2_), channel_id=1, source_target_pairs={{0,2},{1,3},{2,0},{3,1},{4,6},{5,7},{6,4},{7,5},{8,10},{9,11},{10,... | collective-permute-start | bytes 245768 | tf_op jit(solution)/shard_map/ppermute | solution.py:340
  20.4 2.3 %collective-permute-start.9 = (bf16[8,5120]{1,0:T(8,128)(2,1)S(1)}, bf16[8,5120]{1,0:T(8,128)(2,1)S(1)}, u32[]{:S(2)}, u32[]{:S(2)}) collective-permute-start(bf16[8,5120]{1,0:T(8,128)(2,1)S(1)} %collective-permute-done.1.refs_2_), channel_id=1, source_target_pairs={{0,1},{1,0},{2,3},{3,2},{4,5},{5,4},{6,7},{7,6},{8,9},{9,8},{10,11... | collective-permute-start | bytes 245768 | tf_op jit(solution)/shard_map/ppermute | solution.py:340
  21.7 1.3 %collective-permute-start.11 = (bf16[8,5120]{1,0:T(8,128)(2,1)S(1)}, bf16[8,5120]{1,0:T(8,128)(2,1)S(1)}, u32[]{:S(2)}, u32[]{:S(2)}) collective-permute-start(bf16[8,5120]{1,0:T(8,128)(2,1)S(1)} %collective-permute-done.3.refs_4_), channel_id=1, source_target_pairs={{0,1},{1,0},{2,3},{3,2},{4,5},{5,4},{6,7},{7,6},{8,9},{9,8},{10,11... | collective-permute-start | bytes 245768 | tf_op jit(solution)/shard_map/ppermute | solution.py:340
  21.7 1.4 %collective-permute-start.12 = (bf16[8,5120]{1,0:T(8,128)(2,1)S(1)}, bf16[8,5120]{1,0:T(8,128)(2,1)S(1)}, u32[]{:S(2)}, u32[]{:S(2)}) collective-permute-start(bf16[8,5120]{1,0:T(8,128)(2,1)S(1)} %collective-permute-done.4.refs_5_), channel_id=1, source_target_pairs={{0,1},{1,0},{2,3},{3,2},{4,5},{5,4},{6,7},{7,6},{8,9},{9,8},{10,11... | collective-permute-start | bytes 245768 | tf_op jit(solution)/shard_map/ppermute | solution.py:340
  22.2 1.3 %collective-permute-start.13 = (bf16[8,5120]{1,0:T(8,128)(2,1)S(1)}, bf16[8,5120]{1,0:T(8,128)(2,1)S(1)}, u32[]{:S(2)}, u32[]{:S(2)}) collective-permute-start(bf16[8,5120]{1,0:T(8,128)(2,1)S(1)} %collective-permute-done.5.refs_6_), channel_id=1, source_target_pairs={{0,1},{1,0},{2,3},{3,2},{4,5},{5,4},{6,7},{7,6},{8,9},{9,8},{10,11... | collective-permute-start | bytes 245768 | tf_op jit(solution)/shard_map/ppermute | solution.py:340
  22.3 1.4 %collective-permute-start.14 = (bf16[8,5120]{1,0:T(8,128)(2,1)S(1)}, bf16[8,5120]{1,0:T(8,128)(2,1)S(1)}, u32[]{:S(2)}, u32[]{:S(2)}) collective-permute-start(bf16[8,5120]{1,0:T(8,128)(2,1)S(1)} %collective-permute-done.6.refs_7_), channel_id=1, source_target_pairs={{0,1},{1,0},{2,3},{3,2},{4,5},{5,4},{6,7},{7,6},{8,9},{9,8},{10,11... | collective-permute-start | bytes 245768 | tf_op jit(solution)/shard_map/ppermute | solution.py:340
  29.4 8.5 %collective-permute-start.15 = (bf16[64,1152]{1,0:T(8,128)(2,1)S(1)}, bf16[64,1152]{1,0:T(8,128)(2,1)S(1)}, u32[]{:S(2)}, u32[]{:S(2)}) collective-permute-start(bf16[64,1152]{1,0:T(8,128)(2,1)S(1)} %attention.1.refs_1_.block), channel_id=1, source_target_pairs={{0,4},{1,5},{2,6},{3,7},{4,0},{5,1},{6,2},{7,3},{8,12},{9,13},{10,... | collective-permute-start | bytes 442376 | tf_op jit(solution)/shard_map/ppermute | solution.py:340
  33.1 13.4 %collective-permute-start.16 = (bf16[64,1152]{1,0:T(8,128)(2,1)S(1)}, bf16[64,1152]{1,0:T(8,128)(2,1)S(1)}, u32[]{:S(2)}, u32[]{:S(2)}) collective-permute-start(bf16[64,1152]{1,0:T(8,128)(2,1)S(1)} %attention.1.refs_1_.block), channel_id=1, source_target_pairs={{0,8},{1,9},{2,10},{3,11},{4,12},{5,13},{6,14},{7,15},{8,0},{9,1},... | collective-permute-start | bytes 442376 | tf_op jit(solution)/shard_map/ppermute | solution.py:340
  33.1 13.4 %collective-permute-start.17 = (bf16[64,1152]{1,0:T(8,128)(2,1)S(1)}, bf16[64,1152]{1,0:T(8,128)(2,1)S(1)}, u32[]{:S(2)}, u32[]{:S(2)}) collective-permute-start(bf16[64,1152]{1,0:T(8,128)(2,1)S(1)} %attention.1.refs_1_.block), channel_id=1, source_target_pairs={{0,12},{1,13},{2,14},{3,15},{4,8},{5,9},{6,10},{7,11},{8,4},{9,5},... | collective-permute-start | bytes 442376 | tf_op jit(solution)/shard_map/ppermute | solution.py:340
  35.5 13.0 %collective-permute-start.18 = (bf16[64,1152]{1,0:T(8,128)(2,1)S(1)}, bf16[64,1152]{1,0:T(8,128)(2,1)S(1)}, u32[]{:S(2)}, u32[]{:S(2)}) collective-permute-start(bf16[64,1152]{1,0:T(8,128)(2,1)S(1)} %attention.1.refs_1_.block), channel_id=1, source_target_pairs={{0,2},{1,3},{2,0},{3,1},{4,6},{5,7},{6,4},{7,5},{8,10},{9,11},{10,... | collective-permute-start | bytes 442376 | tf_op jit(solution)/shard_map/ppermute | solution.py:340
  35.5 13.0 %collective-permute-start.22 = (bf16[64,1152]{1,0:T(8,128)(2,1)S(1)}, bf16[64,1152]{1,0:T(8,128)(2,1)S(1)}, u32[]{:S(2)}, u32[]{:S(2)}) collective-permute-start(bf16[64,1152]{1,0:T(8,128)(2,1)S(1)} %attention.1.refs_1_.block), channel_id=1, source_target_pairs={{0,1},{1,0},{2,3},{3,2},{4,5},{5,4},{6,7},{7,6},{8,9},{9,8},{10,11... | collective-permute-start | bytes 442376 | tf_op jit(solution)/shard_map/ppermute | solution.py:340
  37.9 11.1 %collective-permute-start.19 = (bf16[64,1152]{1,0:T(8,128)(2,1)S(1)}, bf16[64,1152]{1,0:T(8,128)(2,1)S(1)}, u32[]{:S(2)}, u32[]{:S(2)}) collective-permute-start(bf16[64,1152]{1,0:T(8,128)(2,1)S(1)} %collective-permute-done.15.refs_2_), channel_id=1, source_target_pairs={{0,2},{1,3},{2,0},{3,1},{4,6},{5,7},{6,4},{7,5},{8,10},{9,11},{10,... | collective-permute-start | bytes 442376 | tf_op jit(solution)/shard_map/ppermute | solution.py:340
  46.5 6.7 %collective-permute-start.20 = (bf16[64,1152]{1,0:T(8,128)(2,1)S(1)}, bf16[64,1152]{1,0:T(8,128)(2,1)S(1)}, u32[]{:S(2)}, u32[]{:S(2)}) collective-permute-start(bf16[64,1152]{1,0:T(8,128)(2,1)S(1)} %collective-permute-done.16.refs_3_), channel_id=1, source_target_pairs={{0,2},{1,3},{2,0},{3,1},{4,6},{5,7},{6,4},{7,5},{8,10},{9,11},{10,... | collective-permute-start | bytes 442376 | tf_op jit(solution)/shard_map/ppermute | solution.py:340
  46.5 9.0 %collective-permute-start.21 = (bf16[64,1152]{1,0:T(8,128)(2,1)S(1)}, bf16[64,1152]{1,0:T(8,128)(2,1)S(1)}, u32[]{:S(2)}, u32[]{:S(2)}) collective-permute-start(bf16[64,1152]{1,0:T(8,128)(2,1)S(1)} %collective-permute-done.17.refs_4_), channel_id=1, source_target_pairs={{0,2},{1,3},{2,0},{3,1},{4,6},{5,7},{6,4},{7,5},{8,10},{9,11},{10,... | collective-permute-start | bytes 442376 | tf_op jit(solution)/shard_map/ppermute | solution.py:340
  48.5 7.0 %collective-permute-start.23 = (bf16[64,1152]{1,0:T(8,128)(2,1)S(1)}, bf16[64,1152]{1,0:T(8,128)(2,1)S(1)}, u32[]{:S(2)}, u32[]{:S(2)}) collective-permute-start(bf16[64,1152]{1,0:T(8,128)(2,1)S(1)} %collective-permute-done.15.refs_2_), channel_id=1, source_target_pairs={{0,1},{1,0},{2,3},{3,2},{4,5},{5,4},{6,7},{7,6},{8,9},{9,8},{10,11... | collective-permute-start | bytes 442376 | tf_op jit(solution)/shard_map/ppermute | solution.py:340
  48.5 7.5 %collective-permute-start.24 = (bf16[64,1152]{1,0:T(8,128)(2,1)S(1)}, bf16[64,1152]{1,0:T(8,128)(2,1)S(1)}, u32[]{:S(2)}, u32[]{:S(2)}) collective-permute-start(bf16[64,1152]{1,0:T(8,128)(2,1)S(1)} %collective-permute-done.16.refs_3_), channel_id=1, source_target_pairs={{0,1},{1,0},{2,3},{3,2},{4,5},{5,4},{6,7},{7,6},{8,9},{9,8},{10,11... | collective-permute-start | bytes 442376 | tf_op jit(solution)/shard_map/ppermute | solution.py:340
  49.0 7.3 %collective-permute-start.25 = (bf16[64,1152]{1,0:T(8,128)(2,1)S(1)}, bf16[64,1152]{1,0:T(8,128)(2,1)S(1)}, u32[]{:S(2)}, u32[]{:S(2)}) collective-permute-start(bf16[64,1152]{1,0:T(8,128)(2,1)S(1)} %collective-permute-done.17.refs_4_), channel_id=1, source_target_pairs={{0,1},{1,0},{2,3},{3,2},{4,5},{5,4},{6,7},{7,6},{8,9},{9,8},{10,11... | collective-permute-start | bytes 442376 | tf_op jit(solution)/shard_map/ppermute | solution.py:340
  53.2 3.1 %collective-permute-start.26 = (bf16[64,1152]{1,0:T(8,128)(2,1)S(1)}, bf16[64,1152]{1,0:T(8,128)(2,1)S(1)}, u32[]{:S(2)}, u32[]{:S(2)}) collective-permute-start(bf16[64,1152]{1,0:T(8,128)(2,1)S(1)} %collective-permute-done.18.refs_5_), channel_id=1, source_target_pairs={{0,1},{1,0},{2,3},{3,2},{4,5},{5,4},{6,7},{7,6},{8,9},{9,8},{10,11... | collective-permute-start | bytes 442376 | tf_op jit(solution)/shard_map/ppermute | solution.py:340
  55.5 1.4 %collective-permute-start.27 = (bf16[64,1152]{1,0:T(8,128)(2,1)S(1)}, bf16[64,1152]{1,0:T(8,128)(2,1)S(1)}, u32[]{:S(2)}, u32[]{:S(2)}) collective-permute-start(bf16[64,1152]{1,0:T(8,128)(2,1)S(1)} %collective-permute-done.19.refs_6_), channel_id=1, source_target_pairs={{0,1},{1,0},{2,3},{3,2},{4,5},{5,4},{6,7},{7,6},{8,9},{9,8},{10,11... | collective-permute-start | bytes 442376 | tf_op jit(solution)/shard_map/ppermute | solution.py:340
  55.5 1.6 %collective-permute-start.28 = (bf16[64,1152]{1,0:T(8,128)(2,1)S(1)}, bf16[64,1152]{1,0:T(8,128)(2,1)S(1)}, u32[]{:S(2)}, u32[]{:S(2)}) collective-permute-start(bf16[64,1152]{1,0:T(8,128)(2,1)S(1)} %collective-permute-done.20.refs_7_), channel_id=1, source_target_pairs={{0,1},{1,0},{2,3},{3,2},{4,5},{5,4},{6,7},{7,6},{8,9},{9,8},{10,11... | collective-permute-start | bytes 442376 | tf_op jit(solution)/shard_map/ppermute | solution.py:340
  56.0 1.4 %collective-permute-start.29 = (bf16[64,1152]{1,0:T(8,128)(2,1)S(1)}, bf16[64,1152]{1,0:T(8,128)(2,1)S(1)}, u32[]{:S(2)}, u32[]{:S(2)}) collective-permute-start(bf16[64,1152]{1,0:T(8,128)(2,1)S(1)} %collective-permute-done.21.refs_8_), channel_id=1, source_target_pairs={{0,1},{1,0},{2,3},{3,2},{4,5},{5,4},{6,7},{7,6},{8,9},{9,8},{10,11... | collective-permute-start | bytes 442376 | tf_op jit(solution)/shard_map/ppermute | solution.py:340
  57.4 19.3 %slice-start = ((s8[14680064]{0:T(1024)(128)(4,1)}), s8[4194304]{0:T(1024)(128)(4,1)S(1)}, s32[]{:S(2)}) async-start(s8[14680064]{0:T(1024)(128)(4,1)} %bitcast.6), calls=%async_computation | async-start | bytes 8388608
  57.4 19.3 %slice-start.4 = ((s8[14680064]{0:T(1024)(128)(4,1)}), s8[2097152]{0:T(1024)(128)(4,1)S(1)}, s32[]{:S(2)}) async-start(s8[14680064]{0:T(1024)(128)(4,1)} %bitcast.8), calls=%async_computation.4 | async-start | bytes 4194304
  60.0 16.6 %slice-start.1 = ((s8[14680064]{0:T(1024)(128)(4,1)}), s8[4194304]{0:T(1024)(128)(4,1)S(1)}, s32[]{:S(2)}) async-start(s8[14680064]{0:T(1024)(128)(4,1)} %bitcast.6), calls=%async_computation.1 | async-start | bytes 8388608
  60.1 16.6 %slice-start.2 = ((s8[14680064]{0:T(1024)(128)(4,1)}), s8[4194304]{0:T(1024)(128)(4,1)S(1)}, s32[]{:S(2)}) async-start(s8[14680064]{0:T(1024)(128)(4,1)} %bitcast.6), calls=%async_computation.2 | async-start | bytes 8388608
  60.1 16.6 %slice-start.3 = ((s8[14680064]{0:T(1024)(128)(4,1)}), s8[2097152]{0:T(1024)(128)(4,1)S(1)}, s32[]{:S(2)}) async-start(s8[14680064]{0:T(1024)(128)(4,1)} %bitcast.6), calls=%async_computation.3 | async-start | bytes 4194304
  60.1 16.6 %slice-start.5 = ((s8[14680064]{0:T(1024)(128)(4,1)}), s8[4194304]{0:T(1024)(128)(4,1)S(1)}, s32[]{:S(2)}) async-start(s8[14680064]{0:T(1024)(128)(4,1)} %bitcast.8), calls=%async_computation.5 | async-start | bytes 8388608
  60.1 16.6 %slice-start.6 = ((s8[14680064]{0:T(1024)(128)(4,1)}), s8[4194304]{0:T(1024)(128)(4,1)S(1)}, s32[]{:S(2)}) async-start(s8[14680064]{0:T(1024)(128)(4,1)} %bitcast.8), calls=%async_computation.6 | async-start | bytes 8388608
  60.1 16.6 %slice-start.7 = ((s8[14680064]{0:T(1024)(128)(4,1)}), s8[4194304]{0:T(1024)(128)(4,1)S(1)}, s32[]{:S(2)}) async-start(s8[14680064]{0:T(1024)(128)(4,1)} %bitcast.8), calls=%async_computation.7 | async-start | bytes 8388608
  60.1 16.6 %copy-start.1 = (f32[8192]{0:T(1024)S(1)}, f32[8192]{0:T(1024)}, u32[]{:S(2)}) copy-start(f32[8192]{0:T(1024)} %param.21) | copy-start | bytes 98308
  60.1 10.2 %collective-permute-start.37 = (bf16[128,512]{1,0:T(8,128)(2,1)S(1)}, bf16[128,512]{1,0:T(8,128)(2,1)S(1)}, u32[]{:S(2)}, u32[]{:S(2)}) collective-permute-start(bf16[128,512]{1,0:T(8,128)(2,1)S(1)} %projection.1.refs_0_), channel_id=1, source_target_pairs={{0,8},{1,9},{2,10},{3,11},{4,12},{5,13},{6,14},{7,15},{8,0},{9,1},... | collective-permute-start | bytes 393224 | tf_op jit(solution)/shard_map/ppermute | solution.py:340
  60.4 9.9 %collective-permute-start.30 = (bf16[128,512]{1,0:T(8,128)(2,1)S(1)}, bf16[128,512]{1,0:T(8,128)(2,1)S(1)}, u32[]{:S(2)}, u32[]{:S(2)}) collective-permute-start(bf16[128,512]{1,0:T(8,128)(2,1)S(1)} %projection.1.refs_0_), channel_id=1, source_target_pairs={{0,1},{1,0},{2,3},{3,2},{4,5},{5,4},{6,7},{7,6},{8,9},{9,8},{10,11... | collective-permute-start | bytes 393224 | tf_op jit(solution)/shard_map/ppermute | solution.py:340
  60.5 9.9 %collective-permute-start.43 = (bf16[128,512]{1,0:T(8,128)(2,1)S(1)}, bf16[128,512]{1,0:T(8,128)(2,1)S(1)}, u32[]{:S(2)}, u32[]{:S(2)}) collective-permute-start(bf16[128,512]{1,0:T(8,128)(2,1)S(1)} %projection.1.refs_0_), channel_id=1, source_target_pairs={{0,2},{1,3},{2,0},{3,1},{4,6},{5,7},{6,4},{7,5},{8,10},{9,11},{10,... | collective-permute-start | bytes 393224 | tf_op jit(solution)/shard_map/ppermute | solution.py:340
  61.2 9.7 %collective-permute-start.31 = (bf16[128,512]{1,0:T(8,128)(2,1)S(1)}, bf16[128,512]{1,0:T(8,128)(2,1)S(1)}, u32[]{:S(2)}, u32[]{:S(2)}) collective-permute-start(bf16[128,512]{1,0:T(8,128)(2,1)S(1)} %projection.1.refs_0_), channel_id=1, source_target_pairs={{0,4},{1,5},{2,6},{3,7},{4,0},{5,1},{6,2},{7,3},{8,12},{9,13},{10,... | collective-permute-start | bytes 393224 | tf_op jit(solution)/shard_map/ppermute | solution.py:340
  62.7 10.9 %collective-permute-start.34 = (bf16[128,512]{1,0:T(8,128)(2,1)S(1)}, bf16[128,512]{1,0:T(8,128)(2,1)S(1)}, u32[]{:S(2)}, u32[]{:S(2)}) collective-permute-start(bf16[128,512]{1,0:T(8,128)(2,1)S(1)} %projection.1.refs_0_), channel_id=1, source_target_pairs={{0,12},{1,13},{2,14},{3,15},{4,8},{5,9},{6,10},{7,11},{8,4},{9,5},... | collective-permute-start | bytes 393224 | tf_op jit(solution)/shard_map/ppermute | solution.py:340
  70.3 3.4 %collective-permute-start.42 = (bf16[128,512]{1,0:T(8,128)(2,1)S(1)}, bf16[128,512]{1,0:T(8,128)(2,1)S(1)}, u32[]{:S(2)}, u32[]{:S(2)}) collective-permute-start(bf16[128,512]{1,0:T(8,128)(2,1)S(1)} %collective-permute-done.37.refs_0_), channel_id=1, source_target_pairs={{0,1},{1,0},{2,3},{3,2},{4,5},{5,4},{6,7},{7,6},{8,9},{9,8},{10,11... | collective-permute-start | bytes 393224 | tf_op jit(solution)/shard_map/ppermute | solution.py:340
  70.3 6.4 %collective-permute-start.38 = (bf16[128,512]{1,0:T(8,128)(2,1)S(1)}, bf16[128,512]{1,0:T(8,128)(2,1)S(1)}, u32[]{:S(2)}, u32[]{:S(2)}) collective-permute-start(bf16[128,512]{1,0:T(8,128)(2,1)S(1)} %collective-permute-done.37.refs_0_), channel_id=1, source_target_pairs={{0,2},{1,3},{2,0},{3,1},{4,6},{5,7},{6,4},{7,5},{8,10},{9,11},{10,... | collective-permute-start | bytes 393224 | tf_op jit(solution)/shard_map/ppermute | solution.py:340
  70.4 3.4 %collective-permute-start.44 = (bf16[128,512]{1,0:T(8,128)(2,1)S(1)}, bf16[128,512]{1,0:T(8,128)(2,1)S(1)}, u32[]{:S(2)}, u32[]{:S(2)}) collective-permute-start(bf16[128,512]{1,0:T(8,128)(2,1)S(1)} %collective-permute-done.43.refs_2_), channel_id=1, source_target_pairs={{0,1},{1,0},{2,3},{3,2},{4,5},{5,4},{6,7},{7,6},{8,9},{9,8},{10,11... | collective-permute-start | bytes 393224 | tf_op jit(solution)/shard_map/ppermute | solution.py:340
  70.9 8.6 %collective-permute-start.32 = (bf16[128,512]{1,0:T(8,128)(2,1)S(1)}, bf16[128,512]{1,0:T(8,128)(2,1)S(1)}, u32[]{:S(2)}, u32[]{:S(2)}) collective-permute-start(bf16[128,512]{1,0:T(8,128)(2,1)S(1)} %collective-permute-done.31.refs_0_), channel_id=1, source_target_pairs={{0,2},{1,3},{2,0},{3,1},{4,6},{5,7},{6,4},{7,5},{8,10},{9,11},{10,... | collective-permute-start | bytes 393224 | tf_op jit(solution)/shard_map/ppermute | solution.py:340
  73.6 8.2 %collective-permute-start.35 = (bf16[128,512]{1,0:T(8,128)(2,1)S(1)}, bf16[128,512]{1,0:T(8,128)(2,1)S(1)}, u32[]{:S(2)}, u32[]{:S(2)}) collective-permute-start(bf16[128,512]{1,0:T(8,128)(2,1)S(1)} %collective-permute-done.34.refs_1_), channel_id=1, source_target_pairs={{0,2},{1,3},{2,0},{3,1},{4,6},{5,7},{6,4},{7,5},{8,10},{9,11},{10,... | collective-permute-start | bytes 393224 | tf_op jit(solution)/shard_map/ppermute | solution.py:340
  73.7 10.0 %collective-permute-start.39 = (bf16[128,512]{1,0:T(8,128)(2,1)S(1)}, bf16[128,512]{1,0:T(8,128)(2,1)S(1)}, u32[]{:S(2)}, u32[]{:S(2)}) collective-permute-start(bf16[128,512]{1,0:T(8,128)(2,1)S(1)} %collective-permute-done.31.refs_0_), channel_id=1, source_target_pairs={{0,1},{1,0},{2,3},{3,2},{4,5},{5,4},{6,7},{7,6},{8,9},{9,8},{10,11... | collective-permute-start | bytes 393224 | tf_op jit(solution)/shard_map/ppermute | solution.py:340
  73.7 9.9 %collective-permute-start.40 = (bf16[128,512]{1,0:T(8,128)(2,1)S(1)}, bf16[128,512]{1,0:T(8,128)(2,1)S(1)}, u32[]{:S(2)}, u32[]{:S(2)}) collective-permute-start(bf16[128,512]{1,0:T(8,128)(2,1)S(1)} %collective-permute-done.34.refs_1_), channel_id=1, source_target_pairs={{0,1},{1,0},{2,3},{3,2},{4,5},{5,4},{6,7},{7,6},{8,9},{9,8},{10,11... | collective-permute-start | bytes 393224 | tf_op jit(solution)/shard_map/ppermute | solution.py:340
  76.7 7.0 %collective-permute-start.41 = (bf16[128,512]{1,0:T(8,128)(2,1)S(1)}, bf16[128,512]{1,0:T(8,128)(2,1)S(1)}, u32[]{:S(2)}, u32[]{:S(2)}) collective-permute-start(bf16[128,512]{1,0:T(8,128)(2,1)S(1)} %collective-permute-done.38.refs_2_), channel_id=1, source_target_pairs={{0,1},{1,0},{2,3},{3,2},{4,5},{5,4},{6,7},{7,6},{8,9},{9,8},{10,11... | collective-permute-start | bytes 393224 | tf_op jit(solution)/shard_map/ppermute | solution.py:340
  79.5 7.9 %collective-permute-start.33 = (bf16[128,512]{1,0:T(8,128)(2,1)S(1)}, bf16[128,512]{1,0:T(8,128)(2,1)S(1)}, u32[]{:S(2)}, u32[]{:S(2)}) collective-permute-start(bf16[128,512]{1,0:T(8,128)(2,1)S(1)} %collective-permute-done.32.refs_0_), channel_id=1, source_target_pairs={{0,1},{1,0},{2,3},{3,2},{4,5},{5,4},{6,7},{7,6},{8,9},{9,8},{10,11... | collective-permute-start | bytes 393224 | tf_op jit(solution)/shard_map/ppermute | solution.py:340
  81.8 5.6 %collective-permute-start.36 = (bf16[128,512]{1,0:T(8,128)(2,1)S(1)}, bf16[128,512]{1,0:T(8,128)(2,1)S(1)}, u32[]{:S(2)}, u32[]{:S(2)}) collective-permute-start(bf16[128,512]{1,0:T(8,128)(2,1)S(1)} %collective-permute-done.35.refs_1_), channel_id=1, source_target_pairs={{0,1},{1,0},{2,3},{3,2},{4,5},{5,4},{6,7},{7,6},{8,9},{9,8},{10,11... | collective-permute-start | bytes 393224 | tf_op jit(solution)/shard_map/ppermute | solution.py:340
